TPU v7x, 32 devices: a whole 2x2x4 slice. The times are simulated.
32 devices in a mesh: narrow: 4 (over y, core), wide: 8 (over z, x).
Axes of the slice: x: 2, y: 2, z: 4, core: 2. Of those that a mesh axis runs over, the one named last changes fastest.
Arguments:
- tokens: bfloat16 [8192, 2048], P(('narrow', 'wide')), may hold values from -6 to 6
- attention_gain: bfloat16 [2048], replicated, may hold values from 0.099609375 to 1.8984375
- query_weight: bfloat16 [2048, 2048], P(None, 'wide'), may hold values from -0.125 to 0.125
- key_weight: bfloat16 [2048, 512], replicated, may hold values from -0.125 to 0.125
- value_weight: bfloat16 [2048, 512], replicated, may hold values from -0.125 to 0.125
- query_gain: bfloat16 [64], replicated, may hold values from 0.099609375 to 1.8984375
- key_gain: bfloat16 [64], replicated, may hold values from 0.099609375 to 1.8984375
- output_weight: bfloat16 [2048, 2048], P('wide'), may hold values from -0.75 to 0.75
- feedforward_gain: bfloat16 [2048], replicated, may hold values from 0.099609375 to 1.8984375
- gate_weight: bfloat16 [2048, 8192], P(None, 'wide'), may hold values from -0.125 to 0.125
- up_weight: bfloat16 [2048, 8192], P(None, 'wide'), may hold values from -0.125 to 0.125
- down_weight: bfloat16 [8192, 2048], P('wide'), may hold values from -0.0625 to 0.0625
- cotangent: bfloat16 [8192, 2048], P(('narrow', 'wide')), may hold values from -6 to 6
- corpus_tags: int32 [8192], P(('narrow', 'wide')), may hold values from 0 to 7, as said below
- segments: int32 [4, 2048], P('narrow'), may hold values from 0 to 7, never falling along the last dimension, each value on 1 to 1024 neighbouring positions
Outputs:
- block_output: bfloat16 [8192, 2048], P(('narrow', 'wide'))
- tokens_gradient: bfloat16 [8192, 2048], P(('narrow', 'wide'))
- attention_gain_gradient: float32 [2048], P('wide')
- query_weight_gradient: float32 [2048, 2048], P(None, 'wide')
- key_weight_gradient: float32 [2048, 512], P(None, 'wide')
- value_weight_gradient: float32 [2048, 512], P(None, 'wide')
- query_gain_gradient: float32 [64], P('wide')
- key_gain_gradient: float32 [64], P('wide')
- output_weight_gradient: float32 [2048, 2048], P('wide')
- feedforward_gain_gradient: float32 [2048], P('wide')
- gate_weight_gradient: float32 [2048, 8192], P(None, 'wide')
- up_weight_gradient: float32 [2048, 8192], P(None, 'wide')
- down_weight_gradient: float32 [8192, 2048], P('wide')
Inputs may be any that keep to these rules, and one draw needn't show every extreme that they name: `corpus_tags`: every corpus has at least one token. `segments`: along each sequence the document number never falls; a document has at most 1024 positions.
All inputs are finite; a program needn't handle non-finite values.
Results may differ from a plain program's by a relative error of at most 0.025.
Values may be sent and summed in bfloat16 or wider, within the bound.
A program may use at most 512 MiB of HBM per device.

v0:
```python
from functools import partial

import jax
import jax.numpy as jnp
from jax import lax
from jax.sharding import PartitionSpec as P

SEQ = 2048
CORPORA = 8


epsilon = 1e-06
rope_base = 10000.0


def norm_scale(values, scale_gain):
    return (
        values * lax.rsqrt(jnp.mean(values * values, axis=-1, keepdims=True) + epsilon) * scale_gain
    )


def rotary_tables(row_total, head_size):
    positions = (jnp.arange(row_total) % SEQ).astype(jnp.float32)
    exponents = jnp.arange(head_size // 2).astype(jnp.float32) * (2.0 / head_size)
    frequency = rope_base ** (-exponents)
    angles = positions[:, None] * frequency[None, :]
    return (jnp.cos(angles), jnp.sin(angles))


def rotate(values, cosine_table, sine_table):
    half_width = values.shape[-1] // 2
    table_shape = (values.shape[0],) + (1,) * (values.ndim - 2) + (half_width,)
    cosine_part = cosine_table.reshape(table_shape)
    sine_part = sine_table.reshape(table_shape)
    first_half = values[..., :half_width]
    second_half = values[..., half_width:]
    return jnp.concatenate(
        [
            first_half * cosine_part - second_half * sine_part,
            second_half * cosine_part + first_half * sine_part,
        ],
        axis=-1,
    )


def norm_rotate(values, scale_gain, cosine_table, sine_table):
    return rotate(norm_scale(values, scale_gain), cosine_table, sine_table)


def contract_first(left, right):
    return lax.dot_general(
        left, right, (((0,), (0,)), ((), ())), preferred_element_type=jnp.float32
    )


def contract_last(left, right):
    return lax.dot_general(
        left, right, (((1,), (1,)), ((), ())), preferred_element_type=jnp.float32
    )


def plain_product(left, right):
    return jnp.dot(left, right, preferred_element_type=jnp.float32)


def masked_scores(query_block, key_seq, segment_row, block_index, scale_factor):
    block_rows = query_block.shape[0]
    scores = (
        jnp.einsum("qkgd,skd->kgqs", query_block, key_seq, preferred_element_type=jnp.float32)
        * scale_factor
    )
    query_pos = block_index * block_rows + jnp.arange(block_rows)
    key_pos = jnp.arange(key_seq.shape[0])
    segment_query = lax.dynamic_slice_in_dim(segment_row, block_index * block_rows, block_rows)
    allowed = (key_pos[None, :] <= query_pos[:, None]) & (
        segment_query[:, None] == segment_row[None, :]
    )
    return jnp.where(allowed, scores, -1e30)


def swiglu_back(act_grad, gate_values, up_values):
    sigmoid_gate = lax.logistic(gate_values)
    gate_part = act_grad * up_values * sigmoid_gate * (1.0 + gate_values * (1.0 - sigmoid_gate))
    up_part = act_grad * gate_values * sigmoid_gate
    return (gate_part.astype(jnp.bfloat16), up_part.astype(jnp.bfloat16))


def shards(
    tokens,
    attention_gain,
    query_weight,
    key_weight,
    value_weight,
    query_gain,
    key_gain,
    output_weight,
    feedforward_gain,
    gate_weight,
    up_weight,
    down_weight,
    cotangent,
    corpus_tags,
    segments,
):
    head_size = query_gain.shape[0]
    model_width = tokens.shape[1]
    wide_count = lax.axis_size("wide")
    wide_index = lax.axis_index("wide")
    heads_here = query_weight.shape[1] // head_size
    group_size = heads_here * wide_count // (key_weight.shape[1] // head_size)
    group_local = min(heads_here, group_size)
    key_heads = heads_here // group_local
    key_first = wide_index * heads_here // group_size
    key_columns = lax.dynamic_slice_in_dim(
        key_weight, key_first * head_size, key_heads * head_size, 1
    )
    value_columns = lax.dynamic_slice_in_dim(
        value_weight, key_first * head_size, key_heads * head_size, 1
    )
    scale_factor = head_size ** (-0.5)
    tag_hits = corpus_tags[:, None] == jnp.arange(CORPORA, dtype=jnp.int32)[None, :]
    local_counts = jnp.sum(tag_hits.astype(jnp.float32), axis=0)
    corpus_counts = lax.psum(local_counts, ("narrow", "wide"))
    corpus_scale = jnp.sqrt(jnp.sum(corpus_counts) / (CORPORA * corpus_counts))
    row_weight = jnp.sum(jnp.where(tag_hits, corpus_scale[None, :], 0.0), axis=1)
    out_cot = cotangent.astype(jnp.float32) * row_weight[:, None]
    token_values = tokens.astype(jnp.float32)
    first_gain = attention_gain.astype(jnp.float32)
    second_gain = feedforward_gain.astype(jnp.float32)
    hidden_local = norm_scale(token_values, first_gain).astype(jnp.bfloat16)
    hidden_one = lax.all_gather(hidden_local, "wide", axis=0, tiled=True)
    all_rows = hidden_one.shape[0]
    seq_count = all_rows // SEQ
    block_rows = min(512, SEQ)
    block_count = SEQ // block_rows
    cosine_table, sine_table = rotary_tables(all_rows, head_size)
    rotate_fn = partial(norm_rotate, cosine_table=cosine_table, sine_table=sine_table)
    query_scale = query_gain.astype(jnp.float32)
    key_scale = key_gain.astype(jnp.float32)
    query_raw = plain_product(hidden_one, query_weight).reshape(all_rows, heads_here, head_size)
    key_raw = plain_product(hidden_one, key_columns).reshape(all_rows, key_heads, head_size)
    value_raw = plain_product(hidden_one, value_columns).reshape(all_rows, key_heads, head_size)
    query_low = rotate_fn(query_raw, query_scale).astype(jnp.bfloat16)
    key_low = rotate_fn(key_raw, key_scale).astype(jnp.bfloat16)
    value_low = value_raw.astype(jnp.bfloat16)
    query_blocks = query_low.reshape(
        seq_count, block_count, block_rows, key_heads, group_local, head_size
    )
    key_seqs = key_low.reshape(seq_count, SEQ, key_heads, head_size)
    value_seqs = value_low.reshape(seq_count, SEQ, key_heads, head_size)

    def forward_sequence(sequence_index):
        segment_row = segments[sequence_index]
        key_seq = key_seqs[sequence_index]
        value_seq = value_seqs[sequence_index]

        def forward_block(block_index):
            query_block = query_blocks[sequence_index, block_index]
            scores = masked_scores(query_block, key_seq, segment_row, block_index, scale_factor)
            row_top = jnp.max(scores, axis=-1, keepdims=True)
            shifted = jnp.exp(scores - row_top)
            row_total = jnp.sum(shifted, axis=-1, keepdims=True)
            probability = (shifted / row_total).astype(jnp.bfloat16)
            attended = jnp.einsum(
                "kgqs,skd->qkgd", probability, value_seq, preferred_element_type=jnp.float32
            )
            return (attended, (row_top + jnp.log(row_total))[..., 0])

        return lax.map(forward_block, jnp.arange(block_count))

    attended, log_totals = lax.map(forward_sequence, jnp.arange(seq_count))
    mixed_low = attended.reshape(all_rows, heads_here * head_size).astype(jnp.bfloat16)
    branch = lax.psum_scatter(
        plain_product(mixed_low, output_weight).astype(jnp.bfloat16),
        "wide",
        scatter_dimension=0,
        tiled=True,
    ).astype(jnp.float32)
    middle = token_values + branch
    hidden_two_local = norm_scale(middle, second_gain).astype(jnp.bfloat16)
    hidden_two = lax.all_gather(hidden_two_local, "wide", axis=0, tiled=True)
    gate_values = plain_product(hidden_two, gate_weight)
    up_values = plain_product(hidden_two, up_weight)
    activated = (gate_values * lax.logistic(gate_values) * up_values).astype(jnp.bfloat16)
    result = (
        middle
        + lax.psum_scatter(
            plain_product(activated, down_weight).astype(jnp.bfloat16),
            "wide",
            scatter_dimension=0,
            tiled=True,
        ).astype(jnp.float32)
    ).astype(jnp.bfloat16)
    cot_low = lax.all_gather(out_cot.astype(jnp.bfloat16), "wide", axis=0, tiled=True)
    down_grad = contract_first(activated, cot_low)
    act_grad = contract_last(cot_low, down_weight)
    gate_low, up_low = swiglu_back(act_grad, gate_values, up_values)
    gate_grad = contract_first(hidden_two, gate_low)
    up_grad = contract_first(hidden_two, up_low)
    hidden_two_grad = lax.psum_scatter(
        (contract_last(gate_low, gate_weight) + contract_last(up_low, up_weight)).astype(
            jnp.bfloat16
        ),
        "wide",
        scatter_dimension=0,
        tiled=True,
    ).astype(jnp.float32)
    _, second_pull = jax.vjp(norm_scale, middle, second_gain)
    middle_part, second_gain_grad = second_pull(hidden_two_grad)
    middle_grad = out_cot + middle_part
    branch_low = lax.all_gather(middle_grad.astype(jnp.bfloat16), "wide", axis=0, tiled=True)
    output_weight_grad = contract_first(mixed_low, branch_low)
    mixed_grad = (
        contract_last(branch_low, output_weight)
        .astype(jnp.bfloat16)
        .reshape(seq_count, block_count, block_rows, key_heads, group_local, head_size)
    )

    def backward_sequence(sequence_index):
        segment_row = segments[sequence_index]
        key_seq = key_seqs[sequence_index]
        value_seq = value_seqs[sequence_index]

        def backward_block(running, block_index):
            key_sums, value_sums = running
            query_block = query_blocks[sequence_index, block_index]
            grad_block = mixed_grad[sequence_index, block_index]
            scores = masked_scores(query_block, key_seq, segment_row, block_index, scale_factor)
            probability = jnp.exp(scores - log_totals[sequence_index, block_index][..., None])
            probability_low = probability.astype(jnp.bfloat16)
            prob_grad = jnp.einsum(
                "qkgd,skd->kgqs", grad_block, value_seq, preferred_element_type=jnp.float32
            )
            inner_sum = jnp.sum(probability * prob_grad, axis=-1, keepdims=True)
            score_low = (probability * (prob_grad - inner_sum)).astype(jnp.bfloat16)
            query_part = (
                jnp.einsum("kgqs,skd->qkgd", score_low, key_seq, preferred_element_type=jnp.float32)
                * scale_factor
            )
            key_sums = (
                key_sums
                + jnp.einsum(
                    "kgqs,qkgd->skgd", score_low, query_block, preferred_element_type=jnp.float32
                )
                * scale_factor
            )
            value_sums = value_sums + jnp.einsum(
                "kgqs,qkgd->skgd", probability_low, grad_block, preferred_element_type=jnp.float32
            )
            return ((key_sums, value_sums), query_part)

        empty_sums = jnp.zeros((SEQ, key_heads, group_local, head_size), jnp.float32)
        (key_sums, value_sums), query_parts = lax.scan(
            backward_block, (empty_sums, empty_sums), jnp.arange(block_count)
        )
        return (query_parts, key_sums, value_sums)

    query_parts, key_sums, value_sums = lax.map(backward_sequence, jnp.arange(seq_count))
    _, query_pull = jax.vjp(rotate_fn, query_raw, query_scale)
    query_grad_full, query_gain_grad = query_pull(
        query_parts.reshape(all_rows, heads_here, head_size)
    )
    query_grad = query_grad_full.reshape(all_rows, heads_here * head_size).astype(jnp.bfloat16)
    key_copies = jnp.broadcast_to(
        key_raw[:, :, None, :], (all_rows, key_heads, group_local, head_size)
    )
    _, key_pull = jax.vjp(rotate_fn, key_copies, key_scale)
    key_grad_full, key_gain_grad = key_pull(
        key_sums.reshape(all_rows, key_heads, group_local, head_size)
    )
    key_grad = key_grad_full.astype(jnp.bfloat16)
    value_grad = value_sums.reshape(all_rows, key_heads, group_local, head_size).astype(
        jnp.bfloat16
    )
    query_weight_grad = contract_first(hidden_one, query_grad)
    key_part = jnp.einsum(
        "rd,rkge->dke", hidden_one, key_grad, preferred_element_type=jnp.float32
    ).reshape(model_width, key_heads * head_size)
    value_part = jnp.einsum(
        "rd,rkge->dke", hidden_one, value_grad, preferred_element_type=jnp.float32
    ).reshape(model_width, key_heads * head_size)
    empty_full = jnp.zeros((model_width, key_weight.shape[1]), jnp.float32)
    key_weight_full = lax.dynamic_update_slice_in_dim(
        empty_full, key_part, key_first * head_size, 1
    )
    value_weight_full = lax.dynamic_update_slice_in_dim(
        empty_full, value_part, key_first * head_size, 1
    )
    key_mats = key_columns.reshape(model_width, key_heads, head_size)
    value_mats = value_columns.reshape(model_width, key_heads, head_size)
    hidden_one_grad = lax.psum_scatter(
        (
            contract_last(query_grad, query_weight)
            + jnp.einsum("rkge,dke->rd", key_grad, key_mats, preferred_element_type=jnp.float32)
            + jnp.einsum("rkge,dke->rd", value_grad, value_mats, preferred_element_type=jnp.float32)
        ).astype(jnp.bfloat16),
        "wide",
        scatter_dimension=0,
        tiled=True,
    ).astype(jnp.float32)
    _, first_pull = jax.vjp(norm_scale, token_values, first_gain)
    token_part, first_gain_grad = first_pull(hidden_one_grad)
    tokens_gradient = (middle_grad + token_part).astype(jnp.bfloat16)
    key_share, value_share, first_share, query_gain_share, key_gain_share, second_share = (
        lax.psum_scatter(
            key_weight_full.astype(jnp.bfloat16), "wide", scatter_dimension=1, tiled=True
        ).astype(jnp.float32),
        lax.psum_scatter(
            value_weight_full.astype(jnp.bfloat16), "wide", scatter_dimension=1, tiled=True
        ).astype(jnp.float32),
        lax.psum_scatter(
            first_gain_grad.astype(jnp.bfloat16), "wide", scatter_dimension=0, tiled=True
        ).astype(jnp.float32),
        lax.psum_scatter(
            query_gain_grad.astype(jnp.bfloat16), "wide", scatter_dimension=0, tiled=True
        ).astype(jnp.float32),
        lax.psum_scatter(
            key_gain_grad.astype(jnp.bfloat16), "wide", scatter_dimension=0, tiled=True
        ).astype(jnp.float32),
        lax.psum_scatter(
            second_gain_grad.astype(jnp.bfloat16), "wide", scatter_dimension=0, tiled=True
        ).astype(jnp.float32),
    )
    summed = (
        lax.psum(first_share.astype(jnp.bfloat16), "narrow").astype(jnp.float32),
        lax.psum(query_weight_grad.astype(jnp.bfloat16), "narrow").astype(jnp.float32),
        lax.psum(key_share.astype(jnp.bfloat16), "narrow").astype(jnp.float32),
        lax.psum(value_share.astype(jnp.bfloat16), "narrow").astype(jnp.float32),
        lax.psum(query_gain_share.astype(jnp.bfloat16), "narrow").astype(jnp.float32),
        lax.psum(key_gain_share.astype(jnp.bfloat16), "narrow").astype(jnp.float32),
        lax.psum(output_weight_grad.astype(jnp.bfloat16), "narrow").astype(jnp.float32),
        lax.psum(second_share.astype(jnp.bfloat16), "narrow").astype(jnp.float32),
        lax.psum(gate_grad.astype(jnp.bfloat16), "narrow").astype(jnp.float32),
        lax.psum(up_grad.astype(jnp.bfloat16), "narrow").astype(jnp.float32),
        lax.psum(down_grad.astype(jnp.bfloat16), "narrow").astype(jnp.float32),
    )
    return (
        result,
        tokens_gradient,
        summed[0],
        summed[1],
        summed[2],
        summed[3],
        summed[4],
        summed[5],
        summed[6],
        summed[7],
        summed[8],
        summed[9],
        summed[10],
    )


def solution(mesh):
    placed = (
        P(("narrow", "wide"), None),
        P(),
        P(None, "wide"),
        P(),
        P(),
        P(),
        P(),
        P("wide", None),
        P(),
        P(None, "wide"),
        P(None, "wide"),
        P("wide", None),
        P(("narrow", "wide"), None),
        P(("narrow", "wide")),
        P("narrow", None),
    )
    return jax.shard_map(
        shards,
        mesh=mesh,
        in_specs=placed,
        out_specs=(
            P(("narrow", "wide"), None),
            P(("narrow", "wide"), None),
            P("wide"),
            P(None, "wide"),
            P(None, "wide"),
            P(None, "wide"),
            P("wide"),
            P("wide"),
            P("wide", None),
            P("wide"),
            P(None, "wide"),
            P(None, "wide"),
            P("wide", None),
        ),
        check_vma=False,
    )
```

profile of v0, /device:TPU:0, one launch (start us, length us, event | category | flops | bytes accessed | tf_op | source)
XLA Modules:
  0.0 1985.9 jit_solution(13818820277566493256)
XLA Ops:
  14.5 126.6 %all-gather.5.cloned.1.call-done = bf16[2048,2048]{1,0:T(8,128)(2,1)} async-done(((bf16[256,2048]{1,0:T(8,128)(2,1)}), bf16[2048,2048]{1,0:T(8,128)(2,1)}) %all-gather.5.cloned.1.call-update) | async-done | bytes 8388624 | tf_op jit(solution)/shard_map/all_gather | solution.py:131
  141.1 6.3 multiply_reduce_fusion.6
  161.1 6.9 fusion.63
  168.0 72.0 %while.49 = (s32[]{:T(128)}, bf16[4,512,1,4,64]{1,4,3,2,0:T(8,128)(2,1)}, f32[4,1,4,512]{3,2,1,0:T(4,128)S(1)}, s32[4]{0:T(128)S(1)}, s32[2048]{0:T(1024)S(1)}, ...) while((s32[]{:T(128)}, ...), condition=%wide.region_6.7_spmd, body=%wide.region_3.6_spmd.sunk | while | flops 1127217664 | bytes 65358160 | solution.py:169
  250.2 146.7 %reduce-scatter.7.cloned.1.call-done = bf16[256,2048]{1,0:T(8,128)(2,1)} async-done(((bf16[2048,2048]{1,0:T(8,128)(2,1)}), bf16[256,2048]{1,0:T(8,128)(2,1)}) %reduce-scatter.7.cloned.1.call-update) | async-done | bytes 1048592 | tf_op jit(solution)/shard_map/reduce_scatter | solution.py:173
  401.4 42.4 %psum.84 = f32[8]{0:T(128)S(1)} all-reduce(f32[8]{0:T(128)S(1)} %convert_reduce_fusion.2), channel_id=1, replica_groups=mesh['narrow'=4,'wide'=8] {'narrow','wide'}, use_global_device_ids=true, to_apply=%region_11.12 | all-reduce | flops 8 | bytes 64 | tf_op jit(solution)/shard_map/psum | solution.py:123
  447.6 78.7 %all-gather.7.cloned.1.call-done = bf16[2048,2048]{1,0:T(8,128)(2,1)} async-done(((bf16[256,2048]{1,0:T(8,128)(2,1)}), bf16[2048,2048]{1,0:T(8,128)(2,1)}) %all-gather.7.cloned.1.call-update) | async-done | bytes 8388624 | tf_op jit(solution)/shard_map/all_gather | solution.py:181
  526.3 14.6 fusion.104
  540.9 11.0 fusion.103
  551.9 100.2 %all-gather.9.cloned.1.call-done = bf16[2048,2048]{1,0:T(8,128)(2,1)} async-done(((bf16[256,2048]{1,0:T(8,128)(2,1)}), bf16[2048,2048]{1,0:T(8,128)(2,1)}) %all-gather.9.cloned.1.call-update) | async-done | bytes 8388624 | tf_op jit(solution)/shard_map/all_gather | solution.py:194
  652.1 23.1 %multiply_convert_fusion = (bf16[2048,1024]{1,0:T(8,128)(2,1)}, bf16[2048,1024]{1,0:T(8,128)(2,1)}, bf16[2048,1024]{1,0:T(8,128)(2,1)}) fusion(f32[2048,1024]{1,0:T(8,128)} %fusion.103, f32[2048,1024]{1,0:T(8,128)} %fusion.104, bf16[2048,2048]{1,0:T(8,128)(2,1)} %all-gather.9.cloned.1.call-done, bf16[1024,2048]{1,0:T(8,128)(2,1)} %param.30), kind=kOutput, calls=%fused_computation.66 | convolution fusion | flops 8623489024 | bytes 41943040 | tf_op jit(solution)/shard_map/dot_general | solution.py:57
  675.2 15.5 fusion.105
  690.7 15.8 add_convert_fusion.1
  706.7 147.3 %reduce-scatter.11.cloned.1.call-done = bf16[256,2048]{1,0:T(8,128)(2,1)} async-done(((bf16[2048,2048]{1,0:T(8,128)(2,1)}), bf16[256,2048]{1,0:T(8,128)(2,1)}) %reduce-scatter.11.cloned.1.call-update) | async-done | bytes 1048592 | tf_op jit(solution)/shard_map/reduce_scatter | solution.py:200
  861.4 124.0 %all-gather.11.cloned.1.call-done = bf16[2048,2048]{1,0:T(8,128)(2,1)} async-done(((bf16[256,2048]{1,0:T(8,128)(2,1)}), bf16[2048,2048]{1,0:T(8,128)(2,1)}) %all-gather.11.cloned.1.call-update) | async-done | bytes 8388624 | tf_op jit(solution)/shard_map/all_gather | solution.py:211
  985.4 7.0 convolution_convert_fusion.7
  1000.9 254.6 %while.50 = (s32[]{:T(128)}, f32[2048,1,4,64]{0,3,2,1:T(8,128)}, f32[2048,1,4,64]{0,3,2,1:T(8,128)}, f32[4,512,1,4,64]{1,0,4,3,2:T(4,128)}, s32[4]{0:T(128)S(1)}...) while((s32[]{:T(128)}, f32[2048,1,4,64]{0,3,2,1:T(8,128)}, ...), condition=%wide.region_18.19_spmd.clone, body=%wide.region_16.18_spmd.clone.sunk | while | flops 2753165824 | bytes 210053424 | solution.py:253
  1014.7 7.1 fusion.187
  1021.8 11.9 fusion.184
  1033.7 12.1 fusion.185
  1052.9 11.1 dynamic_update_slice.45
  1077.4 7.5 fusion.187
  1084.9 11.9 fusion.184
  1096.7 12.1 fusion.185
  1116.7 11.1 dynamic_update_slice.45
  1141.2 7.5 fusion.187
  1148.7 11.9 fusion.184
  1160.5 12.1 fusion.185
  1180.5 11.1 dynamic_update_slice.45
  1205.0 7.5 fusion.187
  1212.5 11.9 fusion.184
  1224.3 12.1 fusion.185
  1244.3 11.1 dynamic_update_slice.45
  1262.8 14.1 convolution_convert_fusion.3
  1276.9 13.2 convolution_convert_fusion.2
  1291.8 5.8 convolution_dynamic-update-slice_fusion
  1297.7 14.3 convolution_convert_fusion.4
  1319.9 7.1 convolution_convert_fusion.5
  1330.6 69.1 %reduce-scatter.17.cloned.1.call-done = bf16[2048,64]{0,1:T(8,128)(2,1)} async-done(((bf16[2048,512]{0,1:T(8,128)(2,1)}), bf16[2048,64]{0,1:T(8,128)(2,1)}) %reduce-scatter.17.cloned.1.call-update) | async-done | bytes 262160 | tf_op jit(solution)/shard_map/reduce_scatter | solution.py:308
  1400.2 10.5 fusion.78
  1410.6 8.2 fusion.106
  1418.8 15.8 add_convert_fusion
  1434.8 14.1 convolution_convert_fusion
  1451.4 217.0 %all-reduce.13.cloned.1.call-done = (bf16[2048,256]{1,0:T(8,128)(2,1)}, bf16[2048,64]{0,1:T(8,128)(2,1)}, bf16[2048,64]{0,1:T(8,128)(2,1)}, bf16[256,2048]{1,0:T...) async-done(((bf16[2048,256]{1,0:T(8,128)(2,1)}, bf16[2048,64]{0,1:T(8,128)(2,1)}, bf16[2048,64]{0,1:T(8,128)(2,1)}, ...) | async-done | bytes 15204368 | tf_op jit(solution)/shard_map/psum | solution.py:326
  1691.0 130.2 %reduce-scatter.13.cloned.1.call-done = bf16[256,2048]{1,0:T(8,128)(2,1)} async-done(((bf16[2048,2048]{1,0:T(8,128)(2,1)}), bf16[256,2048]{1,0:T(8,128)(2,1)}) %reduce-scatter.13.cloned.1.call-update) | async-done | bytes 1048592 | tf_op jit(solution)/shard_map/reduce_scatter | solution.py:291
  1823.5 20.6 %all-reduce.8 = (bf16[2048]{0:T(1024)(128)(2,1)S(1)}, bf16[64]{0:T(256)(128)(2,1)S(1)}, bf16[64]{0:T(256)(128)(2,1)S(1)}, bf16[2048]{0:T(1024)(128)(2,1)S(1)}) all-reduce(bf16[2048]{0:T(1024)(128)(2,1)S(1)} %get-tuple-element.351, bf16[64]{0:T(256)(128)(2,1)S(1)} %get-tuple-element.349, ...), channel_id=6, replica_groups=mesh['narrow'=4,'wide'=8] {'wide'}, use_global_device_ids=true, to_apply=%region_26.27.clone | all-reduce | flops 4224 | bytes 16896
  1844.4 6.0 all-reduce.9
  1852.6 121.0 %reduce-scatter.9.cloned.1.call-done = bf16[256,2048]{1,0:T(8,128)(2,1)} async-done(((bf16[2048,2048]{1,0:T(8,128)(2,1)}), bf16[256,2048]{1,0:T(8,128)(2,1)}) %reduce-scatter.9.cloned.1.call-update) | async-done | bytes 1048592 | tf_op jit(solution)/shard_map/reduce_scatter | solution.py:187
  (330 shorter events, 245.1 us)
Async XLA Ops:
  7.2 133.9 %copy-start = (bf16[2048,512]{1,0:T(8,128)(2,1)S(1)}, bf16[2048,512]{1,0:T(8,128)(2,1)}, u32[]{:S(2)}) copy-start(bf16[2048,512]{1,0:T(8,128)(2,1)} %param.22) | copy-start | bytes 6291460
  7.2 6.2 copy-start.62
  7.2 6.2 copy-start.63
  7.2 133.8 %all-gather.5.cloned.1.call-start = ((), (), s32[]{:S(2)}) async-start(), calls=%async_computation.6 | async-start | bytes 9437184 | tf_op jit(solution)/shard_map/all_gather | solution.py:131
  13.3 383.6 %reduce-scatter.7.cloned.1.call-start = ((), (), s32[]{:S(2)}) async-start(), calls=%async_computation.7 | async-start | bytes 9437184 | tf_op jit(solution)/shard_map/reduce_scatter | solution.py:173
  13.4 139.4 %copy-start.55 = (f32[64]{0:T(128)}, f32[64]{0:T(128)S(1)}, u32[]{:S(2)}) copy-start(f32[64]{0:T(128)S(1)} %convert_element_type.295) | copy-start | bytes 772
  13.4 134.6 %copy-start.53 = (f32[64]{0:T(128)}, f32[64]{0:T(128)S(1)}, u32[]{:S(2)}) copy-start(f32[64]{0:T(128)S(1)} %convert_element_type.298) | copy-start | bytes 772
  14.5 140.0 %copy-start.15 = (f32[2048,32]{0,1:T(8,128)}, f32[2048,32]{0,1:T(8,128)S(1)}, u32[]{:S(2)}) copy-start(f32[2048,32]{0,1:T(8,128)S(1)} %get-tuple-element.427) | copy-start | bytes 786436
  14.5 140.0 %copy-start.17 = (f32[2048,32]{0,1:T(8,128)}, f32[2048,32]{0,1:T(8,128)S(1)}, u32[]{:S(2)}) copy-start(f32[2048,32]{0,1:T(8,128)S(1)} %get-tuple-element.428) | copy-start | bytes 786436
  141.1 9.3 copy-start.2
  141.1 9.3 copy-start.26
  161.1 6.9 copy-start.24
  161.1 6.9 copy-start.40
  240.0 9.5 copy-start.8
  249.5 147.4 %copy-start.4 = (bf16[256,2048]{1,0:T(8,128)(2,1)S(1)}, bf16[256,2048]{1,0:T(8,128)(2,1)}, u32[]{:S(2)}) copy-start(bf16[256,2048]{1,0:T(8,128)(2,1)} %param.19) | copy-start | bytes 3145732
  249.5 151.7 %copy-start.58 = (s32[256]{0:T(256)S(1)}, s32[256]{0:T(256)}, u32[]{:S(2)}) copy-start(s32[256]{0:T(256)} %param.32) | copy-start | bytes 3076
  249.6 276.7 %all-gather.7.cloned.1.call-start = ((), (), s32[]{:S(2)}) async-start(), calls=%async_computation.8 | async-start | bytes 9437184 | tf_op jit(solution)/shard_map/all_gather | solution.py:181
  250.2 606.9 %copy-start.32 = (f32[2048]{0:T(1024)}, f32[2048]{0:T(1024)S(1)}, u32[]{:S(2)}) copy-start(f32[2048]{0:T(1024)S(1)} %convert_element_type.305) | copy-start | bytes 24580
  398.6 458.5 %copy-start.42 = (f32[256]{0:T(256)}, f32[256]{0:T(256)S(1)}, u32[]{:S(2)}) copy-start(f32[256]{0:T(256)S(1)} %fusion.101) | copy-start | bytes 3076
  401.2 250.9 %all-gather.9.cloned.1.call-start = ((), (), s32[]{:S(2)}) async-start(), calls=%async_computation.10 | async-start | bytes 9437184 | tf_op jit(solution)/shard_map/all_gather | solution.py:194
  445.1 412.0 %copy-start.47 = (f32[256]{0:T(256)}, f32[256]{0:T(256)S(1)}, u32[]{:S(2)}) copy-start(f32[256]{0:T(256)S(1)} %select_reduce_fusion) | copy-start | bytes 3076
  447.6 406.4 %reduce-scatter.11.cloned.1.call-start = ((), (), s32[]{:S(2)}) async-start(), calls=%async_computation.11 | async-start | bytes 9437184 | tf_op jit(solution)/shard_map/reduce_scatter | solution.py:200
  526.3 14.6 copy-start.59
  526.3 14.6 copy-start.60
  675.2 15.5 copy-start.61
  706.6 278.8 %all-gather.11.cloned.1.call-start = ((), (), s32[]{:S(2)}) async-start(), calls=%async_computation.12 | async-start | bytes 9437184 | tf_op jit(solution)/shard_map/all_gather | solution.py:211
  861.4 469.2 %reduce-scatter.15.cloned.1.call-start = ((), (), s32[]{:S(2)}) async-start(), calls=%async_computation.14 | async-start | bytes 2359296 | tf_op jit(solution)/shard_map/reduce_scatter | solution.py:305
  992.4 8.5 copy-start.12
  1000.9 254.7 %copy-start.16 = (f32[2048,32]{0,1:T(8,128)S(1)}, f32[2048,32]{0,1:T(8,128)}, u32[]{:S(2)}) copy-start(f32[2048,32]{0,1:T(8,128)} %copy-done.15) | copy-start | bytes 786436
  1262.7 137.0 %reduce-scatter.17.cloned.1.call-start = ((), (), s32[]{:S(2)}) async-start(), calls=%async_computation.15 | async-start | bytes 2359296 | tf_op jit(solution)/shard_map/reduce_scatter | solution.py:308
  1262.8 14.1 copy-start.65
  1276.9 13.2 copy-start.23
  1297.6 370.8 %all-reduce.13.cloned.1.call-start = ((), (), s32[]{:S(2)}) async-start(), calls=%async_computation.16 | async-start | bytes 30408704 | tf_op jit(solution)/shard_map/psum | solution.py:326
  1318.7 8.3 slice-start
  1319.9 7.1 slice-start.1
  1399.7 421.5 %reduce-scatter.13.cloned.1.call-start = ((), (), s32[]{:S(2)}) async-start(), calls=%async_computation.13 | async-start | bytes 9437184 | tf_op jit(solution)/shard_map/reduce_scatter | solution.py:291
  1400.1 10.5 copy-start.27
  1434.6 539.1 %reduce-scatter.9.cloned.1.call-start = ((), (), s32[]{:S(2)}) async-start(), calls=%async_computation.9 | async-start | bytes 9437184 | tf_op jit(solution)/shard_map/reduce_scatter | solution.py:187
  1668.4 9.2 copy-start.21
  1686.5 134.7 %copy-start.5 = (bf16[256,2048]{1,0:T(8,128)(2,1)S(1)}, bf16[256,2048]{1,0:T(8,128)(2,1)}, u32[]{:S(2)}) copy-start(bf16[256,2048]{1,0:T(8,128)(2,1)} %param.19) | copy-start | bytes 3145732
  1686.5 134.7 %copy-start.37 = (f32[2048]{0:T(1024)S(1)}, f32[2048]{0:T(1024)}, u32[]{:S(2)}) copy-start(f32[2048]{0:T(1024)} %copy-done.36) | copy-start | bytes 24580
  1686.5 134.7 %copy-start.45 = (f32[256]{0:T(256)S(1)}, f32[256]{0:T(256)}, u32[]{:S(2)}) copy-start(f32[256]{0:T(256)} %copy-done.44) | copy-start | bytes 3076
  1686.5 137.0 %copy-start.46 = (bf16[2048]{0:T(1024)(128)(2,1)S(1)}, bf16[2048]{0:T(1024)(128)(2,1)}, u32[]{:S(2)}) copy-start(bf16[2048]{0:T(1024)(128)(2,1)} %get-tuple-element.345) | copy-start | bytes 12292
  1686.5 166.1 %copy-start.50 = (f32[256]{0:T(256)S(1)}, f32[256]{0:T(256)}, u32[]{:S(2)}) copy-start(f32[256]{0:T(256)} %copy-done.49) | copy-start | bytes 3076
  1686.5 287.1 %copy-start.33 = (f32[2048]{0:T(1024)S(1)}, f32[2048]{0:T(1024)}, u32[]{:S(2)}) copy-start(f32[2048]{0:T(1024)} %copy-done.32) | copy-start | bytes 24580
  1686.5 287.1 %copy-start.43 = (f32[256]{0:T(256)S(1)}, f32[256]{0:T(256)}, u32[]{:S(2)}) copy-start(f32[256]{0:T(256)} %copy-done.42) | copy-start | bytes 3076
  1686.5 287.1 %copy-start.48 = (f32[256]{0:T(256)S(1)}, f32[256]{0:T(256)}, u32[]{:S(2)}) copy-start(f32[256]{0:T(256)} %copy-done.47) | copy-start | bytes 3076
  1686.6 287.1 %copy-start.52 = (f32[256]{0:T(256)S(1)}, f32[256]{0:T(256)}, u32[]{:S(2)}) copy-start(f32[256]{0:T(256)} %copy-done.51) | copy-start | bytes 3076
  (43 other events, 121.9 us)
Sparse Core Ops, SparseCore 0:
  13.4 127.6 all-gather.4
  249.7 147.1 reduce-scatter.6
  401.3 124.9 all-gather.6
  529.1 123.0 all-gather.8
  706.7 147.1 reduce-scatter.10
  861.5 123.9 all-gather.10
  1262.8 65.9 reduce-scatter.14
  1332.9 66.7 reduce-scatter.16
  1404.1 264.3 all-reduce.12
  1671.9 149.2 reduce-scatter.12
  1825.3 148.3 reduce-scatter.8
where the time goes:
time: 2000 us; the launch traced here: 1990 us
  waiting for transfers between devices  1260 us (63%)
  matrix products  369 us (18%)
  other arithmetic  141 us (7%)
  local copies, waits for them, and re-layouts  107 us (5%)
  blocking collectives  69 us (3%)
  loops' own time  21.9 us (1%)
    psum x1, waiting for transfers between devices, shards(): lax.psum(query_weight_grad.astype(jnp.bfloat16), 'narrow')  217 us
    reduce_scatter x1, waiting for transfers between devices, shards(): lax.psum_scatter((contract_last(gate_low, gate_weight) + contract_last(up...  147 us
    reduce_scatter x1, waiting for transfers between devices, shards(): lax.psum_scatter(plain_product(mixed_low, output_weight).astype(jnp.bfloa...  147 us
    reduce_scatter x1, waiting for transfers between devices, shards(): lax.psum_scatter((contract_last(query_grad, query_weight) + jnp.einsum('r...  130 us
    all_gather x1, waiting for transfers between devices, shards(): hidden_one = lax.all_gather(hidden_local, 'wide', axis=0, tiled=True)  127 us
    all_gather x1, waiting for transfers between devices, shards(): lax.all_gather(middle_grad.astype(jnp.bfloat16), 'wide', axis=0, tiled=True)  124 us
    reduce_scatter x1, waiting for transfers between devices, shards(): lax.psum_scatter(plain_product(activated, down_weight).astype(jnp.bfloat1...  121 us
    all_gather x1, waiting for transfers between devices, shards(): lax.all_gather(out_cot.astype(jnp.bfloat16), 'wide', axis=0, tiled=True)  100 us
  transfers between devices with their start and end apart: 11, of which 10 were waited for; matrix products, arithmetic and copies ran while one was open for 9% of the time, Pallas kernels for 0%

commit v1 on v0

v1 whole, which is shorter than its diff:
```python
import numpy as np

import jax
import jax.numpy as jnp
from jax import lax
from jax.experimental import pallas as pl
from jax.experimental.pallas import tpu as pltpu
from jax.sharding import PartitionSpec as P

SEQ = 2048
epsilon = 1e-06
rope_base = 10000.0
BLOCK = 256
NEG = -1e30


def rope_tables(head_size):
    positions = np.arange(SEQ, dtype=np.float32)
    exponents = np.arange(head_size // 2, dtype=np.float32) * np.float32(2.0 / head_size)
    frequency = np.power(np.float32(rope_base), -exponents).astype(np.float32)
    angles = (positions[:, None] * frequency[None, :]).astype(np.float32)
    cosine, sine = np.cos(angles).astype(np.float32), np.sin(angles).astype(np.float32)
    return (
        np.concatenate([cosine, cosine], axis=1),
        np.concatenate([-sine, sine], axis=1),
    )


def dot_nn(left, right):
    return jnp.dot(left, right, preferred_element_type=jnp.float32)


def dot_nt(left, right):
    return lax.dot_general(
        left, right, (((1,), (1,)), ((), ())), preferred_element_type=jnp.float32
    )


def lane_ids(shape):
    return lax.broadcasted_iota(jnp.int32, shape, 1)


def group_ones(width, head_size):
    rows = lax.broadcasted_iota(jnp.int32, (width, width), 0) // head_size
    columns = lax.broadcasted_iota(jnp.int32, (width, width), 1) // head_size
    return jnp.where(rows == columns, 1.0, 0.0).astype(jnp.bfloat16)


def group_sum(values, ones):
    top = values.astype(jnp.bfloat16)
    rest = (values - top.astype(jnp.float32)).astype(jnp.bfloat16)
    return dot_nn(top, ones) + dot_nn(rest, ones)


def swap_halves(values, head_size):
    width, half = values.shape[1], head_size // 2
    if width == head_size:
        return jnp.concatenate([values[:, half:], values[:, :half]], axis=1)
    ahead = pltpu.roll(values, width - half, 1)
    behind = pltpu.roll(values, half, 1)
    return jnp.where(lane_ids(values.shape) % head_size < half, ahead, behind)


def tiled(values, count):
    return jnp.concatenate([values] * count, axis=1) if count > 1 else values


def split_raw(raw, width, head_size, heads):
    query = raw[:, :width]
    key = tiled(raw[:, width : width + head_size], heads)
    value = tiled(raw[:, width + head_size :], heads)
    return query, key, value


def head_masks(block, width, head_size, heads):
    group = lane_ids((block, width)) // head_size
    return [group == h for h in range(heads)]


def attention_forward(raw, query_gain, key_gain, segments, first_block):
    head_size = query_gain.shape[0]
    rows = raw.shape[0]
    heads = raw.shape[1] // head_size - 2
    width = heads * head_size
    seqs, blocks, block = rows // SEQ, SEQ // BLOCK, BLOCK
    scale = head_size ** (-0.5)

    def kernel(
        first_ref, raw_ref, qg_ref, kg_ref, cos_ref, sin_ref, segq_ref, segk_ref,
        mixed_ref, lse_ref, query_ref, key_ref, value_ref, keyt_ref,
        keys, values_t, masked, top, total, acc,
    ):
        s, i = pl.program_id(0), pl.program_id(1)
        cosine, sine = tiled(cos_ref[...], heads), tiled(sin_ref[...], heads)
        ones = group_ones(width, head_size)
        query, key, value = split_raw(raw_ref[...], width, head_size, heads)

        def norm_rope(x, gain):
            x = x * lax.rsqrt(group_sum(x * x, ones) * (1.0 / head_size) + epsilon) * gain
            return x * cosine + swap_halves(x, head_size) * sine

        query_low = norm_rope(query, qg_ref[...]).astype(jnp.bfloat16)
        key_rot = norm_rope(key, kg_ref[...])
        key_low = key_rot.astype(jnp.bfloat16)
        query_ref[...] = query_low
        key_ref[...] = key_low
        value_ref[...] = value.astype(jnp.bfloat16)
        keyt_ref[0] = jnp.transpose(key_rot)[:head_size].astype(jnp.bfloat16)
        keys[pl.ds(pl.multiple_of(i * block, block), block), :] = key_low
        values_t[i] = jnp.transpose(value)[:head_size].astype(jnp.bfloat16)
        scaled = query_low * jnp.bfloat16(scale)
        zero = jnp.zeros_like(scaled)
        for h, mask in enumerate(head_masks(block, width, head_size, heads)):
            masked[h] = jnp.where(mask, scaled, zero)
        top[...] = jnp.full_like(top, NEG)
        total[...] = jnp.zeros_like(total)
        acc[...] = jnp.zeros_like(acc)
        query_pos = i * block + lax.broadcasted_iota(jnp.int32, (block, block), 1)
        segment_query = segq_ref[0]

        def step(j, carry):
            at = pl.multiple_of(j * block, block)
            key_pos = at + lax.broadcasted_iota(jnp.int32, (block, block), 0)
            allowed = (key_pos <= query_pos) & (segk_ref[pl.ds(at, block), :] == segment_query)
            bias = jnp.where(allowed, 0.0, NEG)
            key_block = keys[pl.ds(at, block), :]
            value_t = values_t[j]
            for h in range(heads):
                scores = dot_nt(key_block, masked[h]) + bias
                before = top[h : h + 1, :]
                now = jnp.maximum(before, jnp.max(scores, axis=0, keepdims=True))
                shifted = jnp.exp(scores - now)
                fade = jnp.exp(before - now)
                top[h : h + 1, :] = now
                total[h : h + 1, :] = fade * total[h : h + 1, :] + jnp.sum(
                    shifted, axis=0, keepdims=True
                )
                span = slice(h * head_size, (h + 1) * head_size)
                acc[span, :] = fade * acc[span, :] + dot_nn(value_t, shifted.astype(jnp.bfloat16))
            return carry

        lax.fori_loop(first_ref[s, i], i + 1, step, 0)
        for h in range(heads):
            span = slice(h * head_size, (h + 1) * head_size)
            acc[span, :] = acc[span, :] / total[h : h + 1, :]
        mixed_ref[...] = jnp.transpose(acc[...]).astype(jnp.bfloat16)
        lse_ref[...] = top[...] + jnp.log(jnp.maximum(total[...], 1e-30))

    cosine, sine = rope_tables(head_size)
    at_rows = lambda s, i, first: (s * blocks + i, 0)
    fixed = lambda s, i, first: (0, 0)
    at_lanes = lambda s, i, first: (0, s * blocks + i)
    low = jnp.bfloat16
    pairs = blocks * (blocks + 1) // 2 * seqs * heads
    return pl.pallas_call(
        kernel,
        grid_spec=pltpu.PrefetchScalarGridSpec(
            num_scalar_prefetch=1,
            grid=(seqs, blocks),
            in_specs=[
                pl.BlockSpec((block, raw.shape[1]), at_rows),
                pl.BlockSpec((1, width), fixed),
                pl.BlockSpec((1, width), fixed),
                pl.BlockSpec((block, head_size), lambda s, i, first: (i, 0)),
                pl.BlockSpec((block, head_size), lambda s, i, first: (i, 0)),
                pl.BlockSpec((1, 1, block), lambda s, i, first: (s, 0, i)),
                pl.BlockSpec((SEQ, 1), lambda s, i, first: (s, 0)),
            ],
            out_specs=[
                pl.BlockSpec((block, width), at_rows),
                pl.BlockSpec((8, block), at_lanes),
                pl.BlockSpec((block, width), at_rows),
                pl.BlockSpec((block, width), at_rows),
                pl.BlockSpec((block, width), at_rows),
                pl.BlockSpec((1, head_size, block), lambda s, i, first: (s * blocks + i, 0, 0)),
            ],
            scratch_shapes=[
                pltpu.VMEM((SEQ, width), low),
                pltpu.VMEM((blocks, head_size, block), low),
                pltpu.VMEM((heads, block, width), low),
                pltpu.VMEM((8, block), jnp.float32),
                pltpu.VMEM((8, block), jnp.float32),
                pltpu.VMEM((width, block), jnp.float32),
            ],
        ),
        out_shape=[
            jax.ShapeDtypeStruct((rows, width), low),
            jax.ShapeDtypeStruct((8, rows), jnp.float32),
            jax.ShapeDtypeStruct((rows, width), low),
            jax.ShapeDtypeStruct((rows, width), low),
            jax.ShapeDtypeStruct((rows, width), low),
            jax.ShapeDtypeStruct((rows // block, head_size, block), low),
        ],
        compiler_params=pltpu.CompilerParams(vmem_limit_bytes=40 << 20),
        cost_estimate=pl.CostEstimate(
            flops=pairs * block * block * head_size * 8,
            bytes_accessed=rows * width * 16,
            transcendentals=pairs * block * block,
        ),
        name="attention_forward",
    )(
        first_block, raw,
        tiled(query_gain.astype(jnp.float32)[None], heads),
        tiled(key_gain.astype(jnp.float32)[None], heads),
        cosine, sine, segments[:, None, :], segments.reshape(rows, 1),
    )


def attention_backward(
    raw, query_gain, key_gain, segments, first_block, saved, mixed_grad
):
    mixed, lse, query_low, key_low, value_low, key_t = saved
    head_size = query_gain.shape[0]
    rows, width = mixed.shape
    heads = width // head_size
    seqs, blocks, block = rows // SEQ, SEQ // BLOCK, BLOCK
    scale = head_size ** (-0.5)

    def kernel(
        first_ref, raw_ref, qg_ref, kg_ref, cos_ref, sin_ref, segq_ref, segk_ref,
        mixed_ref, lse_ref, query_ref, grad_ref, keys_ref, values_ref, keyt_ref,
        out_ref, qgg_ref, kgg_ref,
        masked, masked_grad, key_sums, value_sums, query_sums, deltas,
    ):
        s, i = pl.program_id(0), blocks - 1 - pl.program_id(1)

        @pl.when(pl.program_id(1) == 0)
        def _():
            key_sums[...] = jnp.zeros_like(key_sums)
            value_sums[...] = jnp.zeros_like(value_sums)

        @pl.when((pl.program_id(1) == 0) & (s == 0))
        def _():
            qgg_ref[...] = jnp.zeros_like(qgg_ref)
            kgg_ref[...] = jnp.zeros_like(kgg_ref)

        query_sums[...] = jnp.zeros_like(query_sums)
        grad = grad_ref[...]
        scaled = query_ref[...] * jnp.bfloat16(scale)
        zero = jnp.zeros_like(scaled)
        for h, mask in enumerate(head_masks(block, width, head_size, heads)):
            span = slice(h * block, (h + 1) * block)
            masked[span, :] = jnp.where(mask, scaled, zero)
            masked_grad[span, :] = jnp.where(mask, grad, zero)
        product = jnp.transpose(grad.astype(jnp.float32) * mixed_ref[...].astype(jnp.float32))
        for h in range(heads):
            deltas[h : h + 1, :] = jnp.sum(
                product[h * head_size : (h + 1) * head_size], axis=0, keepdims=True
            )
        query_pos = i * block + lax.broadcasted_iota(jnp.int32, (block, block), 1)
        segment_query = segq_ref[0]

        def step(j, carry):
            at = pl.multiple_of(j * block, block)
            key_pos = at + lax.broadcasted_iota(jnp.int32, (block, block), 0)
            allowed = (key_pos <= query_pos) & (segk_ref[pl.ds(at, block), :] == segment_query)
            bias = jnp.where(allowed, 0.0, NEG)
            key_block = keys_ref[pl.ds(at, block), :]
            value_block = values_ref[pl.ds(at, block), :]
            key_t = keyt_ref[j]
            lows, grads = [], []
            for h in range(heads):
                span = slice(h * block, (h + 1) * block)
                scores = dot_nt(key_block, masked[span, :]) + bias
                probability = jnp.exp(scores - lse_ref[h : h + 1, :])
                prob_grad = dot_nt(value_block, masked_grad[span, :])
                score_grad = (probability * (prob_grad - deltas[h : h + 1, :])).astype(jnp.bfloat16)
                lows.append(probability.astype(jnp.bfloat16))
                grads.append(score_grad)
                rows_h = slice(h * head_size, (h + 1) * head_size)
                query_sums[rows_h, :] += dot_nn(key_t, score_grad)
            value_sums[pl.ds(at, block), :] += dot_nn(
                jnp.concatenate(lows, axis=1), masked_grad[...]
            )
            key_sums[pl.ds(at, block), :] += dot_nn(jnp.concatenate(grads, axis=1), masked[...])
            return carry

        lax.fori_loop(first_ref[s, i], i + 1, step, 0)
        cosine, sine = tiled(cos_ref[...], heads), tiled(sin_ref[...], heads)
        ones = group_ones(width, head_size)
        query, key, _ = split_raw(raw_ref[...], width, head_size, heads)

        def all_heads(x):
            total = x
            for h in range(1, heads):
                total = total + pltpu.roll(x, h * head_size, 1)
            return total

        def norm_rope_back(x, up, gain):
            unrot = up * cosine - swap_halves(up, head_size) * sine
            inverse = lax.rsqrt(group_sum(x * x, ones) * (1.0 / head_size) + epsilon)
            gain_part = jnp.sum(unrot * x * inverse, axis=0, keepdims=True)
            scaled_up = unrot * gain
            mean = group_sum(scaled_up * x, ones) * (1.0 / head_size)
            return scaled_up * inverse - x * (mean * inverse * inverse * inverse), gain_part

        query_up = jnp.transpose(query_sums[...]) * scale
        query_grad, query_part = norm_rope_back(query, query_up, qg_ref[...])
        here = pl.ds(pl.multiple_of(i * block, block), block)
        key_up = all_heads(key_sums[here, :])
        key_grad, key_part = norm_rope_back(key, key_up, kg_ref[...])
        value_grad = all_heads(value_sums[here, :])
        out_ref[...] = jnp.concatenate(
            [query_grad, key_grad[:, :head_size], value_grad[:, :head_size]], axis=1
        ).astype(jnp.bfloat16)
        qgg_ref[...] += query_part
        kgg_ref[...] += key_part

    cosine, sine = rope_tables(head_size)
    at_rows = lambda s, i, first: (s * blocks + blocks - 1 - i, 0)
    fixed = lambda s, i, first: (0, 0)
    at_lanes = lambda s, i, first: (0, s * blocks + blocks - 1 - i)
    at_seq = lambda s, i, first: (s, 0)
    low = jnp.bfloat16
    pairs = blocks * (blocks + 1) // 2 * seqs * heads
    grads, query_part, key_part = pl.pallas_call(
        kernel,
        grid_spec=pltpu.PrefetchScalarGridSpec(
            num_scalar_prefetch=1,
            grid=(seqs, blocks),
            in_specs=[
                pl.BlockSpec((block, raw.shape[1]), at_rows),
                pl.BlockSpec((1, width), fixed),
                pl.BlockSpec((1, width), fixed),
                pl.BlockSpec((block, head_size), lambda s, i, first: (blocks - 1 - i, 0)),
                pl.BlockSpec((block, head_size), lambda s, i, first: (blocks - 1 - i, 0)),
                pl.BlockSpec((1, 1, block), lambda s, i, first: (s, 0, blocks - 1 - i)),
                pl.BlockSpec((SEQ, 1), at_seq),
                pl.BlockSpec((block, width), at_rows),
                pl.BlockSpec((8, block), at_lanes),
                pl.BlockSpec((block, width), at_rows),
                pl.BlockSpec((block, width), at_rows),
                pl.BlockSpec((SEQ, width), at_seq),
                pl.BlockSpec((SEQ, width), at_seq),
                pl.BlockSpec((blocks, head_size, block), lambda s, i, first: (s, 0, 0)),
            ],
            out_specs=[
                pl.BlockSpec((block, raw.shape[1]), at_rows),
                pl.BlockSpec((1, width), fixed),
                pl.BlockSpec((1, width), fixed),
            ],
            scratch_shapes=[
                pltpu.VMEM((heads * block, width), low),
                pltpu.VMEM((heads * block, width), low),
                pltpu.VMEM((SEQ, width), jnp.float32),
                pltpu.VMEM((SEQ, width), jnp.float32),
                pltpu.VMEM((width, block), jnp.float32),
                pltpu.VMEM((8, block), jnp.float32),
            ],
        ),
        out_shape=[
            jax.ShapeDtypeStruct(raw.shape, low),
            jax.ShapeDtypeStruct((1, width), jnp.float32),
            jax.ShapeDtypeStruct((1, width), jnp.float32),
        ],
        compiler_params=pltpu.CompilerParams(vmem_limit_bytes=48 << 20),
        cost_estimate=pl.CostEstimate(
            flops=pairs * block * block * head_size * 20,
            bytes_accessed=rows * width * 24,
            transcendentals=pairs * block * block,
        ),
        name="attention_backward",
    )(
        first_block, raw,
        tiled(query_gain.astype(jnp.float32)[None], heads),
        tiled(key_gain.astype(jnp.float32)[None], heads),
        cosine, sine, segments[:, None, :], segments.reshape(rows, 1),
        mixed, lse, query_low, mixed_grad, key_low, value_low, key_t,
    )
    return (
        grads,
        jnp.sum(query_part.reshape(heads, head_size), axis=0),
        key_part[0, :head_size],
    )


def first_blocks(segments):
    starts = segments[:, :: BLOCK]
    below = jnp.sum(segments[:, None, :] < starts[:, :, None], axis=-1, dtype=jnp.int32)
    return below // BLOCK

MESH = pl.DeviceIdType.MESH


class Lattice:
    def __init__(self, count):
        self.depth = count // 2
        me = lax.axis_index("wide")
        self.z, self.x = me // 2, me % 2
        self.below = jnp.minimum(self.z, self.depth - 1 - self.z)
        self.low_side = self.z > self.depth - 1 - self.z

    def at(self, z, x):
        return z * 2 + x

    def order(self, m):
        near = m <= 2 * self.below
        r = jnp.where(near, (m + 1) // 2, m - self.below)
        minus = jnp.where(near, m % 2 == 1, self.low_side)
        return jnp.where(minus, self.z - r, self.z + r), r


def greet(lat):
    barrier = pltpu.get_barrier_semaphore()
    last = lat.depth - 1

    def each(act):
        act(lat.at(lat.z, 1 - lat.x))

        @pl.when(lat.z > 0)
        def _():
            act(lat.at(lat.z - 1, lat.x))

        @pl.when(lat.z < last)
        def _():
            act(lat.at(lat.z + 1, lat.x))

    each(lambda who: pl.semaphore_signal(barrier, inc=1, device_id={"wide": who}, device_id_type=MESH))
    pl.semaphore_wait(barrier, 1 + jnp.minimum(lat.z, 1) + jnp.minimum(last - lat.z, 1))


def gather_chunks(lat, full, send_sems, recv_sems, compute):
    z, x, depth = lat.z, lat.x, lat.depth
    last = depth - 1

    def copy(chunk, way, slot, target):
        return pltpu.make_async_remote_copy(
            src_ref=full.at[chunk], dst_ref=full.at[chunk],
            send_sem=send_sems.at[way, slot], recv_sem=recv_sems.at[chunk],
            device_id={"wide": target}, device_id_type=MESH,
        )

    def up(zz):
        return copy(lat.at(zz, x), 0, zz, lat.at(z + 1, x))

    def down(zz):
        return copy(lat.at(zz, x), 1, zz, lat.at(z - 1, x))

    def across(zz):
        return copy(lat.at(zz, x), 2, zz, lat.at(z, 1 - x))

    def arrived(chunk):
        copy(chunk, 2, 0, lat.at(z, 1 - x)).wait_recv()

    @pl.when(z < last)
    def _():
        up(z).start()

    @pl.when(z > 0)
    def _():
        down(z).start()

    across(z).start()

    def step(m, carry):
        zz, r = lat.order(m)
        _, before = lat.order(m - 1)

        @pl.when((m >= 1) & (m < depth) & (r != before))
        def _():
            @pl.when(z - r >= 0)
            def _():
                arrived(lat.at(z - r, x))

                @pl.when(z < last)
                def _():
                    up(z - r).start()

                across(z - r).start()

            @pl.when(z + r <= last)
            def _():
                arrived(lat.at(z + r, x))

                @pl.when(z > 0)
                def _():
                    down(z + r).start()

                across(z + r).start()

        mirror = lat.order(jnp.maximum(m - 1, 0))[0]

        def part(p, carry):
            @pl.when((p == 0) & (m < depth))
            def _():
                pass

            @pl.when((p == 1) & (m >= 1))
            def _():
                arrived(lat.at(mirror, 1 - x))

            @pl.when(((p == 0) & (m < depth)) | ((p == 1) & (m >= 1)))
            def _():
                compute(jnp.where(p == 0, lat.at(zz, x), lat.at(mirror, 1 - x)))

            return carry

        return lax.fori_loop(0, 2, part, carry)

    lax.fori_loop(0, depth + 1, step, 0)

    def settle(zz, carry):
        @pl.when((z < last) & (zz <= z))
        def _():
            up(zz).wait_send()

        @pl.when((z > 0) & (zz >= z))
        def _():
            down(zz).wait_send()

        across(zz).wait_send()
        return carry

    lax.fori_loop(0, depth, settle, 0)


def project_gathered(local, weights, wide_count, collective_id):
    rows, model = local.shape
    columns = weights.shape[1]
    depth = wide_count // 2

    def kernel(local_ref, weights_ref, full_ref, out_ref, full, send_sems, recv_sems, load_sem, store_sems):
        lat = Lattice(wide_count)
        me = lat.at(lat.z, lat.x)
        load = pltpu.make_async_copy(local_ref, full.at[me], load_sem)
        load.start()
        greet(lat)
        load.wait()

        def keep(chunk):
            return pltpu.make_async_copy(full.at[chunk], full_ref.at[chunk], store_sems.at[chunk])

        def compute(chunk):
            keep(chunk).start()
            at = pl.multiple_of(chunk * rows, rows)
            out_ref[pl.ds(at, rows), :] = jnp.dot(
                full[chunk], weights_ref[...], preferred_element_type=jnp.float32
            )

        gather_chunks(lat, full, send_sems, recv_sems, compute)
        lax.fori_loop(0, wide_count, lambda c, carry: (keep(c).wait(), carry)[1], 0)

    full, out = pl.pallas_call(
        kernel,
        in_specs=[pl.BlockSpec(memory_space=pl.ANY), pl.BlockSpec(memory_space=pltpu.VMEM)],
        out_specs=[pl.BlockSpec(memory_space=pl.ANY), pl.BlockSpec(memory_space=pltpu.VMEM)],
        out_shape=[
            jax.ShapeDtypeStruct((wide_count, rows, model), local.dtype),
            jax.ShapeDtypeStruct((wide_count * rows, columns), jnp.float32),
        ],
        scratch_shapes=[
            pltpu.VMEM((wide_count, rows, model), local.dtype),
            pltpu.SemaphoreType.DMA((3, depth)),
            pltpu.SemaphoreType.DMA((wide_count,)),
            pltpu.SemaphoreType.DMA,
            pltpu.SemaphoreType.DMA((wide_count,)),
        ],
        compiler_params=pltpu.CompilerParams(
            collective_id=collective_id, has_side_effects=True, vmem_limit_bytes=32 << 20
        ),
        name="project_gathered",
    )(local, weights)
    return full.reshape(wide_count * rows, model), out


def nt(left, right):
    return lax.dot_general(
        left, right, (((1,), (1,)), ((), ())), preferred_element_type=jnp.float32
    )


def forward_gathered(local, gate_weight, up_weight, down_weight, wide_count, collective_id):
    rows, model = local.shape
    hidden = gate_weight.shape[1]
    depth = wide_count // 2
    tile = min(256, hidden)
    wide_tile = min(512, model)

    def kernel(
        local_ref, gate_ref, up_ref, down_ref, full_ref, gates_ref, ups_ref, acts_ref, downs_ref,
        full, gates, ups, acts, downs, send_sems, recv_sems, load_sem, store_sems,
    ):
        lat = Lattice(wide_count)
        me = lat.at(lat.z, lat.x)
        load = pltpu.make_async_copy(local_ref, full.at[me], load_sem)
        load.start()
        greet(lat)
        load.wait()
        kept = ((full, full_ref), (gates, gates_ref), (ups, ups_ref), (acts, acts_ref), (downs, downs_ref))

        def keep(which, chunk):
            source, target = kept[which]
            return pltpu.make_async_copy(source.at[chunk], target.at[chunk], store_sems.at[which, chunk])

        def compute(chunk):
            keep(0, chunk).start()
            rows_in = full[chunk]

            def inner(t, carry):
                at = pl.ds(pl.multiple_of(t * tile, tile), tile)
                gate = jnp.dot(rows_in, gate_ref[:, at], preferred_element_type=jnp.float32)
                up = jnp.dot(rows_in, up_ref[:, at], preferred_element_type=jnp.float32)
                gates[chunk, :, at] = gate
                ups[chunk, :, at] = up
                acts[chunk, :, at] = (gate * lax.logistic(gate) * up).astype(jnp.bfloat16)
                return carry

            lax.fori_loop(0, hidden // tile, inner, 0)
            for which in (1, 2, 3):
                keep(which, chunk).start()
            act = acts[chunk]

            def outer(t, carry):
                at = pl.ds(pl.multiple_of(t * wide_tile, wide_tile), wide_tile)
                downs[chunk, :, at] = jnp.dot(
                    act, down_ref[:, at], preferred_element_type=jnp.float32
                ).astype(jnp.bfloat16)
                return carry

            lax.fori_loop(0, model // wide_tile, outer, 0)
            keep(4, chunk).start()

        gather_chunks(lat, full, send_sems, recv_sems, compute)
        for which in range(5):
            lax.fori_loop(0, wide_count, lambda c, carry: (keep(which, c).wait(), carry)[1], 0)

    low = jnp.bfloat16
    outs = [
        ((wide_count, rows, model), low),
        ((wide_count, rows, hidden), jnp.float32),
        ((wide_count, rows, hidden), jnp.float32),
        ((wide_count, rows, hidden), low),
        ((wide_count, rows, model), low),
    ]
    vmem = pl.BlockSpec(memory_space=pltpu.VMEM)
    hbm = pl.BlockSpec(memory_space=pl.ANY)
    results = pl.pallas_call(
        kernel,
        in_specs=[hbm, vmem, vmem, vmem],
        out_specs=[hbm] * 5,
        out_shape=[jax.ShapeDtypeStruct(*o) for o in outs],
        scratch_shapes=[pltpu.VMEM(*o) for o in outs]
        + [
            pltpu.SemaphoreType.DMA((3, depth)),
            pltpu.SemaphoreType.DMA((wide_count,)),
            pltpu.SemaphoreType.DMA,
            pltpu.SemaphoreType.DMA((5, wide_count)),
        ],
        compiler_params=pltpu.CompilerParams(
            collective_id=collective_id, has_side_effects=True, vmem_limit_bytes=60 << 20
        ),
        name="forward_gathered",
    )(local, gate_weight, up_weight, down_weight)
    return [r.reshape(wide_count * rows, r.shape[2]) for r in results]


def backward_scattered(
    cot, gates, ups, gate_weight, up_weight, down_weight, wide_count, collective_id
):
    model = cot.shape[1]
    rows = cot.shape[0] // wide_count
    hidden = gate_weight.shape[1]
    depth = wide_count // 2
    tile = min(256, hidden)
    wide_tile = min(512, model)
    low = jnp.bfloat16

    def kernel(
        cot_ref, gates_ref, ups_ref, gate_ref, up_ref, down_ref, sum_ref, gate_low_ref, up_low_ref,
        cots, gate_in, up_in, gate_low, up_low, foreign, own, crossed, from_low, from_high,
        in_sems, out_sems, cross_send, cross_recv, chain_send, low_recv, high_recv,
    ):
        lat = Lattice(wide_count)
        z, x, last = lat.z, lat.x, depth - 1

        def place(e):
            zz = lat.order(depth - 1 - e % depth)[0]
            return zz, lat.at(zz, jnp.where(e < depth, 1 - x, x))

        def loads(e):
            slot = e % 2
            chunk = place(e)[1]
            return [
                pltpu.make_async_copy(source.at[chunk], target.at[slot], in_sems.at[k, slot])
                for k, (source, target) in enumerate(
                    ((cot_ref, cots), (gates_ref, gate_in), (ups_ref, up_in))
                )
            ]

        def stores(e):
            slot = e % 2
            chunk = place(e)[1]
            return [
                pltpu.make_async_copy(source.at[slot], target.at[chunk], out_sems.at[k, slot])
                for k, (source, target) in enumerate(((gate_low, gate_low_ref), (up_low, up_low_ref)))
            ]

        def cross(zz):
            return pltpu.make_async_remote_copy(
                src_ref=foreign.at[zz], dst_ref=crossed.at[zz],
                send_sem=cross_send.at[zz], recv_sem=cross_recv.at[zz],
                device_id={"wide": lat.at(z, 1 - x)}, device_id_type=MESH,
            )

        def rise(zz):
            return pltpu.make_async_remote_copy(
                src_ref=own.at[zz], dst_ref=from_low.at[zz],
                send_sem=chain_send.at[zz], recv_sem=low_recv.at[zz],
                device_id={"wide": lat.at(z + 1, x)}, device_id_type=MESH,
            )

        def sink(zz):
            return pltpu.make_async_remote_copy(
                src_ref=own.at[zz], dst_ref=from_high.at[zz],
                send_sem=chain_send.at[zz], recv_sem=high_recv.at[zz],
                device_id={"wide": lat.at(z - 1, x)}, device_id_type=MESH,
            )

        for copy in loads(0):
            copy.start()
        greet(lat)

        def partial(e, target, zz):
            slot = e % 2
            for copy in loads(e):
                copy.wait()

            @pl.when(e + 1 < 2 * depth)
            def _():
                for copy in loads(e + 1):
                    copy.start()

            @pl.when(e >= 2)
            def _():
                for copy in stores(e - 2):
                    copy.wait()

            cot_rows = cots[slot]

            def inner(t, carry):
                at = pl.ds(pl.multiple_of(t * tile, tile), tile)
                act_grad = nt(cot_rows, down_ref[at, :])
                gate, up = gate_in[slot, :, at], up_in[slot, :, at]
                sigmoid = lax.logistic(gate)
                gate_low[slot, :, at] = (
                    act_grad * up * sigmoid * (1.0 + gate * (1.0 - sigmoid))
                ).astype(low)
                up_low[slot, :, at] = (act_grad * gate * sigmoid).astype(low)
                return carry

            lax.fori_loop(0, hidden // tile, inner, 0)
            for copy in stores(e):
                copy.start()
            gate_rows, up_rows = gate_low[slot], up_low[slot]

            def outer(t, carry):
                at = pl.ds(pl.multiple_of(t * wide_tile, wide_tile), wide_tile)
                target[zz, :, at] = (
                    nt(gate_rows, gate_ref[at, :]) + nt(up_rows, up_ref[at, :])
                ).astype(low)
                return carry

            lax.fori_loop(0, model // wide_tile, outer, 0)

        def send_step(e, carry):
            zz, _ = place(e)
            partial(e, foreign, zz)
            cross(zz).start()
            return carry

        lax.fori_loop(0, depth, send_step, 0)

        def chain_step(e, carry):
            zz, _ = place(e)
            partial(e, own, zz)
            cross(zz).wait_recv()
            wide = jnp.float32

            @pl.when((zz > z) & (z > 0))
            def _():
                rise(zz).wait_recv()
                own[zz] = (own[zz].astype(wide) + crossed[zz].astype(wide) + from_low[zz].astype(wide)).astype(low)

            @pl.when((zz < z) & (z < last))
            def _():
                sink(zz).wait_recv()
                own[zz] = (own[zz].astype(wide) + crossed[zz].astype(wide) + from_high[zz].astype(wide)).astype(low)

            @pl.when(((zz > z) & (z == 0)) | ((zz < z) & (z == last)))
            def _():
                own[zz] = (own[zz].astype(wide) + crossed[zz].astype(wide)).astype(low)

            @pl.when(zz > z)
            def _():
                rise(zz).start()

            @pl.when(zz < z)
            def _():
                sink(zz).start()

            @pl.when(zz == z)
            def _():
                sum_ref[...] = own[zz].astype(wide) + crossed[zz].astype(wide)

                @pl.when(z > 0)
                def _():
                    rise(zz).wait_recv()
                    sum_ref[...] += from_low[zz].astype(wide)

                @pl.when(z < last)
                def _():
                    sink(zz).wait_recv()
                    sum_ref[...] += from_high[zz].astype(wide)

            return carry

        lax.fori_loop(depth, 2 * depth, chain_step, 0)
        for e in (2 * depth - 2, 2 * depth - 1):
            for copy in stores(e):
                copy.wait()

        def settle(zz, carry):
            cross(zz).wait_send()

            @pl.when(zz > z)
            def _():
                rise(zz).wait_send()

            @pl.when(zz < z)
            def _():
                sink(zz).wait_send()

            return carry

        lax.fori_loop(0, depth, settle, 0)

    vmem = pl.BlockSpec(memory_space=pltpu.VMEM)
    hbm = pl.BlockSpec(memory_space=pl.ANY)
    total, gate_low, up_low = pl.pallas_call(
        kernel,
        in_specs=[hbm, hbm, hbm, vmem, vmem, vmem],
        out_specs=[vmem, hbm, hbm],
        out_shape=[
            jax.ShapeDtypeStruct((rows, model), jnp.float32),
            jax.ShapeDtypeStruct((wide_count, rows, hidden), low),
            jax.ShapeDtypeStruct((wide_count, rows, hidden), low),
        ],
        scratch_shapes=[
            pltpu.VMEM((2, rows, model), low),
            pltpu.VMEM((2, rows, hidden), jnp.float32),
            pltpu.VMEM((2, rows, hidden), jnp.float32),
            pltpu.VMEM((2, rows, hidden), low),
            pltpu.VMEM((2, rows, hidden), low),
        ]
        + [pltpu.VMEM((depth, rows, model), low)] * 5
        + [
            pltpu.SemaphoreType.DMA((3, 2)),
            pltpu.SemaphoreType.DMA((2, 2)),
        ]
        + [pltpu.SemaphoreType.DMA((depth,))] * 5,
        compiler_params=pltpu.CompilerParams(
            collective_id=collective_id, has_side_effects=True, vmem_limit_bytes=58 << 20
        ),
        name="backward_scattered",
    )(
        cot.reshape(wide_count, rows, model),
        gates.reshape(wide_count, rows, hidden),
        ups.reshape(wide_count, rows, hidden),
        gate_weight, up_weight, down_weight,
    )
    flat = wide_count * rows
    return total, gate_low.reshape(flat, hidden), up_low.reshape(flat, hidden)


def sum_everywhere(values, counts, collective_id):
    axes = ("narrow", "wide")

    def kernel(in_ref, out_ref, mine, held, total, load_sem, send_sems, recv_sems, wide_send, wide_recv):
        here = [lax.axis_index(axis) for axis in axes]

        def peers(k, act):
            def one(step, carry):
                act((here[k] + step) % counts[k])
                return carry

            lax.fori_loop(1, counts[k], one, 0)

        barrier = pltpu.get_barrier_semaphore()
        for k, axis in enumerate(axes):
            peers(k, lambda who: pl.semaphore_signal(
                barrier, inc=1, device_id={axis: who}, device_id_type=MESH))
        load = pltpu.make_async_copy(in_ref, mine, load_sem)
        load.start()
        load.wait()
        pl.semaphore_wait(barrier, counts[0] + counts[1] - 2)

        def exchange(k, source, slots, sends, recvs, target):
            def copy(who):
                return pltpu.make_async_remote_copy(
                    src_ref=source, dst_ref=slots.at[here[k]],
                    send_sem=sends.at[who], recv_sem=recvs.at[here[k]],
                    device_id={axes[k]: who}, device_id_type=MESH,
                )

            def arrival(who):
                return pltpu.make_async_remote_copy(
                    src_ref=source, dst_ref=slots.at[who],
                    send_sem=sends.at[who], recv_sem=recvs.at[who],
                    device_id={axes[k]: who}, device_id_type=MESH,
                )

            peers(k, lambda who: copy(who).start())
            slots[here[k]] = source[...]
            peers(k, lambda who: arrival(who).wait_recv())
            sums = slots[0]
            for n in range(1, counts[k]):
                sums = sums + slots[n]
            target[...] = sums
            peers(k, lambda who: copy(who).wait_send())

        exchange(0, mine, held.at[0], send_sems, recv_sems, total)
        exchange(1, total, held.at[1], wide_send, wide_recv, out_ref)

    most = max(counts)
    shape = values.shape
    return pl.pallas_call(
        kernel,
        in_specs=[pl.BlockSpec(memory_space=pl.ANY)],
        out_specs=pl.BlockSpec(memory_space=pltpu.VMEM),
        out_shape=jax.ShapeDtypeStruct(shape, jnp.float32),
        scratch_shapes=[
            pltpu.VMEM(shape, jnp.float32),
            pltpu.VMEM((2, most) + shape, jnp.float32),
            pltpu.VMEM(shape, jnp.float32),
            pltpu.SemaphoreType.DMA,
            pltpu.SemaphoreType.DMA((counts[0],)),
            pltpu.SemaphoreType.DMA((counts[0],)),
            pltpu.SemaphoreType.DMA((counts[1],)),
            pltpu.SemaphoreType.DMA((counts[1],)),
        ],
        compiler_params=pltpu.CompilerParams(collective_id=collective_id, has_side_effects=True),
        name="sum_everywhere",
    )(values)

CORPORA = 8
GATHER_BYTES = 8 << 20


def norm_scale(values, scale_gain):
    return (
        values * lax.rsqrt(jnp.mean(values * values, axis=-1, keepdims=True) + epsilon) * scale_gain
    )


def contract_first(left, right):
    return lax.dot_general(
        left, right, (((0,), (0,)), ((), ())), preferred_element_type=jnp.float32
    )


def gather_wide(values):
    return lax.all_gather(values, "wide", axis=0, tiled=True)


def scatter_wide(values):
    return lax.psum_scatter(
        values.astype(jnp.bfloat16), "wide", scatter_dimension=0, tiled=True
    ).astype(jnp.float32)


def own_part(values, axis, index, count):
    size = values.shape[axis] // count
    return lax.dynamic_slice_in_dim(values, index * size, size, axis)


def sum_narrow(values):
    part = lax.psum_scatter(
        values.astype(jnp.bfloat16), "narrow", scatter_dimension=0, tiled=True
    )
    return lax.all_gather(part, "narrow", axis=0, tiled=True).astype(jnp.float32)


def swiglu_back(act_grad, gate_values, up_values):
    sigmoid_gate = lax.logistic(gate_values)
    gate_part = act_grad * up_values * sigmoid_gate * (1.0 + gate_values * (1.0 - sigmoid_gate))
    up_part = act_grad * gate_values * sigmoid_gate
    return (gate_part.astype(jnp.bfloat16), up_part.astype(jnp.bfloat16))


def shards(
    tokens,
    attention_gain,
    query_weight,
    key_weight,
    value_weight,
    query_gain,
    key_gain,
    output_weight,
    feedforward_gain,
    gate_weight,
    up_weight,
    down_weight,
    cotangent,
    corpus_tags,
    segments,
):
    low, wide_type = jnp.bfloat16, jnp.float32
    head_size = query_gain.shape[0]
    own_rows, model_width = tokens.shape
    wide_count, narrow_count = lax.axis_size("wide"), lax.axis_size("narrow")
    wide_index, narrow_index = lax.axis_index("wide"), lax.axis_index("narrow")
    key_total = key_weight.shape[1] // head_size
    width = query_weight.shape[1]
    key_head = wide_index * key_total // wide_count
    all_rows = own_rows * wide_count
    chained = wide_count % 2 == 0 and all_rows * model_width * 2 <= GATHER_BYTES

    tag_hits = corpus_tags[:, None] == jnp.arange(CORPORA, dtype=jnp.int32)[None, :]
    local_counts = jnp.sum(tag_hits.astype(wide_type), axis=0)
    corpus_counts = sum_everywhere(
        jnp.pad(local_counts[None], ((0, 7), (0, 128 - CORPORA))), (narrow_count, wide_count), 1
    )[0, :CORPORA]
    corpus_scale = jnp.sqrt(jnp.sum(corpus_counts) / (CORPORA * corpus_counts))
    row_weight = jnp.sum(jnp.where(tag_hits, corpus_scale[None, :], 0.0), axis=1)
    out_cot = cotangent.astype(wide_type) * row_weight[:, None]
    token_values = tokens.astype(wide_type)
    first_gain = attention_gain.astype(wide_type)
    second_gain = feedforward_gain.astype(wide_type)

    key_columns = lax.dynamic_slice_in_dim(key_weight, key_head * head_size, head_size, 1)
    value_columns = lax.dynamic_slice_in_dim(value_weight, key_head * head_size, head_size, 1)
    own_weights = jnp.concatenate([query_weight, key_columns, value_columns], axis=1)
    output_full = lax.all_gather(
        own_part(output_weight, 0, narrow_index, narrow_count), ("wide", "narrow"), axis=0, tiled=True
    )

    hidden_local = norm_scale(token_values, first_gain).astype(low)
    if chained:
        hidden_one, raw = project_gathered(hidden_local, own_weights, wide_count, 2)
    else:
        hidden_one = gather_wide(hidden_local)
        raw = dot_nn(hidden_one, own_weights)
    cot_local, raw = lax.optimization_barrier((out_cot.astype(low), raw))
    cot_low = gather_wide(cot_local)

    first_block = first_blocks(segments)
    saved = attention_forward(raw, query_gain, key_gain, segments, first_block)
    mixed = lax.all_to_all(saved[0], "wide", split_axis=0, concat_axis=1, tiled=True)
    middle = token_values + dot_nn(mixed, output_full)

    hidden_two_local = norm_scale(middle, second_gain).astype(low)
    if chained:
        hidden_two, gate_values, up_values, activated, down_part = forward_gathered(
            hidden_two_local, gate_weight, up_weight, down_weight, wide_count, 3
        )
        hidden_two_grad, gate_low, up_low = backward_scattered(
            cot_low, gate_values, up_values, gate_weight, up_weight, down_weight, wide_count, 4
        )
        down_part, hidden_two_grad = lax.optimization_barrier((down_part, hidden_two_grad))
    else:
        hidden_two = gather_wide(hidden_two_local)
        gate_values = dot_nn(hidden_two, gate_weight)
        up_values = dot_nn(hidden_two, up_weight)
        activated = (gate_values * lax.logistic(gate_values) * up_values).astype(low)
        down_part = dot_nn(activated, down_weight)
        gate_low, up_low = swiglu_back(dot_nt(cot_low, down_weight), gate_values, up_values)
        hidden_two_grad = scatter_wide(dot_nt(gate_low, gate_weight) + dot_nt(up_low, up_weight))
    result = (middle + scatter_wide(down_part)).astype(low)
    down_grad = sum_narrow(contract_first(activated, cot_low))
    gate_grad = sum_narrow(contract_first(hidden_two, gate_low))
    up_grad = sum_narrow(contract_first(hidden_two, up_low))

    _, second_pull = jax.vjp(norm_scale, middle, second_gain)
    middle_part, second_gain_grad = second_pull(hidden_two_grad)
    middle_grad = out_cot + middle_part
    middle_low = middle_grad.astype(low)
    output_grad = lax.all_gather(
        lax.psum_scatter(
            contract_first(mixed, middle_low).astype(low),
            ("wide", "narrow"),
            scatter_dimension=0,
            tiled=True,
        ),
        "narrow",
        axis=0,
        tiled=True,
    ).astype(wide_type)
    mixed_grad = lax.all_to_all(
        dot_nt(middle_low, output_full).astype(low), "wide", split_axis=1, concat_axis=0, tiled=True
    )
    grads, query_gain_grad, key_gain_grad = attention_backward(
        raw, query_gain, key_gain, segments, first_block, saved, mixed_grad
    )

    query_turned = lax.all_gather(
        jnp.transpose(own_part(query_weight, 1, narrow_index, narrow_count)),
        ("wide", "narrow"),
        axis=0,
        tiled=True,
    )
    sent = lax.all_to_all(grads, "wide", split_axis=0, concat_axis=1, tiled=True).reshape(
        own_rows, wide_count, width + 2 * head_size
    )
    shared = wide_count // key_total

    def key_side(start):
        part = sent[:, :, start : start + head_size]
        if shared > 1:
            part = jnp.sum(
                part.astype(wide_type).reshape(own_rows, key_total, shared, head_size), axis=2
            ).astype(low)
        return part.reshape(own_rows, key_total * head_size)

    hidden_one_grad = (
        dot_nn(sent[:, :, :width].reshape(own_rows, wide_count * width), query_turned)
        + dot_nt(key_side(width), key_weight)
        + dot_nt(key_side(width + head_size), value_weight)
    )
    _, first_pull = jax.vjp(norm_scale, token_values, first_gain)
    token_part, first_gain_grad = first_pull(hidden_one_grad)
    tokens_gradient = (middle_grad + token_part).astype(low)

    weight_grads = contract_first(hidden_one, grads)
    if shared == 1:
        weight_sums = sum_narrow(weight_grads)
        key_weight_grad = weight_sums[:, width : width + head_size]
        value_weight_grad = weight_sums[:, width + head_size :]
    else:
        weight_sums = sum_narrow(weight_grads[:, :width])

        def spread(part):
            whole = jnp.zeros((model_width, key_total * head_size), wide_type)
            whole = lax.dynamic_update_slice_in_dim(whole, part, key_head * head_size, 1)
            share = lax.psum_scatter(whole.astype(low), "wide", scatter_dimension=1, tiled=True)
            return lax.psum(share, "narrow").astype(wide_type)

        key_weight_grad = spread(weight_grads[:, width : width + head_size])
        value_weight_grad = spread(weight_grads[:, width + head_size :])

    gain_parts = jnp.concatenate([first_gain_grad, second_gain_grad, query_gain_grad, key_gain_grad])
    lines = -(-gain_parts.shape[0] // 1024) * 8
    gain_parts = jnp.pad(gain_parts, (0, lines * 128 - gain_parts.shape[0])).reshape(lines, 128)
    gains = sum_everywhere(gain_parts, (narrow_count, wide_count), 5).reshape(-1)
    starts = (0, model_width, 2 * model_width, 2 * model_width + head_size)
    sizes = (model_width, model_width, head_size, head_size)
    first_out, second_out, query_gain_out, key_gain_out = (
        own_part(gains[start : start + size], 0, wide_index, wide_count)
        for start, size in zip(starts, sizes)
    )
    return (
        result,
        tokens_gradient,
        first_out,
        weight_sums[:, :width],
        key_weight_grad,
        value_weight_grad,
        query_gain_out,
        key_gain_out,
        output_grad,
        second_out,
        gate_grad,
        up_grad,
        down_grad,
    )


def solution(mesh):
    rows = P(("narrow", "wide"), None)
    columns, first = P(None, "wide"), P("wide", None)
    return jax.shard_map(
        shards,
        mesh=mesh,
        in_specs=(
            rows, P(), columns, P(), P(), P(), P(), first, P(), columns, columns, first,
            rows, P(("narrow", "wide")), P("narrow", None),
        ),
        out_specs=(
            rows, rows, P("wide"), columns, columns, columns, P("wide"), P("wide"),
            first, P("wide"), columns, columns, first,
        ),
        check_vma=False,
    )
```

time: 2000 us -> 1220 us (0.61)
  waiting for transfers between devices: 1260 us -> 531 us
  Pallas kernels: 0 us -> 465 us
  matrix products: 369 us -> 78.8 us
  other arithmetic: 141 us -> 43.3 us
  local copies, waits for them, and re-layouts: 107 us -> 42.3 us
  blocking collectives: 69 us -> 29.5 us
  loops' own time: 21.9 us -> 0 us
    pallas_call x0 -> x7, Pallas kernels: none -> 465 us  [the longest x1 142 us: forward_gathered(): pl.pallas_call(kernel, in_specs=[hbm, vmem, vmem, vmem], out_specs=[hbm]...]
    reduce_scatter x6, waiting for transfers between devices: 614 us -> 298 us  [the longest x1 127 us: shards(): lax.psum_scatter(contract_first(mixed, middle_low).astype(low), ('wide',...]
    dot_general x44 -> x5, matrix products: 317 us -> 22.7 us  [the longest x2 12.3 us: dot_nn(): return jnp.dot(left, right, preferred_element_type=jnp.float32)]
    all_gather x4 -> x8, waiting for transfers between devices: 429 us -> 186 us  [the longest x4 105 us: sum_narrow(): lax.all_gather(part, 'narrow', axis=0, tiled=True).astype(jnp.float32)]
    psum x1 -> x0, waiting for transfers between devices: 217 us -> none  [shards(): lax.psum(query_weight_grad.astype(jnp.bfloat16), 'narrow')]
    another operation x9 -> x0, other arithmetic: 51.2 us -> none
    psum x2 -> x0, blocking collectives: 48.4 us -> none  [the longest x1 42.4 us: shards(): corpus_counts = lax.psum(local_counts, ('narrow', 'wide'))]
    dynamic_update_slice x8 -> x0, local copies, waits for them, and re-layouts: 46.6 us -> none  [forward_sequence(): return lax.map(forward_block, jnp.arange(block_count))]
  transfers between devices with their start and end apart: 11 -> 16, of which waited for: 10 -> 12; matrix products, arithmetic and copies ran while one was open for 9% -> 12% of each run, Pallas kernels for 0% -> 30%
where the time goes in v1:
time: 1220 us
  waiting for transfers between devices  531 us (44%)
  Pallas kernels  465 us (38%)
  matrix products  78.8 us (6%)
  other arithmetic  43.3 us (4%)
  local copies, waits for them, and re-layouts  42.3 us (3%)
  blocking collectives  29.5 us (2%)
  between operations  14.6 us (1%)
    pallas_call x1, Pallas kernels, forward_gathered(): pl.pallas_call(kernel, in_specs=[hbm, vmem, vmem, vmem], out_specs=[hbm]...  142 us
    pallas_call x1, Pallas kernels, project_gathered(): pl.pallas_call(kernel, in_specs=[pl.BlockSpec(memory_space=pl.ANY), pl.Bl...  130 us
    reduce_scatter x1, waiting for transfers between devices, shards(): lax.psum_scatter(contract_first(mixed, middle_low).astype(low), ('wide',...  127 us
    all_gather x4, waiting for transfers between devices, sum_narrow(): lax.all_gather(part, 'narrow', axis=0, tiled=True).astype(jnp.float32)  105 us
    reduce_scatter x1, waiting for transfers between devices, scatter_wide(): lax.psum_scatter(values.astype(jnp.bfloat16), 'wide', scatter_dimension=0...  104 us
    pallas_call x1, Pallas kernels, backward_scattered(): pl.pallas_call(kernel, in_specs=[hbm, hbm, hbm, vmem, vmem, vmem], out_sp...  104 us
    all_gather x1, waiting for transfers between devices, shards(): lax.all_gather(jnp.transpose(own_part(query_weight, 1, narrow_index, narr...  70.4 us
    reduce_scatter x4, waiting for transfers between devices, sum_narrow(): lax.psum_scatter(values.astype(jnp.bfloat16), 'narrow', scatter_dimension...  67.3 us
  transfers between devices with their start and end apart: 16, of which 12 were waited for; matrix products, arithmetic and copies ran while one was open for 12% of the time, Pallas kernels for 30%

profile of v1, /device:TPU:0, one launch (start us, length us, event | category | flops | bytes accessed | tf_op | source)
XLA Modules:
  0.0 1216.1 jit_solution(3234776933878657436)
XLA Ops:
  11.3 12.3 %sum_everywhere.2 = f32[8,128]{1,0:T(8,128)} custom-call(f32[8,128]{1,0:T(8,128)} %pad.8.in_ref), custom_call_target="tpu_custom_call" | custom-call | tf_op jit(solution)/shard_map/sum_everywhere/pallas_call | solution.py:926
  23.6 1.5 fusion.7
  25.2 1.6 constant_dynamic-slice_fusion.2
  28.3 130.0 %project_gathered.1 = (bf16[8,256,2048]{2,1,0:T(8,128)(2,1)S(1)}, f32[2048,384]{1,0:T(8,128)S(1)}) custom-call(bf16[256,2048]{1,0:T(8,128)(2,1)S(1)} %fusion.2.local_ref, bf16[2048,384]{1,0:T(8,128)(2,1)S(1)} %pad_maximum_fusion.weights_ref), custom_call_target="tpu_custom_call" | custom-call | tf_op jit(solution)/shard_map/project_gathered/pallas_call | solution.py:543
  158.3 3.4 copy-done.3
  161.7 1.6 copy-done.4
  168.1 1.9 copy-done.5
  172.5 25.6 %attention_forward.1 = (bf16[2048,256]{1,0:T(8,128)(2,1)S(1)}, f32[8,2048]{1,0:T(8,128)S(1)}, bf16[2048,256]{1,0:T(8,128)(2,1)S(1)}, bf16[2048,256]{1,0:T(8,128)...) custom-call(s32[1,8]{1,0:T(1,128)S(1)} %and_select_fusion.first_ref, ...), custom_call_target="tpu_custom_call" | custom-call | flops 4831838208 | bytes 8388608 | tf_op jit(solution)/shard_map/attention_forward/pallas_call | solution.py:155
  202.3 4.4 all-to-all-start
  206.7 46.1 %all-to-all-done = bf16[8,256,256]{1,2,0:T(8,128)(2,1)} async-done(((bf16[8,256,256]{1,2,0:T(8,128)(2,1)}), bf16[8,256,256]{1,2,0:T(8,128)(2,1)}, u32[]{:S(2)}, u32[]{:S(2)}) %all-to-all-start) | async-done | bytes 1048608 | tf_op jit(solution)/shard_map/all_to_all | solution.py:1048
  252.8 6.4 multiply_reduce_fusion.2
  261.8 142.3 %forward_gathered.1 = (bf16[8,256,2048]{2,1,0:T(8,128)(2,1)}, f32[8,256,1024]{2,1,0:T(8,128)}, f32[8,256,1024]{2,1,0:T(8,128)}, bf16[8,256,1024]{2,1,0:T(8,128)(2,1)}, bf16[8,256,2048]{2,1,0:T(8,128)(2,1)}) custom-call(bf16[256,2048]{1,0:T(8,128)(2,1)} %multiply_convert_fusion.local_ref, bf16[2048,1024]{1,0:T(8,128)(2,1)} %gate_ref.3, ...), custom_call_target="tpu_custom_call" | custom-call | tf_op jit(solution)/shard_map/forward_gathered/pallas_call | solution.py:637
  404.1 103.8 %backward_scattered.1 = (f32[256,2048]{1,0:T(8,128)}, bf16[8,256,1024]{2,1,0:T(8,128)(2,1)}, bf16[8,256,1024]{2,1,0:T(8,128)(2,1)}) custom-call(bf16[8,256,2048]{2,1,0:T(8,128)(2,1)} %bitcast.78, f32[8,256,1024]{2,1,0:T(8,128)} %get-tuple-element.41.gates_ref, f32[8,256,1024]{2,1,0:T(8,128)} %get-tuple-element.42.ups_ref, bf16[2048,1024]{1,0:T(8,128)(2,1)} %gate_ref.3, ...), custom_call_target="tpu_custom_call" | custom-call | tf_op jit(solution)/shard_map/backward_scattered/pallas_call | solution.py:839
  508.0 14.0 %bitcast_convert_fusion = bf16[2048,1024]{1,0:T(8,128)(2,1)} fusion(bf16[8,256,2048]{2,1,0:T(8,128)(2,1)} %get-tuple-element.55, bf16[8,256,1024]{2,1,0:T(8,128)(2,1)} %get-tuple-element.57), kind=kOutput, calls=%fused_computation | convolution fusion | flops 8592031744 | bytes 16777216 | tf_op jit(solution)/shard_map/dot_general | solution.py:956
  522.6 14.0 %bitcast_convert_fusion.1 = bf16[2048,1024]{1,0:T(8,128)(2,1)} fusion(bf16[8,256,2048]{2,1,0:T(8,128)(2,1)} %get-tuple-element.55, bf16[8,256,1024]{2,1,0:T(8,128)(2,1)} %get-tuple-element.56), kind=kOutput, calls=%fused_computation.1 | convolution fusion | flops 8592031744 | bytes 16777216 | tf_op jit(solution)/shard_map/dot_general | solution.py:956
  536.7 14.2 %convolution_convert_fusion.1 = bf16[1024,2048]{1,0:T(8,128)(2,1)} fusion(bf16[2048,1024]{1,0:T(8,128)(2,1)} %bitcast.92, bf16[2048,2048]{1,0:T(8,128)(2,1)} %all-gather.11.cloned.1.call-done), kind=kOutput, calls=%fused_computation.8 | convolution fusion | flops 8592031744 | bytes 16777216 | tf_op jit(solution)/shard_map/dot_general | solution.py:956
  551.1 3.0 multiply_reduce_fusion
  554.1 104.1 %reduce-scatter.7.cloned.1.call-done = bf16[256,2048]{1,0:T(8,128)(2,1)} async-done(((bf16[2048,2048]{1,0:T(8,128)(2,1)}), bf16[256,2048]{1,0:T(8,128)(2,1)}) %reduce-scatter.7.cloned.1.call-update) | async-done | bytes 1048592 | tf_op jit(solution)/shard_map/reduce_scatter | solution.py:966
  658.2 4.6 fusion.4
  662.8 7.2 convolution_convert_fusion.3
  670.1 29.5 %all_to_all.54 = bf16[256,8,256]{2,0,1:T(8,128)(2,1)} all-to-all(bf16[256,8,256]{2,0,1:T(8,128)(2,1)S(1)} %bitcast.80), channel_id=1, replica_groups=mesh['narrow'=4,'wide'=8] {'wide'}, dimensions={1} | all-to-all | bytes 2097152 | tf_op jit(solution)/shard_map/all_to_all | solution.py:1088
  699.7 38.5 %attention_backward.1 = (bf16[2048,384]{1,0:T(8,128)(2,1)}, f32[1,256]{1,0:T(1,128)S(1)}, f32[1,256]{1,0:T(1,128)S(1)}) custom-call(s32[1,8]{1,0:T(1,128)S(1)} %and_select_fusion.first_ref, f32[2048,384]{1,0:T(8,128)} %copy-done.4, f32[1,256]{1,0:T(1,128)S(1)} %get-tuple-element.130.qg_ref, f32[1,256]{1,0:T(1,128)S(1)} %get-tuple-element.131.kg_ref, ...), custom_call_target="tpu_custom_call" | custom-call | flops 12079595520 | bytes 12582912 | tf_op jit(solution)/shard_map/attention_backward/pallas_call | solution.py:316
  738.1 7.0 convolution_convert_fusion.2
  746.0 6.4 reduce-scatter.13.cloned.1.call-done
  752.4 47.0 %reduce-scatter.17.cloned.1.call-done = bf16[256,2048]{1,0:T(8,128)(2,1)} async-done(((bf16[1024,2048]{1,0:T(8,128)(2,1)}), bf16[256,2048]{1,0:T(8,128)(2,1)}) %reduce-scatter.17.cloned.1.call-update) | async-done | bytes 1048592 | tf_op jit(solution)/shard_map/reduce_scatter | solution.py:977
  801.7 6.8 convolution_convert_fusion
  808.6 2.6 copy.60
  811.3 5.4 all-to-all-start.2
  816.8 14.0 %reduce-scatter.9.cloned.1.call-done = bf16[512,384]{1,0:T(8,128)(2,1)} async-done(((bf16[2048,384]{1,0:T(8,128)(2,1)}), bf16[512,384]{1,0:T(8,128)(2,1)}) %reduce-scatter.9.cloned.1.call-update) | async-done | bytes 393232 | tf_op jit(solution)/shard_map/reduce_scatter | solution.py:977
  831.0 35.9 %all-gather.21.cloned.1.call-done = bf16[2048,1024]{1,0:T(8,128)(2,1)} async-done(((bf16[512,1024]{1,0:T(8,128)(2,1)}), bf16[2048,1024]{1,0:T(8,128)(2,1)}) %all-gather.21.cloned.1.call-update) | async-done | bytes 4194320 | tf_op jit(solution)/shard_map/all_gather | solution.py:980
  866.9 6.6 convert_element_type.109
  873.5 29.5 %all-gather.19.cloned.1.call-done = bf16[2048,1024]{1,0:T(8,128)(2,1)} async-done(((bf16[512,1024]{1,0:T(8,128)(2,1)}), bf16[2048,1024]{1,0:T(8,128)(2,1)}) %all-gather.19.cloned.1.call-update) | async-done | bytes 4194320 | tf_op jit(solution)/shard_map/all_gather | solution.py:980
  903.0 6.6 convert_element_type.107
  909.7 29.4 %all-gather.23.cloned.1.call-done = bf16[1024,2048]{1,0:T(8,128)(2,1)} async-done(((bf16[256,2048]{1,0:T(8,128)(2,1)}), bf16[1024,2048]{1,0:T(8,128)(2,1)}) %all-gather.23.cloned.1.call-update) | async-done | bytes 4194320 | tf_op jit(solution)/shard_map/all_gather | solution.py:980
  939.0 6.7 convert_element_type.111
  948.3 1.8 fusion.15
  950.1 70.4 %all-gather.13.cloned.1.call-done = bf16[2048,2048]{1,0:T(8,128)(2,1)} async-done(((bf16[64,2048]{1,0:T(8,128)(2,1)}), bf16[2048,2048]{1,0:T(8,128)(2,1)}) %all-gather.13.cloned.1.call-update) | async-done | bytes 8388624 | tf_op jit(solution)/shard_map/all_gather | solution.py:1095
  1020.5 5.9 fusion.17
  1028.5 2.4 fusion.3
  1031.6 12.7 %sum_everywhere.3 = f32[40,128]{1,0:T(8,128)} custom-call(f32[40,128]{1,0:T(8,128)} %pad_bitcast_fusion.in_ref), custom_call_target="tpu_custom_call" | custom-call | tf_op jit(solution)/shard_map/sum_everywhere/pallas_call | solution.py:926
  1044.3 126.7 %reduce-scatter.11.cloned.1.call-done = bf16[64,2048]{1,0:T(8,128)(2,1)} async-done(((bf16[2048,2048]{1,0:T(8,128)(2,1)}), bf16[64,2048]{1,0:T(8,128)(2,1)}) %reduce-scatter.11.cloned.1.call-update) | async-done | bytes 262160 | tf_op jit(solution)/shard_map/reduce_scatter | solution.py:1078
  1175.0 3.3 fusion.6
  1178.3 10.0 all-gather.15.cloned.1.call-done
  1188.3 2.4 fusion.14
  1190.7 2.5 copy.64
  1194.3 1.5 slice.66
  1195.8 10.8 all-gather.17.cloned.1.call-done
  1206.5 2.8 convert_element_type.105
  (133 shorter events, 34.5 us)
Async XLA Ops:
  7.2 1.2 copy-start
  7.2 19.6 %copy-start.23 = (bf16[2048,256]{1,0:T(8,128)(2,1)S(1)}, bf16[2048,256]{1,0:T(8,128)(2,1)}, u32[]{:S(2)}) copy-start(bf16[2048,256]{1,0:T(8,128)(2,1)} %param.21) | copy-start | bytes 3145732
  7.2 245.6 %all-gather.9.cloned.1.call-start = ((), (), s32[]{:S(2)}) async-start(), calls=%async_computation.9 | async-start | bytes 8650752 | tf_op jit(solution)/shard_map/all_gather | solution.py:1033
  9.2 394.9 %all-gather.11.cloned.1.call-start = ((), (), s32[]{:S(2)}) async-start(), calls=%async_computation.10 | async-start | bytes 9437184 | tf_op jit(solution)/shard_map/all_gather | solution.py:962
  26.7 1.2 copy-start.15
  28.0 138.0 %copy-start.26 = (s32[256]{0:T(256)S(1)}, s32[256]{0:T(256)}, u32[]{:S(2)}) copy-start(s32[256]{0:T(256)} %param.32) | copy-start | bytes 3076
  28.0 138.1 %copy-start.20 = (bf16[256,2048]{1,0:T(8,128)(2,1)S(1)}, bf16[256,2048]{1,0:T(8,128)(2,1)}, u32[]{:S(2)}) copy-start(bf16[256,2048]{1,0:T(8,128)(2,1)} %param.31) | copy-start | bytes 3145732
  158.3 3.4 copy-start.3
  161.7 1.6 copy-start.4
  163.3 4.0 copy-start.2
  166.1 1.7 copy-start.27
  166.1 1.7 copy-start.28
  168.1 1.9 copy-start.5
  170.0 1.2 copy-start.6
  171.2 1.2 copy-start.8
  198.0 1.0 copy-start.10
  199.0 1.0 copy-start.12
  200.0 1.0 copy-start.13
  201.0 5.7 copy-start.25
  202.3 50.5 %all-to-all-start = ((bf16[8,256,256]{1,2,0:T(8,128)(2,1)}), bf16[8,256,256]{1,2,0:T(8,128)(2,1)}, u32[]{:S(2)}, u32[]{:S(2)}) async-start(bf16[8,256,256]{1,2,0:T(8,128)(2,1)} %copy.57), calls=%async_computation | async-start | bytes 2097152 | tf_op jit(solution)/shard_map/all_to_all | solution.py:1048
  206.6 451.6 %reduce-scatter.7.cloned.1.call-start = ((), (), s32[]{:S(2)}) async-start(), calls=%async_computation.11 | async-start | bytes 9437184 | tf_op jit(solution)/shard_map/reduce_scatter | solution.py:966
  259.3 1.3 copy-start.14
  508.0 237.3 %reduce-scatter.15.cloned.1.call-start = ((), (), s32[]{:S(2)}) async-start(), calls=%async_computation.19 | async-start | bytes 5242880 | tf_op jit(solution)/shard_map/reduce_scatter | solution.py:977
  522.0 230.4 %reduce-scatter.13.cloned.1.call-start = ((), (), s32[]{:S(2)}) async-start(), calls=%async_computation.17 | async-start | bytes 5242880 | tf_op jit(solution)/shard_map/reduce_scatter | solution.py:977
  536.7 262.8 %reduce-scatter.17.cloned.1.call-start = ((), (), s32[]{:S(2)}) async-start(), calls=%async_computation.21 | async-start | bytes 5242880 | tf_op jit(solution)/shard_map/reduce_scatter | solution.py:977
  550.9 279.8 %reduce-scatter.9.cloned.1.call-start = ((), (), s32[]{:S(2)}) async-start(), calls=%async_computation.13 | async-start | bytes 1966080 | tf_op jit(solution)/shard_map/reduce_scatter | solution.py:977
  662.8 7.2 copy-start.17
  670.0 29.7 %copy-start.7 = (f32[2048,64]{1,0:T(8,128)S(1)}, f32[2048,64]{1,0:T(8,128)}, u32[]{:S(2)}) copy-start(f32[2048,64]{1,0:T(8,128)} %constant.64.clone.cos_ref) | copy-start | bytes 1572868
  670.0 29.7 %copy-start.9 = (f32[2048,64]{1,0:T(8,128)S(1)}, f32[2048,64]{1,0:T(8,128)}, u32[]{:S(2)}) copy-start(f32[2048,64]{1,0:T(8,128)} %constant.65.clone.sin_ref) | copy-start | bytes 1572868
  670.0 29.7 %copy-start.11 = (bf16[2048,256]{1,0:T(8,128)(2,1)S(1)}, bf16[2048,256]{1,0:T(8,128)(2,1)}, u32[]{:S(2)}) copy-start(bf16[2048,256]{1,0:T(8,128)(2,1)} %copy-done.10) | copy-start | bytes 3145732
  670.0 68.1 %slice-start = ((s8[8388608]{0:T(1024)(128)(4,1)}), s8[4194304]{0:T(1024)(128)(4,1)S(1)}, s32[]{:S(2)}) async-start(s8[8388608]{0:T(1024)(128)(4,1)} %bitcast.74), calls=%async_computation.23 | async-start | bytes 8388608
  699.6 38.5 %slice-start.1 = ((s8[8388608]{0:T(1024)(128)(4,1)}), s8[4194304]{0:T(1024)(128)(4,1)S(1)}, s32[]{:S(2)}) async-start(s8[8388608]{0:T(1024)(128)(4,1)} %bitcast.74), calls=%async_computation.24 | async-start | bytes 8388608
  745.2 121.7 %all-gather.21.cloned.1.call-start = ((), (), s32[]{:S(2)}) async-start(), calls=%async_computation.20 | async-start | bytes 5242880 | tf_op jit(solution)/shard_map/all_gather | solution.py:980
  746.0 157.1 %all-gather.19.cloned.1.call-start = ((), (), s32[]{:S(2)}) async-start(), calls=%async_computation.18 | async-start | bytes 5242880 | tf_op jit(solution)/shard_map/all_gather | solution.py:980
  752.4 49.4 %copy-start.18 = (f32[256,2048]{1,0:T(8,128)S(1)}, f32[256,2048]{1,0:T(8,128)}, u32[]{:S(2)}) copy-start(f32[256,2048]{1,0:T(8,128)} %copy-done.17) | copy-start | bytes 6291460
  752.4 186.6 %all-gather.23.cloned.1.call-start = ((), (), s32[]{:S(2)}) async-start(), calls=%async_computation.22 | async-start | bytes 5242880 | tf_op jit(solution)/shard_map/all_gather | solution.py:980
  799.5 221.0 %all-gather.13.cloned.1.call-start = ((), (), s32[]{:S(2)}) async-start(), calls=%async_computation.12 | async-start | bytes 8650752 | tf_op jit(solution)/shard_map/all_gather | solution.py:1095
  801.7 369.3 %reduce-scatter.11.cloned.1.call-start = ((), (), s32[]{:S(2)}) async-start(), calls=%async_computation.15 | async-start | bytes 8650752 | tf_op jit(solution)/shard_map/reduce_scatter | solution.py:1078
  811.3 135.7 %all-to-all-start.2 = ((bf16[8,256,384]{1,2,0:T(8,128)(2,1)}), bf16[8,256,384]{1,2,0:T(8,128)(2,1)}, u32[]{:S(2)}, u32[]{:S(2)}) async-start(bf16[8,256,384]{1,2,0:T(8,128)(2,1)} %copy.60), calls=%async_computation.3 | async-start | bytes 3145728 | tf_op jit(solution)/shard_map/all_to_all | solution.py:1101
  816.7 371.6 %all-gather.15.cloned.1.call-start = ((), (), s32[]{:S(2)}) async-start(), calls=%async_computation.14 | async-start | bytes 1966080 | tf_op jit(solution)/shard_map/all_gather | solution.py:980
  830.8 375.8 %all-gather.17.cloned.1.call-start = ((), (), s32[]{:S(2)}) async-start(), calls=%async_computation.16 | async-start | bytes 1310720 | tf_op jit(solution)/shard_map/all_gather | solution.py:1077
  1020.5 5.9 copy-start.21
  1020.5 5.9 copy-start.24
  1026.4 1.4 copy-start.16
  1026.4 2.1 copy-start.22
  1190.7 3.6 copy-start.19
  1194.3 15.0 %copy-start.1 = (bf16[256,2048]{1,0:T(8,128)(2,1)S(1)}, bf16[256,2048]{1,0:T(8,128)(2,1)}, u32[]{:S(2)}) copy-start(bf16[256,2048]{1,0:T(8,128)(2,1)} %param.26) | copy-start | bytes 3145732
Sparse Core Ops, SparseCore 0:
  11.5 109.0 all-gather.8
  167.4 158.8 all-gather.10
  508.1 150.0 reduce-scatter.6
  661.3 43.4 reduce-scatter.14
  707.8 44.5 reduce-scatter.12
  754.9 44.4 reduce-scatter.16
  802.5 28.1 reduce-scatter.8
  832.4 34.4 all-gather.20
  868.5 34.4 all-gather.18
  904.5 34.4 all-gather.22
  942.9 77.5 all-gather.12
  1022.7 148.2 reduce-scatter.10
  1172.7 15.5 all-gather.14
  1189.8 16.7 all-gather.16

commit v2 on v1

--- a/solution.py
+++ b/solution.py
@@ -192,11 +192,7 @@
             jax.ShapeDtypeStruct((rows // block, head_size, block), low),
         ],
         compiler_params=pltpu.CompilerParams(vmem_limit_bytes=40 << 20),
-        cost_estimate=pl.CostEstimate(
-            flops=pairs * block * block * head_size * 8,
-            bytes_accessed=rows * width * 16,
-            transcendentals=pairs * block * block,
-        ),
+        cost_estimate=pl.CostEstimate(flops=0, bytes_accessed=0, transcendentals=0),
         name="attention_forward",
     )(
         first_block, raw,
@@ -354,11 +350,7 @@
             jax.ShapeDtypeStruct((1, width), jnp.float32),
         ],
         compiler_params=pltpu.CompilerParams(vmem_limit_bytes=48 << 20),
-        cost_estimate=pl.CostEstimate(
-            flops=pairs * block * block * head_size * 20,
-            bytes_accessed=rows * width * 24,
-            transcendentals=pairs * block * block,
-        ),
+        cost_estimate=pl.CostEstimate(flops=0, bytes_accessed=0, transcendentals=0),
         name="attention_backward",
     )(
         first_block, raw,
@@ -400,9 +392,13 @@
         return jnp.where(minus, self.z - r, self.z + r), r
 
 
-def greet(lat):
+def greet(lat, partners=()):
     barrier = pltpu.get_barrier_semaphore()
     last = lat.depth - 1
+    for partner in partners:
+        pl.semaphore_signal(
+            barrier, inc=1, device_id={"narrow": partner}, device_id_type=MESH
+        )
 
     def each(act):
         act(lat.at(lat.z, 1 - lat.x))
@@ -416,41 +412,48 @@
             act(lat.at(lat.z + 1, lat.x))
 
     each(lambda who: pl.semaphore_signal(barrier, inc=1, device_id={"wide": who}, device_id_type=MESH))
-    pl.semaphore_wait(barrier, 1 + jnp.minimum(lat.z, 1) + jnp.minimum(last - lat.z, 1))
-
-
-def gather_chunks(lat, full, send_sems, recv_sems, compute):
+    own = 1 + len(partners)
+    pl.semaphore_wait(barrier, own + jnp.minimum(lat.z, 1) + jnp.minimum(last - lat.z, 1))
+
+
+def gather_chunks(lat, buffers, send_sems, recv_sems, compute, meanwhile=None, landed=None):
     z, x, depth = lat.z, lat.x, lat.depth
     last = depth - 1
-
-    def copy(chunk, way, slot, target):
+    every = range(len(buffers))
+
+    def copy(k, chunk, way, slot, target):
         return pltpu.make_async_remote_copy(
-            src_ref=full.at[chunk], dst_ref=full.at[chunk],
-            send_sem=send_sems.at[way, slot], recv_sem=recv_sems.at[chunk],
+            src_ref=buffers[k].at[chunk], dst_ref=buffers[k].at[chunk],
+            send_sem=send_sems.at[k, way, slot], recv_sem=recv_sems.at[k, chunk],
             device_id={"wide": target}, device_id_type=MESH,
         )
 
-    def up(zz):
-        return copy(lat.at(zz, x), 0, zz, lat.at(z + 1, x))
-
-    def down(zz):
-        return copy(lat.at(zz, x), 1, zz, lat.at(z - 1, x))
-
-    def across(zz):
-        return copy(lat.at(zz, x), 2, zz, lat.at(z, 1 - x))
-
-    def arrived(chunk):
-        copy(chunk, 2, 0, lat.at(z, 1 - x)).wait_recv()
-
-    @pl.when(z < last)
-    def _():
-        up(z).start()
-
-    @pl.when(z > 0)
-    def _():
-        down(z).start()
-
-    across(z).start()
+    def up(k, zz):
+        return copy(k, lat.at(zz, x), 0, zz, lat.at(z + 1, x))
+
+    def down(k, zz):
+        return copy(k, lat.at(zz, x), 1, zz, lat.at(z - 1, x))
+
+    def across(k, zz):
+        return copy(k, lat.at(zz, x), 2, zz, lat.at(z, 1 - x))
+
+    def arrived(k, chunk):
+        copy(k, chunk, 2, 0, lat.at(z, 1 - x)).wait_recv()
+        if landed is not None:
+            landed(k, chunk)
+
+    for k in every:
+        @pl.when(z < last)
+        def _():
+            up(k, z).start()
+
+        @pl.when(z > 0)
+        def _():
+            down(k, z).start()
+
+        across(k, z).start()
+    if meanwhile is not None:
+        meanwhile()
 
     def step(m, carry):
         zz, r = lat.order(m)
@@ -458,36 +461,34 @@
 
         @pl.when((m >= 1) & (m < depth) & (r != before))
         def _():
-            @pl.when(z - r >= 0)
-            def _():
-                arrived(lat.at(z - r, x))
-
-                @pl.when(z < last)
+            for k in every:
+                @pl.when(z - r >= 0)
                 def _():
-                    up(z - r).start()
-
-                across(z - r).start()
-
-            @pl.when(z + r <= last)
-            def _():
-                arrived(lat.at(z + r, x))
-
-                @pl.when(z > 0)
+                    arrived(k, lat.at(z - r, x))
+
+                    @pl.when(z < last)
+                    def _():
+                        up(k, z - r).start()
+
+                    across(k, z - r).start()
+
+                @pl.when(z + r <= last)
                 def _():
-                    down(z + r).start()
-
-                across(z + r).start()
+                    arrived(k, lat.at(z + r, x))
+
+                    @pl.when(z > 0)
+                    def _():
+                        down(k, z + r).start()
+
+                    across(k, z + r).start()
 
         mirror = lat.order(jnp.maximum(m - 1, 0))[0]
 
         def part(p, carry):
-            @pl.when((p == 0) & (m < depth))
-            def _():
-                pass
-
             @pl.when((p == 1) & (m >= 1))
             def _():
-                arrived(lat.at(mirror, 1 - x))
+                for k in every:
+                    arrived(k, lat.at(mirror, 1 - x))
 
             @pl.when(((p == 0) & (m < depth)) | ((p == 1) & (m >= 1)))
             def _():
@@ -500,67 +501,180 @@
     lax.fori_loop(0, depth + 1, step, 0)
 
     def settle(zz, carry):
-        @pl.when((z < last) & (zz <= z))
-        def _():
-            up(zz).wait_send()
-
-        @pl.when((z > 0) & (zz >= z))
-        def _():
-            down(zz).wait_send()
-
-        across(zz).wait_send()
+        for k in every:
+            @pl.when((z < last) & (zz <= z))
+            def _():
+                up(k, zz).wait_send()
+
+            @pl.when((z > 0) & (zz >= z))
+            def _():
+                down(k, zz).wait_send()
+
+            across(k, zz).wait_send()
         return carry
 
     lax.fori_loop(0, depth, settle, 0)
 
 
-def project_gathered(local, weights, wide_count, collective_id):
+def project_gathered(local, weights, values, strips, counts, collective_id):
     rows, model = local.shape
     columns = weights.shape[1]
+    narrow_count, wide_count = counts
     depth = wide_count // 2
-
-    def kernel(local_ref, weights_ref, full_ref, out_ref, full, send_sems, recv_sems, load_sem, store_sems):
+    strip = strips[0].shape[0]
+    tall = strip * len(strips)
+
+    def kernel(
+        local_ref, weights_ref, values_ref, *refs
+    ):
+        strip_refs, refs = refs[: len(strips)], refs[len(strips) :]
+        full_ref, out_ref, sum_ref, refs = refs[0], refs[1], refs[2], refs[3:]
+        spread_refs, refs = refs[: len(strips)], refs[len(strips) :]
+        (full, spread, send_sems, recv_sems, own_sems, store_sems, spread_sems, y_send, core_send, spread_recv,
+         mine, held, total, load_sem, *sems) = refs
         lat = Lattice(wide_count)
         me = lat.at(lat.z, lat.x)
-        load = pltpu.make_async_copy(local_ref, full.at[me], load_sem)
-        load.start()
-        greet(lat)
-        load.wait()
+        narrow_me = lax.axis_index("narrow")
+        core_side, y_side = narrow_me + 1 - 2 * (narrow_me % 2), (narrow_me + 2) % 4
+        corner = y_side + 1 - 2 * (y_side % 2)
+        loads = [
+            pltpu.make_async_copy(local_ref, full.at[me], own_sems.at[0]),
+            pltpu.make_async_copy(values_ref, mine, load_sem),
+        ] + [
+            pltpu.make_async_copy(
+                ref, spread.at[narrow_me, me, pl.ds(k * strip, strip)], own_sems.at[1 + k]
+            )
+            for k, ref in enumerate(strip_refs)
+        ]
+        for load in loads:
+            load.start()
+        arrive = greet_all(counts)
+        for load in loads:
+            load.wait()
+        arrive()
+        narrow, wide = exchange_pair(counts, mine, held, total, *sems)
+
+        def to_side(n, chunk, target, send_sem):
+            return pltpu.make_async_remote_copy(
+                src_ref=spread.at[n, chunk], dst_ref=spread.at[n, chunk],
+                send_sem=send_sem, recv_sem=spread_recv.at[n, chunk],
+                device_id={"narrow": target}, device_id_type=MESH,
+            )
+
+        def to_y(chunk):
+            return to_side(narrow_me, chunk, y_side, y_send.at[chunk])
+
+        def to_core(n, chunk):
+            return to_side(n, chunk, core_side, core_send.at[n // 2, chunk])
+
+        def spread_out(chunk):
+            to_y(chunk).start()
+            to_core(narrow_me, chunk).start()
+
+        def landed(k, chunk):
+            if k == 0:
+                spread_out(chunk)
+
+        def meanwhile():
+            spread_out(me)
+            narrow.start()
+            total[...] = narrow.total()
+            wide.start()
 
         def keep(chunk):
             return pltpu.make_async_copy(full.at[chunk], full_ref.at[chunk], store_sems.at[chunk])
 
+        def keep_strip(n, chunk, k):
+            return pltpu.make_async_copy(
+                spread.at[n, chunk, pl.ds(k * strip, strip)], spread_refs[k].at[n, chunk],
+                spread_sems.at[k, n, chunk],
+            )
+
+        def keep_strips(n, chunk):
+            for k in range(len(strips)):
+                keep_strip(n, chunk, k).start()
+
         def compute(chunk):
             keep(chunk).start()
+            keep_strips(narrow_me, chunk)
             at = pl.multiple_of(chunk * rows, rows)
             out_ref[pl.ds(at, rows), :] = jnp.dot(
                 full[chunk], weights_ref[...], preferred_element_type=jnp.float32
             )
 
-        gather_chunks(lat, full, send_sems, recv_sems, compute)
-        lax.fori_loop(0, wide_count, lambda c, carry: (keep(c).wait(), carry)[1], 0)
-
-    full, out = pl.pallas_call(
+        gather_chunks(
+            lat, [spread.at[narrow_me], full], send_sems, recv_sems, compute, meanwhile, landed
+        )
+
+        def event(e):
+            zz = lat.order(e // 2)[0]
+            return lat.at(zz, jnp.where(e % 2 == 0, lat.x, 1 - lat.x))
+
+        def pass_on(e, carry):
+            chunk = event(e)
+            to_side(y_side, chunk, y_side, y_send.at[chunk]).wait_recv()
+            to_core(y_side, chunk).start()
+            keep_strips(y_side, chunk)
+            return carry
+
+        def take(e, carry):
+            chunk = event(e)
+            for n in (core_side, corner):
+                to_side(n, chunk, core_side, core_send.at[0, chunk]).wait_recv()
+                keep_strips(n, chunk)
+            return carry
+
+        lax.fori_loop(0, wide_count, pass_on, 0)
+        lax.fori_loop(0, wide_count, take, 0)
+        sum_ref[...] = wide.total()
+        narrow.settle()
+        wide.settle()
+
+        def settle(c, carry):
+            keep(c).wait()
+            to_y(c).wait_send()
+            to_core(narrow_me, c).wait_send()
+            to_core(y_side, c).wait_send()
+            for k in range(len(strips)):
+                for n in range(narrow_count):
+                    keep_strip(n, c, k).wait()
+            return carry
+
+        lax.fori_loop(0, wide_count, settle, 0)
+
+    vmem = pl.BlockSpec(memory_space=pltpu.VMEM)
+    hbm = pl.BlockSpec(memory_space=pl.ANY)
+    low = local.dtype
+    full, out, sums, *gathered = pl.pallas_call(
         kernel,
-        in_specs=[pl.BlockSpec(memory_space=pl.ANY), pl.BlockSpec(memory_space=pltpu.VMEM)],
-        out_specs=[pl.BlockSpec(memory_space=pl.ANY), pl.BlockSpec(memory_space=pltpu.VMEM)],
+        in_specs=[hbm, vmem, hbm] + [hbm] * len(strips),
+        out_specs=[hbm, vmem, vmem] + [hbm] * len(strips),
         out_shape=[
-            jax.ShapeDtypeStruct((wide_count, rows, model), local.dtype),
+            jax.ShapeDtypeStruct((wide_count, rows, model), low),
             jax.ShapeDtypeStruct((wide_count * rows, columns), jnp.float32),
-        ],
+            jax.ShapeDtypeStruct(values.shape, jnp.float32),
+        ]
+        + [jax.ShapeDtypeStruct((narrow_count, wide_count, strip, model), low)] * len(strips),
         scratch_shapes=[
-            pltpu.VMEM((wide_count, rows, model), local.dtype),
-            pltpu.SemaphoreType.DMA((3, depth)),
+            pltpu.VMEM((wide_count, rows, model), low),
+            pltpu.VMEM((narrow_count, wide_count, tall, model), low),
+            pltpu.SemaphoreType.DMA((2, 3, depth)),
+            pltpu.SemaphoreType.DMA((2, wide_count)),
+            pltpu.SemaphoreType.DMA((1 + len(strips),)),
             pltpu.SemaphoreType.DMA((wide_count,)),
-            pltpu.SemaphoreType.DMA,
+            pltpu.SemaphoreType.DMA((len(strips), narrow_count, wide_count)),
             pltpu.SemaphoreType.DMA((wide_count,)),
-        ],
+            pltpu.SemaphoreType.DMA((2, wide_count)),
+            pltpu.SemaphoreType.DMA((narrow_count, wide_count)),
+        ]
+        + exchange_scratch(values.shape, counts),
         compiler_params=pltpu.CompilerParams(
-            collective_id=collective_id, has_side_effects=True, vmem_limit_bytes=32 << 20
+            collective_id=collective_id, has_side_effects=True, vmem_limit_bytes=48 << 20
         ),
         name="project_gathered",
-    )(local, weights)
-    return full.reshape(wide_count * rows, model), out
+    )(local, weights, values, *strips)
+    flat = narrow_count * wide_count * strip
+    return full.reshape(wide_count * rows, model), out, sums, [g.reshape(flat, model) for g in gathered]
 
 
 def nt(left, right):
@@ -620,7 +734,7 @@
             lax.fori_loop(0, model // wide_tile, outer, 0)
             keep(4, chunk).start()
 
-        gather_chunks(lat, full, send_sems, recv_sems, compute)
+        gather_chunks(lat, [full], send_sems, recv_sems, compute)
         for which in range(5):
             lax.fori_loop(0, wide_count, lambda c, carry: (keep(which, c).wait(), carry)[1], 0)
 
@@ -641,8 +755,8 @@
         out_shape=[jax.ShapeDtypeStruct(*o) for o in outs],
         scratch_shapes=[pltpu.VMEM(*o) for o in outs]
         + [
-            pltpu.SemaphoreType.DMA((3, depth)),
-            pltpu.SemaphoreType.DMA((wide_count,)),
+            pltpu.SemaphoreType.DMA((1, 3, depth)),
+            pltpu.SemaphoreType.DMA((1, wide_count)),
             pltpu.SemaphoreType.DMA,
             pltpu.SemaphoreType.DMA((5, wide_count)),
         ],
@@ -654,8 +768,14 @@
     return [r.reshape(wide_count * rows, r.shape[2]) for r in results]
 
 
+def tn(left, right):
+    return lax.dot_general(
+        left, right, (((0,), (0,)), ((), ())), preferred_element_type=jnp.float32
+    )
+
+
 def backward_scattered(
-    cot, gates, ups, gate_weight, up_weight, down_weight, wide_count, collective_id
+    cot, gates, ups, hidden_rows, carried, gate_weight, up_weight, down_weight, wide_count, collective_id
 ):
     model = cot.shape[1]
     rows = cot.shape[0] // wide_count
@@ -665,13 +785,24 @@
     wide_tile = min(512, model)
     low = jnp.bfloat16
 
+    half = model // 2
+    slab = min(256, half)
+    per = half // slab
+
     def kernel(
-        cot_ref, gates_ref, ups_ref, gate_ref, up_ref, down_ref, sum_ref, gate_low_ref, up_low_ref,
+        cot_ref, gates_ref, ups_ref, hidden_ref, carried_ref, gate_ref, up_ref, down_ref,
+        sum_ref, gate_half_ref, up_half_ref, swapped_ref,
         cots, gate_in, up_in, gate_low, up_low, foreign, own, crossed, from_low, from_high,
-        in_sems, out_sems, cross_send, cross_recv, chain_send, low_recv, high_recv,
+        columns, given, taken, kept,
+        in_sems, cross_send, cross_recv, chain_send, low_recv, high_recv,
+        column_sems, give_send, give_recv, kept_sems, carry_sems,
     ):
         lat = Lattice(wide_count)
         z, x, last = lat.z, lat.x, depth - 1
+        narrow = lax.axis_index("narrow")
+        core = narrow % 2
+        partner = narrow + 1 - 2 * core
+        across = (narrow + 2) % 4
 
         def place(e):
             zz = lat.order(depth - 1 - e % depth)[0]
@@ -687,14 +818,6 @@
                 )
             ]
 
-        def stores(e):
-            slot = e % 2
-            chunk = place(e)[1]
-            return [
-                pltpu.make_async_copy(source.at[slot], target.at[chunk], out_sems.at[k, slot])
-                for k, (source, target) in enumerate(((gate_low, gate_low_ref), (up_low, up_low_ref)))
-            ]
-
         def cross(zz):
             return pltpu.make_async_remote_copy(
                 src_ref=foreign.at[zz], dst_ref=crossed.at[zz],
@@ -716,9 +839,79 @@
                 device_id={"wide": lat.at(z - 1, x)}, device_id_type=MESH,
             )
 
+        def slab_of(e):
+            side = jnp.where(e < 2 * per, 1 - core, core)
+            return e // per % 2, e % per, side * per + e % per
+
+        def column_load(e):
+            at = pl.ds(pl.multiple_of(slab_of(e)[2] * slab, slab), slab)
+            return pltpu.make_async_copy(
+                hidden_ref.at[:, :, at], columns.at[e % 2], column_sems.at[e % 2]
+            )
+
+        def give(e):
+            which, n, _ = slab_of(e)
+            return pltpu.make_async_remote_copy(
+                src_ref=given.at[e % 2], dst_ref=taken.at[which, n],
+                send_sem=give_send.at[e % 2], recv_sem=give_recv.at[which, n],
+                device_id={"narrow": partner}, device_id_type=MESH,
+            )
+
+        def keep(e, k):
+            target = (gate_half_ref, up_half_ref)[k]
+            return pltpu.make_async_copy(kept.at[e % 2], target.at[slab_of(e)[1]], kept_sems.at[e % 2])
+
+        def weight_slab(e):
+            which, n, _ = slab_of(e)
+            column_load(e).wait()
+
+            @pl.when(e + 1 < 4 * per)
+            def _():
+                column_load(e + 1).start()
+
+            tokens = columns[e % 2].reshape(wide_count * rows, slab)
+
+            @pl.when((e >= 2) & (e < 2 * per + 2))
+            def _():
+                give(e - 2).wait_send()
+
+            @pl.when(e >= 2 * per + 2)
+            def _():
+                keep(e - 2, 0).wait()
+
+            def product(k):
+                source = (gate_low, up_low)[k]
+                value = tn(tokens, source[...].reshape(wide_count * rows, hidden))
+
+                @pl.when(e < 2 * per)
+                def _():
+                    given[e % 2] = value.astype(low)
+                    give(e).start()
+
+                @pl.when(e >= 2 * per)
+                def _():
+                    give(e).wait_recv()
+                    kept[e % 2] = (value + taken[k, n].astype(jnp.float32)).astype(low)
+                    keep(e, k).start()
+
+            @pl.when(which == 0)
+            def _():
+                product(0)
+
+            @pl.when(which == 1)
+            def _():
+                product(1)
+
         for copy in loads(0):
             copy.start()
-        greet(lat)
+        column_load(0).start()
+        greet(lat, (partner, across))
+        carry = pltpu.make_async_remote_copy(
+            src_ref=carried_ref, dst_ref=swapped_ref,
+            send_sem=carry_sems.at[0], recv_sem=carry_sems.at[1],
+            device_id={"narrow": across}, device_id_type=MESH,
+        )
+        carry.start()
 
         def partial(e, target, zz):
             slot = e % 2
@@ -730,28 +923,22 @@
                 for copy in loads(e + 1):
                     copy.start()
 
-            @pl.when(e >= 2)
-            def _():
-                for copy in stores(e - 2):
-                    copy.wait()
-
             cot_rows = cots[slot]
+            chunk = place(e)[1]
 
             def inner(t, carry):
                 at = pl.ds(pl.multiple_of(t * tile, tile), tile)
                 act_grad = nt(cot_rows, down_ref[at, :])
                 gate, up = gate_in[slot, :, at], up_in[slot, :, at]
                 sigmoid = lax.logistic(gate)
-                gate_low[slot, :, at] = (
+                gate_low[chunk, :, at] = (
                     act_grad * up * sigmoid * (1.0 + gate * (1.0 - sigmoid))
                 ).astype(low)
-                up_low[slot, :, at] = (act_grad * gate * sigmoid).astype(low)
+                up_low[chunk, :, at] = (act_grad * gate * sigmoid).astype(low)
                 return carry
 
             lax.fori_loop(0, hidden // tile, inner, 0)
-            for copy in stores(e):
-                copy.start()
-            gate_rows, up_rows = gate_low[slot], up_low[slot]
+            gate_rows, up_rows = gate_low[chunk], up_low[chunk]
 
             def outer(t, carry):
                 at = pl.ds(pl.multiple_of(t * wide_tile, wide_tile), wide_tile)
@@ -770,9 +957,17 @@
 
         lax.fori_loop(0, depth, send_step, 0)
 
-        def chain_step(e, carry):
+        def own_step(e, carry):
             zz, _ = place(e)
             partial(e, own, zz)
+
+            @pl.when(e == depth)
+            def _():
+                chain(zz)
+
+            return carry
+
+        def chain(zz):
             cross(zz).wait_recv()
             wide = jnp.float32
 
@@ -812,12 +1007,24 @@
                     sink(zz).wait_recv()
                     sum_ref[...] += from_high[zz].astype(wide)
 
+        lax.fori_loop(depth, 2 * depth, own_step, 0)
+
+        def slab_step(e, carry):
+            for k in range(1, depth):
+                @pl.when(e == 4 * per * (k - 1) // (depth - 2))
+                def _():
+                    chain(place(depth + k)[0])
+
+            @pl.when(e < 4 * per)
+            def _():
+                weight_slab(e)
+
             return carry
 
-        lax.fori_loop(depth, 2 * depth, chain_step, 0)
-        for e in (2 * depth - 2, 2 * depth - 1):
-            for copy in stores(e):
-                copy.wait()
+        lax.fori_loop(0, 4 * per + 1, slab_step, 0)
+        for e in (4 * per - 2, 4 * per - 1):
+            keep(e, 1).wait()
+        carry.wait()
 
         def settle(zz, carry):
             cross(zz).wait_send()
@@ -836,108 +1043,144 @@
 
     vmem = pl.BlockSpec(memory_space=pltpu.VMEM)
     hbm = pl.BlockSpec(memory_space=pl.ANY)
-    total, gate_low, up_low = pl.pallas_call(
+    total, gate_half, up_half, swapped = pl.pallas_call(
         kernel,
-        in_specs=[hbm, hbm, hbm, vmem, vmem, vmem],
-        out_specs=[vmem, hbm, hbm],
+        in_specs=[hbm, hbm, hbm, hbm, hbm, vmem, vmem, vmem],
+        out_specs=[vmem, hbm, hbm, hbm],
         out_shape=[
             jax.ShapeDtypeStruct((rows, model), jnp.float32),
-            jax.ShapeDtypeStruct((wide_count, rows, hidden), low),
-            jax.ShapeDtypeStruct((wide_count, rows, hidden), low),
+            jax.ShapeDtypeStruct((per, slab, hidden), low),
+            jax.ShapeDtypeStruct((per, slab, hidden), low),
+            jax.ShapeDtypeStruct(carried.shape, low),
         ],
         scratch_shapes=[
             pltpu.VMEM((2, rows, model), low),
             pltpu.VMEM((2, rows, hidden), jnp.float32),
             pltpu.VMEM((2, rows, hidden), jnp.float32),
-            pltpu.VMEM((2, rows, hidden), low),
-            pltpu.VMEM((2, rows, hidden), low),
+            pltpu.VMEM((wide_count, rows, hidden), low),
+            pltpu.VMEM((wide_count, rows, hidden), low),
         ]
         + [pltpu.VMEM((depth, rows, model), low)] * 5
         + [
+            pltpu.VMEM((2, wide_count, rows, slab), low),
+            pltpu.VMEM((2, slab, hidden), low),
+            pltpu.VMEM((2, per, slab, hidden), low),
+            pltpu.VMEM((2, slab, hidden), low),
             pltpu.SemaphoreType.DMA((3, 2)),
-            pltpu.SemaphoreType.DMA((2, 2)),
         ]
-        + [pltpu.SemaphoreType.DMA((depth,))] * 5,
+        + [pltpu.SemaphoreType.DMA((depth,))] * 5
+        + [
+            pltpu.SemaphoreType.DMA((2,)),
+            pltpu.SemaphoreType.DMA((2,)),
+            pltpu.SemaphoreType.DMA((2, per)),
+            pltpu.SemaphoreType.DMA((2,)),
+            pltpu.SemaphoreType.DMA((2,)),
+        ],
         compiler_params=pltpu.CompilerParams(
-            collective_id=collective_id, has_side_effects=True, vmem_limit_bytes=58 << 20
+            collective_id=collective_id, has_side_effects=True, vmem_limit_bytes=67043328
         ),
         name="backward_scattered",
     )(
         cot.reshape(wide_count, rows, model),
         gates.reshape(wide_count, rows, hidden),
         ups.reshape(wide_count, rows, hidden),
+        hidden_rows.reshape(wide_count, rows, model),
+        carried,
         gate_weight, up_weight, down_weight,
     )
-    flat = wide_count * rows
-    return total, gate_low.reshape(flat, hidden), up_low.reshape(flat, hidden)
+    return total, gate_half.reshape(half, hidden), up_half.reshape(half, hidden), swapped
+
+
+AXES = ("narrow", "wide")
+
+
+def peers(k, counts, act):
+    here = lax.axis_index(AXES[k])
+
+    def one(step, carry):
+        act((here + step) % counts[k])
+        return carry
+
+    lax.fori_loop(1, counts[k], one, 0)
+
+
+def greet_all(counts):
+    barrier = pltpu.get_barrier_semaphore()
+    for k, axis in enumerate(AXES):
+        peers(k, counts, lambda who: pl.semaphore_signal(
+            barrier, inc=1, device_id={axis: who}, device_id_type=MESH))
+    return lambda: pl.semaphore_wait(barrier, counts[0] + counts[1] - 2)
+
+
+class Exchange:
+    def __init__(self, k, counts, source, slots, sends, recvs):
+        self.k, self.counts, self.source = k, counts, source
+        self.slots, self.sends, self.recvs = slots, sends, recvs
+        self.here = lax.axis_index(AXES[k])
+
+    def copy(self, who, slot):
+        return pltpu.make_async_remote_copy(
+            src_ref=self.source, dst_ref=self.slots.at[slot],
+            send_sem=self.sends.at[who], recv_sem=self.recvs.at[slot],
+            device_id={AXES[self.k]: who}, device_id_type=MESH,
+        )
+
+    def start(self):
+        peers(self.k, self.counts, lambda who: self.copy(who, self.here).start())
+        self.slots[self.here] = self.source[...]
+
+    def total(self):
+        peers(self.k, self.counts, lambda who: self.copy(who, who).wait_recv())
+        sums = self.slots[0]
+        for n in range(1, self.counts[self.k]):
+            sums = sums + self.slots[n]
+        return sums
+
+    def settle(self):
+        peers(self.k, self.counts, lambda who: self.copy(who, self.here).wait_send())
+
+
+def exchange_scratch(shape, counts):
+    return [
+        pltpu.VMEM(shape, jnp.float32),
+        pltpu.VMEM((2, max(counts)) + shape, jnp.float32),
+        pltpu.VMEM(shape, jnp.float32),
+        pltpu.SemaphoreType.DMA,
+        pltpu.SemaphoreType.DMA((counts[0],)),
+        pltpu.SemaphoreType.DMA((counts[0],)),
+        pltpu.SemaphoreType.DMA((counts[1],)),
+        pltpu.SemaphoreType.DMA((counts[1],)),
+    ]
+
+
+def exchange_pair(counts, mine, held, total, narrow_send, narrow_recv, wide_send, wide_recv):
+    return (
+        Exchange(0, counts, mine, held.at[0], narrow_send, narrow_recv),
+        Exchange(1, counts, total, held.at[1], wide_send, wide_recv),
+    )
 
 
 def sum_everywhere(values, counts, collective_id):
-    axes = ("narrow", "wide")
-
-    def kernel(in_ref, out_ref, mine, held, total, load_sem, send_sems, recv_sems, wide_send, wide_recv):
-        here = [lax.axis_index(axis) for axis in axes]
-
-        def peers(k, act):
-            def one(step, carry):
-                act((here[k] + step) % counts[k])
-                return carry
-
-            lax.fori_loop(1, counts[k], one, 0)
-
-        barrier = pltpu.get_barrier_semaphore()
-        for k, axis in enumerate(axes):
-            peers(k, lambda who: pl.semaphore_signal(
-                barrier, inc=1, device_id={axis: who}, device_id_type=MESH))
+    def kernel(in_ref, out_ref, mine, held, total, load_sem, *sems):
         load = pltpu.make_async_copy(in_ref, mine, load_sem)
         load.start()
+        arrive = greet_all(counts)
         load.wait()
-        pl.semaphore_wait(barrier, counts[0] + counts[1] - 2)
-
-        def exchange(k, source, slots, sends, recvs, target):
-            def copy(who):
-                return pltpu.make_async_remote_copy(
-                    src_ref=source, dst_ref=slots.at[here[k]],
-                    send_sem=sends.at[who], recv_sem=recvs.at[here[k]],
-                    device_id={axes[k]: who}, device_id_type=MESH,
-                )
-
-            def arrival(who):
-                return pltpu.make_async_remote_copy(
-                    src_ref=source, dst_ref=slots.at[who],
-                    send_sem=sends.at[who], recv_sem=recvs.at[who],
-                    device_id={axes[k]: who}, device_id_type=MESH,
-                )
-
-            peers(k, lambda who: copy(who).start())
-            slots[here[k]] = source[...]
-            peers(k, lambda who: arrival(who).wait_recv())
-            sums = slots[0]
-            for n in range(1, counts[k]):
-                sums = sums + slots[n]
-            target[...] = sums
-            peers(k, lambda who: copy(who).wait_send())
-
-        exchange(0, mine, held.at[0], send_sems, recv_sems, total)
-        exchange(1, total, held.at[1], wide_send, wide_recv, out_ref)
-
-    most = max(counts)
-    shape = values.shape
+        arrive()
+        narrow, wide = exchange_pair(counts, mine, held, total, *sems)
+        narrow.start()
+        total[...] = narrow.total()
+        wide.start()
+        out_ref[...] = wide.total()
+        narrow.settle()
+        wide.settle()
+
     return pl.pallas_call(
         kernel,
         in_specs=[pl.BlockSpec(memory_space=pl.ANY)],
         out_specs=pl.BlockSpec(memory_space=pltpu.VMEM),
-        out_shape=jax.ShapeDtypeStruct(shape, jnp.float32),
-        scratch_shapes=[
-            pltpu.VMEM(shape, jnp.float32),
-            pltpu.VMEM((2, most) + shape, jnp.float32),
-            pltpu.VMEM(shape, jnp.float32),
-            pltpu.SemaphoreType.DMA,
-            pltpu.SemaphoreType.DMA((counts[0],)),
-            pltpu.SemaphoreType.DMA((counts[0],)),
-            pltpu.SemaphoreType.DMA((counts[1],)),
-            pltpu.SemaphoreType.DMA((counts[1],)),
-        ],
+        out_shape=jax.ShapeDtypeStruct(values.shape, jnp.float32),
+        scratch_shapes=exchange_scratch(values.shape, counts),
         compiler_params=pltpu.CompilerParams(collective_id=collective_id, has_side_effects=True),
         name="sum_everywhere",
     )(values)
@@ -973,11 +1216,38 @@
     return lax.dynamic_slice_in_dim(values, index * size, size, axis)
 
 
+def swap_narrow(values, bit):
+    count = lax.axis_size("narrow")
+    return lax.ppermute(values, "narrow", [(i, i ^ bit) for i in range(count)])
+
+
+def keep_half(values, axis, bit):
+    side = lax.axis_index("narrow") // bit % 2
+    mine = lax.dynamic_index_in_dim(values, side, axis, keepdims=False)
+    other = lax.dynamic_index_in_dim(values, 1 - side, axis, keepdims=False)
+    return add_low(mine, swap_narrow(other, bit))
+
+
+def add_low(left, right):
+    return (left.astype(jnp.float32) + right.astype(jnp.float32)).astype(jnp.bfloat16)
+
+
+def core_half(values):
+    rows, columns = values.shape
+    return keep_half(values.astype(jnp.bfloat16).reshape(2, rows // 2, columns), 0, 1)
+
+
 def sum_narrow(values):
-    part = lax.psum_scatter(
-        values.astype(jnp.bfloat16), "narrow", scatter_dimension=0, tiled=True
-    )
-    return lax.all_gather(part, "narrow", axis=0, tiled=True).astype(jnp.float32)
+    half = core_half(values)
+    return hand_back(add_low(half, swap_narrow(half, 2)))
+
+
+def hand_back(half):
+    other = swap_narrow(half, 1)
+    first = lax.axis_index("narrow") % 2 == 0
+    return jnp.concatenate(
+        [jnp.where(first, half, other), jnp.where(first, other, half)], axis=0
+    ).astype(jnp.float32)
 
 
 def swiglu_back(act_grad, gate_values, up_values):
@@ -1017,90 +1287,109 @@
 
     tag_hits = corpus_tags[:, None] == jnp.arange(CORPORA, dtype=jnp.int32)[None, :]
     local_counts = jnp.sum(tag_hits.astype(wide_type), axis=0)
-    corpus_counts = sum_everywhere(
-        jnp.pad(local_counts[None], ((0, 7), (0, 128 - CORPORA))), (narrow_count, wide_count), 1
-    )[0, :CORPORA]
+    local_counts = jnp.pad(local_counts[None], ((0, 7), (0, 128 - CORPORA)))
+    token_values = tokens.astype(wide_type)
+    first_gain = attention_gain.astype(wide_type)
+    second_gain = feedforward_gain.astype(wide_type)
+
+    key_columns = lax.dynamic_slice_in_dim(key_weight, key_head * head_size, head_size, 1)
+    value_columns = lax.dynamic_slice_in_dim(value_weight, key_head * head_size, head_size, 1)
+    own_weights = jnp.concatenate([query_weight, key_columns, value_columns], axis=1)
+    strip = width // narrow_count
+
+    def gather_strips(part):
+        return lax.all_gather(gather_wide(part), "narrow", axis=0, tiled=True)
+
+    def narrow_first(values):
+        values = values.reshape(-1, wide_count, narrow_count, strip)
+        return values.transpose(0, 2, 1, 3).reshape(-1, wide_count * width)
+
+    def wide_first(values):
+        values = values.reshape(-1, narrow_count, wide_count, strip)
+        return values.transpose(0, 2, 1, 3).reshape(-1, wide_count * width)
+
+    strips = [
+        own_part(output_weight, 0, narrow_index, narrow_count),
+        jnp.transpose(own_part(query_weight, 1, narrow_index, narrow_count)),
+    ]
+    hidden_local = norm_scale(token_values, first_gain).astype(low)
+    if chained:
+        hidden_one, raw, corpus_counts, gathered = project_gathered(
+            hidden_local, own_weights, local_counts, strips, (narrow_count, wide_count), 2
+        )
+    else:
+        hidden_one = gather_wide(hidden_local)
+        raw = dot_nn(hidden_one, own_weights)
+        corpus_counts = sum_everywhere(local_counts, (narrow_count, wide_count), 1)
+        gathered = [gather_strips(part) for part in strips]
+    output_full, query_turned = gathered
+    corpus_counts = corpus_counts[0, :CORPORA]
     corpus_scale = jnp.sqrt(jnp.sum(corpus_counts) / (CORPORA * corpus_counts))
     row_weight = jnp.sum(jnp.where(tag_hits, corpus_scale[None, :], 0.0), axis=1)
     out_cot = cotangent.astype(wide_type) * row_weight[:, None]
-    token_values = tokens.astype(wide_type)
-    first_gain = attention_gain.astype(wide_type)
-    second_gain = feedforward_gain.astype(wide_type)
-
-    key_columns = lax.dynamic_slice_in_dim(key_weight, key_head * head_size, head_size, 1)
-    value_columns = lax.dynamic_slice_in_dim(value_weight, key_head * head_size, head_size, 1)
-    own_weights = jnp.concatenate([query_weight, key_columns, value_columns], axis=1)
-    output_full = lax.all_gather(
-        own_part(output_weight, 0, narrow_index, narrow_count), ("wide", "narrow"), axis=0, tiled=True
-    )
-
-    hidden_local = norm_scale(token_values, first_gain).astype(low)
-    if chained:
-        hidden_one, raw = project_gathered(hidden_local, own_weights, wide_count, 2)
-    else:
-        hidden_one = gather_wide(hidden_local)
-        raw = dot_nn(hidden_one, own_weights)
-    cot_local, raw = lax.optimization_barrier((out_cot.astype(low), raw))
-    cot_low = gather_wide(cot_local)
+    cot_low, raw = lax.optimization_barrier((out_cot.astype(low), raw))
+    cot_low = gather_wide(cot_low)
 
     first_block = first_blocks(segments)
     saved = attention_forward(raw, query_gain, key_gain, segments, first_block)
-    mixed = lax.all_to_all(saved[0], "wide", split_axis=0, concat_axis=1, tiled=True)
+    mixed = narrow_first(lax.all_to_all(saved[0], "wide", split_axis=0, concat_axis=1, tiled=True))
     middle = token_values + dot_nn(mixed, output_full)
 
+    together = lax.optimization_barrier
     hidden_two_local = norm_scale(middle, second_gain).astype(low)
     if chained:
         hidden_two, gate_values, up_values, activated, down_part = forward_gathered(
             hidden_two_local, gate_weight, up_weight, down_weight, wide_count, 3
         )
-        hidden_two_grad, gate_low, up_low = backward_scattered(
-            cot_low, gate_values, up_values, gate_weight, up_weight, down_weight, wide_count, 4
+        down_half = core_half(contract_first(activated, cot_low))
+        hidden_two_grad, gate_half, up_half, down_other = backward_scattered(
+            cot_low, gate_values, up_values, hidden_two, down_half, gate_weight, up_weight, down_weight,
+            wide_count, 4,
         )
-        down_part, hidden_two_grad = lax.optimization_barrier((down_part, hidden_two_grad))
+        down_part, hidden_two_grad = together((down_part, hidden_two_grad))
     else:
         hidden_two = gather_wide(hidden_two_local)
         gate_values = dot_nn(hidden_two, gate_weight)
         up_values = dot_nn(hidden_two, up_weight)
         activated = (gate_values * lax.logistic(gate_values) * up_values).astype(low)
         down_part = dot_nn(activated, down_weight)
+        down_half = core_half(contract_first(activated, cot_low))
         gate_low, up_low = swiglu_back(dot_nt(cot_low, down_weight), gate_values, up_values)
         hidden_two_grad = scatter_wide(dot_nt(gate_low, gate_weight) + dot_nt(up_low, up_weight))
-    result = (middle + scatter_wide(down_part)).astype(low)
-    down_grad = sum_narrow(contract_first(activated, cot_low))
-    gate_grad = sum_narrow(contract_first(hidden_two, gate_low))
-    up_grad = sum_narrow(contract_first(hidden_two, up_low))
+        gate_half = core_half(contract_first(hidden_two, gate_low))
+        up_half = core_half(contract_first(hidden_two, up_low))
+        down_other = swap_narrow(down_half, 2)
+    down_half = add_low(down_half, down_other)
+    hidden_two_grad, down_half = together((hidden_two_grad, down_half))
+    down_sum = scatter_wide(down_part)
 
     _, second_pull = jax.vjp(norm_scale, middle, second_gain)
     middle_part, second_gain_grad = second_pull(hidden_two_grad)
     middle_grad = out_cot + middle_part
     middle_low = middle_grad.astype(low)
-    output_grad = lax.all_gather(
-        lax.psum_scatter(
-            contract_first(mixed, middle_low).astype(low),
-            ("wide", "narrow"),
-            scatter_dimension=0,
-            tiled=True,
-        ),
-        "narrow",
-        axis=0,
-        tiled=True,
-    ).astype(wide_type)
-    mixed_grad = lax.all_to_all(
-        dot_nt(middle_low, output_full).astype(low), "wide", split_axis=1, concat_axis=0, tiled=True
-    )
+    mixed_grad = wide_first(dot_nt(middle_low, output_full).astype(low))
+    mixed_grad, mixed, middle_low = together((mixed_grad, mixed, middle_low))
+    mixed_grad = lax.all_to_all(mixed_grad, "wide", split_axis=1, concat_axis=0, tiled=True)
+    output_part = contract_first(mixed, middle_low).astype(low)
+    output_part = output_part.reshape(2, 2, wide_count * strip, model_width)
+    output_part = keep_half(output_part, 1, 1)
+    mixed_grad, output_part = together((mixed_grad, output_part))
+    output_part = keep_half(output_part, 0, 2)
+    gate_half = add_low(gate_half, swap_narrow(gate_half, 2))
     grads, query_gain_grad, key_gain_grad = attention_backward(
         raw, query_gain, key_gain, segments, first_block, saved, mixed_grad
     )
-
-    query_turned = lax.all_gather(
-        jnp.transpose(own_part(query_weight, 1, narrow_index, narrow_count)),
-        ("wide", "narrow"),
-        axis=0,
-        tiled=True,
-    )
+    grads, output_part, gate_half, up_half = together((grads, output_part, gate_half, up_half))
+    up_half = add_low(up_half, swap_narrow(up_half, 2))
     sent = lax.all_to_all(grads, "wide", split_axis=0, concat_axis=1, tiled=True).reshape(
         own_rows, wide_count, width + 2 * head_size
     )
+    sent, down_sum, output_part = together((sent, down_sum, output_part))
+    output_part = output_part.reshape(wide_count, strip, model_width)
+    output_part = lax.all_to_all(output_part, "wide", split_axis=0, concat_axis=0, tiled=True)
+    output_part = jnp.sum(output_part.astype(wide_type), axis=0).astype(low)
+    output_grad = lax.all_gather(output_part, "narrow", axis=0, tiled=True).astype(wide_type)
+    down_grad, gate_grad, up_grad = (hand_back(h) for h in (down_half, gate_half, up_half))
     shared = wide_count // key_total
 
     def key_side(start):
@@ -1112,13 +1401,15 @@
         return part.reshape(own_rows, key_total * head_size)
 
     hidden_one_grad = (
-        dot_nn(sent[:, :, :width].reshape(own_rows, wide_count * width), query_turned)
+        dot_nn(narrow_first(sent[:, :, :width]), query_turned)
         + dot_nt(key_side(width), key_weight)
         + dot_nt(key_side(width + head_size), value_weight)
     )
     _, first_pull = jax.vjp(norm_scale, token_values, first_gain)
     token_part, first_gain_grad = first_pull(hidden_one_grad)
     tokens_gradient = (middle_grad + token_part).astype(low)
+    tokens_gradient, down_sum = lax.optimization_barrier((tokens_gradient, down_sum))
+    result = (middle + down_sum).astype(low)
 
     weight_grads = contract_first(hidden_one, grads)
     if shared == 1:

time: 1220 us -> 880 us (0.72)
  waiting for transfers between devices: 531 us -> 151 us
  other arithmetic: 43.3 us -> 85.3 us
  matrix products: 78.8 us -> 38.3 us
  Pallas kernels: 465 us -> 498 us
  blocking collectives: 29.5 us -> 0 us
  local copies, waits for them, and re-layouts: 42.3 us -> 60.6 us
  starting transfers between devices: 11.3 us -> 24.1 us
    reduce_scatter x5 -> x0, waiting for transfers between devices: 194 us -> none  [the longest x1 127 us: shards(): lax.psum_scatter(contract_first(mixed, middle_low).astype(low), ('wide',...]
    all_gather x7 -> x1, waiting for transfers between devices: 186 us -> 0.01 us  [shards(): lax.all_gather(output_part, 'narrow', axis=0, tiled=True).astype(wide_type)]
    reduce_scatter x1, waiting for transfers between devices: 104 us -> 0.01 us  [scatter_wide(): lax.psum_scatter(values.astype(jnp.bfloat16), 'wide', scatter_dimension=0...]
    all_to_all x0 -> x2, waiting for transfers between devices: none -> 75.9 us  [the longest x1 52.4 us: shards(): lax.all_to_all(mixed_grad, 'wide', split_axis=1, concat_axis=0, tiled=True)]
    pallas_call x2, Pallas kernels: 234 us -> 273 us  [the longest x1 154 us: project_gathered(): pl.pallas_call(kernel, in_specs=[hbm, vmem, hbm] + [hbm] * len(strips), o...]
    convert_element_type x5 -> x17, other arithmetic: 23.9 us -> 58.8 us  [the longest x8 30 us: add_low(): (left.astype(jnp.float32) + right.astype(jnp.float32)).astype(jnp.bfloat16)]
    dot_general x5 -> x3, matrix products: 56.1 us -> 23.1 us  [contract_first(): lax.dot_general(left, right, (((0,), (0,)), ((), ())), preferred_element_...]
    all_to_all x1 -> x0, blocking collectives: 29.5 us -> none  [shards(): lax.all_to_all(dot_nt(middle_low, output_full).astype(low), 'wide', split...]
  transfers between devices with their start and end apart: 16 -> 18, of which waited for: 12 -> 6; matrix products, arithmetic and copies ran while one was open for 12% -> 15% of each run, Pallas kernels for 30% -> 26%
where the time goes in v2:
time: 880 us; the launch traced here: 872 us
  Pallas kernels  498 us (57%)
  waiting for transfers between devices  151 us (17%)
  other arithmetic  85.3 us (10%)
  local copies, waits for them, and re-layouts  60.6 us (7%)
  matrix products  38.3 us (4%)
  starting transfers between devices  24.1 us (3%)
  between operations  15.1 us (2%)
    pallas_call x1, Pallas kernels, project_gathered(): pl.pallas_call(kernel, in_specs=[hbm, vmem, hbm] + [hbm] * len(strips), o...  154 us
    pallas_call x1, Pallas kernels, forward_gathered(): pl.pallas_call(kernel, in_specs=[hbm, vmem, vmem, vmem], out_specs=[hbm]...  138 us
    pallas_call x1, Pallas kernels, backward_scattered(): pl.pallas_call(kernel, in_specs=[hbm, hbm, hbm, hbm, hbm, vmem, vmem, vme...  119 us
    all_to_all x1, waiting for transfers between devices, shards(): lax.all_to_all(mixed_grad, 'wide', split_axis=1, concat_axis=0, tiled=True)  52.4 us
    all_to_all x1, waiting for transfers between devices, shards(): lax.all_to_all(saved[0], 'wide', split_axis=0, concat_axis=1, tiled=True)  49.1 us
    pallas_call x1, Pallas kernels, attention_backward(): pl.pallas_call(kernel, grid_spec=pltpu.PrefetchScalarGridSpec(num_scalar_...  44.9 us
    pallas_call x1, Pallas kernels, attention_forward(): pl.pallas_call(kernel, grid_spec=pltpu.PrefetchScalarGridSpec(num_scalar_...  30.2 us
    convert_element_type x8, other arithmetic, add_low(): (left.astype(jnp.float32) + right.astype(jnp.float32)).astype(jnp.bfloat16)  30 us
  transfers between devices with their start and end apart: 18, of which 6 were waited for; matrix products, arithmetic and copies ran while one was open for 15% of the time, Pallas kernels for 26%

profile of v2, /device:TPU:0, one launch (start us, length us, event | category | flops | bytes accessed | tf_op | source)
XLA Modules:
  0.0 872.1 jit_solution(17526600342856976325)
XLA Ops:
  16.6 154.1 %project_gathered.1 = (bf16[8,256,2048]{2,1,0:T(8,128)(2,1)}, f32[2048,384]{1,0:T(8,128)}, f32[8,128]{1,0:T(8,128)S(1)}, bf16[4,8,64,2048]{3,2,1,0:T(8,128)(2,1)}, bf16[4,8,64,2048]{3,2,1,0:T(8,128)(2,1)}) custom-call(bf16[256,2048]{1,0:T(8,128)(2,1)S(1)} %fusion.5.local_ref, bf16[2048,384]{1,0:T(8,128)(2,1)S(1)} %pad_maximum_fusion.weights_ref, ...), custom_call_target="tpu_custom_call" | custom-call | tf_op jit(solution)/shard_map/project_gathered/pallas_call | solution.py:648
  179.2 30.2 %attention_forward.1 = (bf16[2048,256]{1,0:T(8,128)(2,1)S(1)}, f32[8,2048]{1,0:T(8,128)S(1)}, bf16[2048,256]{1,0:T(8,128)(2,1)S(1)}, bf16[2048,256]{1,0:T(8,128)...) custom-call(s32[1,8]{1,0:T(1,128)S(1)} %and_select_fusion.first_ref, f32[2048,384]{1,0:T(8,128)S(1)} %copy-done, ...), custom_call_target="tpu_custom_call" | custom-call | tf_op jit(solution)/shard_map/attention_forward/pallas_call | solution.py:155
  214.7 2.3 copy.51
  217.1 4.7 all-to-all-start
  221.9 49.1 %all-to-all-done = bf16[8,256,256]{1,2,0:T(8,128)(2,1)S(1)} async-done(((bf16[8,256,256]{1,2,0:T(8,128)(2,1)}), bf16[8,256,256]{1,2,0:T(8,128)(2,1)S(1)}, u32[]{:S(2)}, u32[]{:S(2)}) %all-to-all-start) | async-done | bytes 1048608 | tf_op jit(solution)/shard_map/all_to_all | solution.py:1335
  271.1 6.3 multiply_reduce_fusion.2
  279.9 138.2 %forward_gathered.1 = (bf16[8,256,2048]{2,1,0:T(8,128)(2,1)}, f32[8,256,1024]{2,1,0:T(8,128)}, f32[8,256,1024]{2,1,0:T(8,128)}, bf16[8,256,1024]{2,1,0:T(8,128)(2,1)}, bf16[8,256,2048]{2,1,0:T(8,128)(2,1)}) custom-call(bf16[256,2048]{1,0:T(8,128)(2,1)} %multiply_convert_fusion.local_ref, bf16[2048,1024]{1,0:T(8,128)(2,1)} %gate_ref.3, ...), custom_call_target="tpu_custom_call" | custom-call | tf_op jit(solution)/shard_map/forward_gathered/pallas_call | solution.py:751
  418.1 12.7 %convolution_convert_fusion.1 = bf16[1024,2048]{1,0:T(8,128)(2,1)S(1)} fusion(bf16[2048,1024]{1,0:T(8,128)(2,1)} %bitcast.145, bf16[2048,2048]{1,0:T(8,128)(2,1)} %all-gather.3.cloned.1.call-done), kind=kOutput, calls=%fused_computation.19 | convolution fusion | flops 8592031744 | bytes 16777216 | tf_op jit(solution)/shard_map/dot_general | solution.py:1199
  433.5 4.4 collective-permute-done
  437.9 3.7 fusion.2.carried_ref
  441.5 118.8 %backward_scattered.1 = (f32[256,2048]{1,0:T(8,128)}, bf16[4,256,1024]{2,1,0:T(8,128)(2,1)}, bf16[4,256,1024]{2,1,0:T(8,128)(2,1)}, bf16[512,2048]{1,0:T(8,128)(2,1)}) custom-call(bf16[8,256,2048]{2,1,0:T(8,128)(2,1)} %bitcast.125, f32[8,256,1024]{2,1,0:T(8,128)} %get-tuple-element.63.gates_ref, f32[8,256,1024]{2,1,0:T(8,128)} %get-tuple-element.64.ups_ref, ...), custom_call_target="tpu_custom_call" | custom-call | tf_op jit(solution)/shard_map/backward_scattered/pallas_call | solution.py:1046
  563.1 3.8 add_convert_fusion.2
  570.6 3.3 convolution_convert_fusion.3
  573.9 2.3 copy.53
  576.2 2.4 copy.54
  578.6 2.4 convolution_convert_fusion
  581.0 2.5 dynamic-slice_bitcast_fusion
  585.7 4.4 all-to-all-start.1
  590.0 52.4 %all-to-all-done.1 = bf16[256,8,256]{0,2,1:T(8,128)(2,1)S(1)} async-done(((bf16[256,8,256]{0,2,1:T(8,128)(2,1)}), bf16[256,8,256]{0,2,1:T(8,128)(2,1)S(1)}, u32[]{:S(2)}, u32[]{:S(2)}) %all-to-all-start.1) | async-done | bytes 1048608 | tf_op jit(solution)/shard_map/all_to_all | solution.py:1372
  643.7 5.5 fusion
  652.1 4.7 add_convert_fusion.1
  656.9 44.9 %attention_backward.1 = (bf16[2048,384]{1,0:T(8,128)(2,1)}, f32[1,256]{1,0:T(1,128)S(1)}, f32[1,256]{1,0:T(1,128)S(1)}) custom-call(s32[1,8]{1,0:T(1,128)S(1)} %copy-done.24, f32[2048,384]{1,0:T(8,128)} %get-tuple-element.58.raw_ref, f32[1,256]{1,0:T(1,128)S(1)} %copy-done.20, f32[1,256]{1,0:T(1,128)S(1)} %copy-done.22, f32[2048,64]{1,0:T(8,128)S(1)} %copy-done.8, ...), custom_call_target="tpu_custom_call" | custom-call | tf_op jit(solution)/shard_map/attention_backward/pallas_call | solution.py:312
  701.9 3.8 fusion.1
  707.7 8.0 convolution_convert_fusion.2
  716.8 2.3 copy.60
  719.7 4.5 broadcast_select_fusion.1
  725.4 2.7 copy.57
  728.1 4.4 all-to-all-start.2
  732.5 2.5 fusion.13
  736.3 5.9 maximum_convert_fusion.2
  742.2 11.8 %collective-permute-done.8 = bf16[1024,1024]{1,0:T(8,128)(2,1)} collective-permute-done((bf16[1024,1024]{1,0:T(8,128)(2,1)}, bf16[1024,1024]{1,0:T(8,128)(2,1)}, u32[]{:S(2)}, u32[]{:S(2)}) %collective-permute-start.8) | collective-permute-done | bytes 2097184 | tf_op jit(solution)/shard_map/ppermute | solution.py:1221
  754.1 4.5 add_convert_fusion
  761.6 9.2 %collective-permute-done.5 = bf16[1024,384]{0,1:T(8,128)(2,1)S(1)} collective-permute-done((bf16[1024,384]{0,1:T(8,128)(2,1)}, bf16[1024,384]{0,1:T(8,128)(2,1)S(1)}, u32[]{:S(2)}, u32[]{:S(2)}) %collective-permute-start.5) | collective-permute-done | bytes 786464 | tf_op jit(solution)/shard_map/ppermute | solution.py:1221
  772.6 2.1 broadcast_select_fusion.5
  774.8 4.5 maximum_convert_fusion
  780.2 2.8 convert_element_type.199
  783.0 4.3 all-to-all-start.3
  790.4 3.1 copy.61
  795.6 2.5 broadcast_select_fusion.3
  798.1 5.4 maximum_convert_fusion.1
  806.0 2.4 convolution_bitcast_fusion
  810.3 2.5 fusion.6
  812.8 23.5 %all-to-all-done.3 = bf16[8,64,2048]{2,1,0:T(8,128)(2,1)} async-done(((bf16[8,64,2048]{2,1,0:T(8,128)(2,1)}), bf16[8,64,2048]{2,1,0:T(8,128)(2,1)}, u32[]{:S(2)}, u32[]{:S(2)}) %all-to-all-start.3) | async-done | bytes 2097184 | tf_op jit(solution)/shard_map/all_to_all | solution.py:1389
  836.3 2.7 reduce_sum.149
  839.0 3.8 fusion.9
  843.5 12.0 %sum_everywhere.1 = f32[40,128]{1,0:T(8,128)} custom-call(f32[40,128]{1,0:T(8,128)} %pad_bitcast_fusion.in_ref), custom_call_target="tpu_custom_call" | custom-call | tf_op jit(solution)/shard_map/sum_everywhere/pallas_call | solution.py:1178
  859.5 2.8 add_convert_fusion.3
  862.3 2.8 convert_element_type.211
  (227 shorter events, 67.0 us)
Async XLA Ops:
  7.2 410.9 %all-gather.3.cloned.1.call-start = ((), (), s32[]{:S(2)}) async-start(), calls=%async_computation.5 | async-start | bytes 9437184 | tf_op jit(solution)/shard_map/all_gather | solution.py:1205
  10.2 5.2 copy-start.53
  16.5 155.4 %copy-start.64 = (s32[256]{0:T(256)S(1)}, s32[256]{0:T(256)}, u32[]{:S(2)}) copy-start(s32[256]{0:T(256)} %param.32) | copy-start | bytes 3076
  16.5 156.0 %copy-start.40 = (bf16[256,2048]{1,0:T(8,128)(2,1)S(1)}, bf16[256,2048]{1,0:T(8,128)(2,1)}, u32[]{:S(2)}) copy-start(bf16[256,2048]{1,0:T(8,128)(2,1)} %param.31) | copy-start | bytes 3145732
  175.3 34.1 %copy-start.19 = (f32[1,256]{1,0:T(1,128)}, f32[1,256]{1,0:T(1,128)S(1)}, u32[]{:S(2)}) copy-start(f32[1,256]{1,0:T(1,128)S(1)} %get-tuple-element.167.qg_ref) | copy-start | bytes 3076
  175.3 34.1 %copy-start.21 = (f32[1,256]{1,0:T(1,128)}, f32[1,256]{1,0:T(1,128)S(1)}, u32[]{:S(2)}) copy-start(f32[1,256]{1,0:T(1,128)S(1)} %get-tuple-element.168.kg_ref) | copy-start | bytes 3076
  175.5 33.9 %copy-start.23 = (s32[1,8]{1,0:T(1,128)}, s32[1,8]{1,0:T(1,128)S(1)}, u32[]{:S(2)}) copy-start(s32[1,8]{1,0:T(1,128)S(1)} %and_select_fusion.first_ref) | copy-start | bytes 100
  214.7 7.2 copy-start.63
  214.7 56.3 %copy-start.29 = (bf16[256,2048]{1,0:T(8,128)(2,1)S(1)}, bf16[256,2048]{1,0:T(8,128)(2,1)}, u32[]{:S(2)}) copy-start(bf16[256,2048]{1,0:T(8,128)(2,1)} %param.19) | copy-start | bytes 3145732
  217.1 54.0 %all-to-all-start = ((bf16[8,256,256]{1,2,0:T(8,128)(2,1)}), bf16[8,256,256]{1,2,0:T(8,128)(2,1)S(1)}, u32[]{:S(2)}, u32[]{:S(2)}) async-start(bf16[8,256,256]{1,2,0:T(8,128)(2,1)} %copy.51), calls=%async_computation | async-start | bytes 2097152 | tf_op jit(solution)/shard_map/all_to_all | solution.py:1335
  221.8 558.4 %reduce-scatter.2.cloned.1.call-start = ((), (), s32[]{:S(2)}) async-start(), calls=%async_computation.6 | async-start | bytes 9437184 | tf_op jit(solution)/shard_map/reduce_scatter | solution.py:1209
  221.9 56.0 %copy-start.51 = (f32[2048]{0:T(1024)}, f32[2048]{0:T(1024)S(1)}, u32[]{:S(2)}) copy-start(f32[2048]{0:T(1024)S(1)} %convert_element_type.175) | copy-start | bytes 24580
  271.1 6.3 copy-start.34
  433.5 4.4 collective-permute-start
  561.5 5.5 copy-start.37
  561.5 5.5 copy-start.52
  561.5 5.5 copy-start.56
  563.1 7.5 slice-start
  585.7 58.1 %collective-permute-start.1 = (bf16[2,512,2048]{2,1,0:T(8,128)(2,1)}, bf16[2,512,2048]{2,1,0:T(8,128)(2,1)}, u32[]{:S(2)}, u32[]{:S(2)}) collective-permute-start(bf16[2,512,2048]{2,1,0:T(8,128)(2,1)} %dynamic-slice_bitcast_fusion), channel_id=1, source_target_pairs={{0,8},{8,0},{16,24},{24,16},{1,9},{9,1},{17,25},{25,17},{2,10},{10... | collective-permute-start | bytes 12582920 | tf_op jit(solution)/shard_map/ppermute | solution.py:1221
  585.7 56.8 %all-to-all-start.1 = ((bf16[256,8,256]{0,2,1:T(8,128)(2,1)}), bf16[256,8,256]{0,2,1:T(8,128)(2,1)S(1)}, u32[]{:S(2)}, u32[]{:S(2)}) async-start(bf16[256,8,256]{0,2,1:T(8,128)(2,1)} %bitcast.27), calls=%async_computation.1 | async-start | bytes 2097152 | tf_op jit(solution)/shard_map/all_to_all | solution.py:1372
  590.0 62.1 %collective-permute-start.3 = (bf16[1024,1024]{1,0:T(8,128)(2,1)}, bf16[1024,1024]{1,0:T(8,128)(2,1)}, u32[]{:S(2)}, u32[]{:S(2)}) collective-permute-start(bf16[1024,1024]{1,0:T(8,128)(2,1)} %bitcast.133), channel_id=1, source_target_pairs={{0,16},{8,24},{16,0},{24,8},{1,17},{9,25},{17,1},{25,9},{2,18},{10... | collective-permute-start | bytes 6291464 | tf_op jit(solution)/shard_map/ppermute | solution.py:1221
  651.9 50.0 %collective-permute-start.2 = (bf16[512,2048]{1,0:T(8,128)(2,1)}, bf16[512,2048]{1,0:T(8,128)(2,1)}, u32[]{:S(2)}, u32[]{:S(2)}) collective-permute-start(bf16[512,2048]{1,0:T(8,128)(2,1)} %dynamic-slice_bitcast_fusion.1), channel_id=1, source_target_pairs={{0,16},{8,24},{16,0},{24,8},{1,17},{9,25},{17,1},{25,9},{2,18},{10... | collective-permute-start | bytes 6291464 | tf_op jit(solution)/shard_map/ppermute | solution.py:1221
  651.9 4.9 copy-start.2
  651.9 4.9 copy-start.4
  651.9 4.9 copy-start.6
  651.9 4.9 copy-start.8
  651.9 4.9 copy-start.10
  651.9 4.9 copy-start.14
  652.0 4.9 copy-start.16
  652.0 4.9 copy-start.18
  652.0 4.9 copy-start.20
  652.0 4.9 copy-start.22
  652.0 4.9 copy-start.24
  652.0 67.7 %collective-permute-start.10 = (bf16[512,2048]{1,0:T(8,128)(2,1)}, bf16[512,2048]{1,0:T(8,128)(2,1)}, u32[]{:S(2)}, u32[]{:S(2)}) collective-permute-start(bf16[512,2048]{1,0:T(8,128)(2,1)} %add_convert_fusion.2), channel_id=1, source_target_pairs={{0,8},{8,0},{16,24},{24,16},{1,9},{9,1},{17,25},{25,17},{2,10},{10... | collective-permute-start | bytes 6291464 | tf_op jit(solution)/shard_map/ppermute | solution.py:1221
  656.9 45.0 %copy-start.33 = (bf16[2,512,2048]{2,1,0:T(8,128)(2,1)S(1)}, bf16[2,512,2048]{2,1,0:T(8,128)(2,1)}, u32[]{:S(2)}) copy-start(bf16[2,512,2048]{2,1,0:T(8,128)(2,1)} %copy-done.32) | copy-start | bytes 12582916
  701.8 5.9 copy-start.48
  705.7 48.4 %collective-permute-start.8 = (bf16[1024,1024]{1,0:T(8,128)(2,1)}, bf16[1024,1024]{1,0:T(8,128)(2,1)}, u32[]{:S(2)}, u32[]{:S(2)}) collective-permute-start(bf16[1024,1024]{1,0:T(8,128)(2,1)} %bitcast.36), channel_id=1, source_target_pairs={{0,16},{8,24},{16,0},{24,8},{1,17},{9,25},{17,1},{25,9},{2,18},{10... | collective-permute-start | bytes 6291464 | tf_op jit(solution)/shard_map/ppermute | solution.py:1221
  719.1 13.4 %collective-permute-start.4 = (bf16[1024,384]{0,1:T(8,128)(2,1)}, bf16[1024,384]{0,1:T(8,128)(2,1)}, u32[]{:S(2)}, u32[]{:S(2)}) collective-permute-start(bf16[1024,384]{0,1:T(8,128)(2,1)} %bitcast.138), channel_id=1, source_target_pairs={{0,8},{8,0},{16,24},{24,16},{1,9},{9,1},{17,25},{25,17},{2,10},{10... | collective-permute-start | bytes 2359304 | tf_op jit(solution)/shard_map/ppermute | solution.py:1221
  719.7 52.9 %collective-permute-start.7 = (bf16[1024,1024]{1,0:T(8,128)(2,1)}, bf16[1024,1024]{1,0:T(8,128)(2,1)}, u32[]{:S(2)}, u32[]{:S(2)}) collective-permute-start(bf16[1024,1024]{1,0:T(8,128)(2,1)} %add_convert_fusion.1), channel_id=1, source_target_pairs={{0,8},{8,0},{16,24},{24,16},{1,9},{9,1},{17,25},{25,17},{2,10},{10... | collective-permute-start | bytes 6291464 | tf_op jit(solution)/shard_map/ppermute | solution.py:1221
  728.1 55.0 %all-to-all-start.2 = ((bf16[8,256,384]{1,2,0:T(8,128)(2,1)}), bf16[8,256,384]{1,2,0:T(8,128)(2,1)}, u32[]{:S(2)}, u32[]{:S(2)}) async-start(bf16[8,256,384]{1,2,0:T(8,128)(2,1)} %copy.57), calls=%async_computation.2 | async-start | bytes 3145728 | tf_op jit(solution)/shard_map/all_to_all | solution.py:1384
  735.0 35.8 %collective-permute-start.5 = (bf16[1024,384]{0,1:T(8,128)(2,1)}, bf16[1024,384]{0,1:T(8,128)(2,1)S(1)}, u32[]{:S(2)}, u32[]{:S(2)}) collective-permute-start(bf16[1024,384]{0,1:T(8,128)(2,1)} %fusion.13), channel_id=1, source_target_pairs={{0,16},{8,24},{16,0},{24,8},{1,17},{9,25},{17,1},{25,9},{2,18},{10... | collective-permute-start | bytes 2359304 | tf_op jit(solution)/shard_map/ppermute | solution.py:1221
  758.6 37.0 %collective-permute-start.9 = (bf16[1024,1024]{1,0:T(8,128)(2,1)}, bf16[1024,1024]{1,0:T(8,128)(2,1)}, u32[]{:S(2)}, u32[]{:S(2)}) collective-permute-start(bf16[1024,1024]{1,0:T(8,128)(2,1)} %add_convert_fusion), channel_id=1, source_target_pairs={{0,8},{8,0},{16,24},{24,16},{1,9},{9,1},{17,25},{25,17},{2,10},{10... | collective-permute-start | bytes 6291464 | tf_op jit(solution)/shard_map/ppermute | solution.py:1221
  761.6 11.0 %copy-start.36 = (bf16[1024,1024]{1,0:T(8,128)(2,1)S(1)}, bf16[1024,1024]{1,0:T(8,128)(2,1)}, u32[]{:S(2)}) copy-start(bf16[1024,1024]{1,0:T(8,128)(2,1)} %add_convert_fusion.1) | copy-start | bytes 6291460
  772.3 7.0 collective-permute-start.6
  783.0 53.2 %all-to-all-start.3 = ((bf16[8,64,2048]{2,1,0:T(8,128)(2,1)}), bf16[8,64,2048]{2,1,0:T(8,128)(2,1)}, u32[]{:S(2)}, u32[]{:S(2)}) async-start(bf16[8,64,2048]{2,1,0:T(8,128)(2,1)} %bitcast.118), calls=%async_computation.4 | async-start | bytes 4194304 | tf_op jit(solution)/shard_map/all_to_all | solution.py:1389
  787.4 74.9 %all-gather.5.cloned.1.call-start = ((), (), s32[]{:S(2)}) async-start(), calls=%async_computation.7 | async-start | bytes 1310720 | tf_op jit(solution)/shard_map/all_gather | solution.py:1391
  798.1 7.9 slice-start.2
  798.1 7.9 slice-start.3
  (41 other events, 90.4 us)
Sparse Core Ops, SparseCore 0:
  173.9 159.1 all-gather.2
  560.5 170.8 reduce-scatter.1
  839.2 17.5 all-gather.4

commit v3 on v2

--- a/solution.py
+++ b/solution.py
@@ -586,7 +586,7 @@
 
         def keep_strip(n, chunk, k):
             return pltpu.make_async_copy(
-                spread.at[n, chunk, pl.ds(k * strip, strip)], spread_refs[k].at[n, chunk],
+                spread.at[n, chunk, pl.ds(k * strip, strip)], spread_refs[k].at[chunk, n],
                 spread_sems.at[k, n, chunk],
             )
 
@@ -654,7 +654,7 @@
             jax.ShapeDtypeStruct((wide_count * rows, columns), jnp.float32),
             jax.ShapeDtypeStruct(values.shape, jnp.float32),
         ]
-        + [jax.ShapeDtypeStruct((narrow_count, wide_count, strip, model), low)] * len(strips),
+        + [jax.ShapeDtypeStruct((wide_count, narrow_count, strip, model), low)] * len(strips),
         scratch_shapes=[
             pltpu.VMEM((wide_count, rows, model), low),
             pltpu.VMEM((narrow_count, wide_count, tall, model), low),
@@ -775,7 +775,7 @@
 
 
 def backward_scattered(
-    cot, gates, ups, hidden_rows, carried, gate_weight, up_weight, down_weight, wide_count, collective_id
+    cot, gates, ups, hidden_rows, gate_weight, up_weight, down_weight, wide_count, collective_id
 ):
     model = cot.shape[1]
     rows = cot.shape[0] // wide_count
@@ -790,19 +790,18 @@
     per = half // slab
 
     def kernel(
-        cot_ref, gates_ref, ups_ref, hidden_ref, carried_ref, gate_ref, up_ref, down_ref,
-        sum_ref, gate_half_ref, up_half_ref, swapped_ref,
+        cot_ref, gates_ref, ups_ref, hidden_ref, gate_ref, up_ref, down_ref,
+        sum_ref, gate_half_ref, up_half_ref,
         cots, gate_in, up_in, gate_low, up_low, foreign, own, crossed, from_low, from_high,
         columns, given, taken, kept,
         in_sems, cross_send, cross_recv, chain_send, low_recv, high_recv,
-        column_sems, give_send, give_recv, kept_sems, carry_sems,
+        column_sems, give_send, give_recv, kept_sems,
     ):
         lat = Lattice(wide_count)
         z, x, last = lat.z, lat.x, depth - 1
         narrow = lax.axis_index("narrow")
         core = narrow % 2
         partner = narrow + 1 - 2 * core
-        across = (narrow + 2) % 4
 
         def place(e):
             zz = lat.order(depth - 1 - e % depth)[0]
@@ -905,13 +904,7 @@
         for copy in loads(0):
             copy.start()
         column_load(0).start()
-        greet(lat, (partner, across))
-        carry = pltpu.make_async_remote_copy(
-            src_ref=carried_ref, dst_ref=swapped_ref,
-            send_sem=carry_sems.at[0], recv_sem=carry_sems.at[1],
-            device_id={"narrow": across}, device_id_type=MESH,
-        )
-        carry.start()
+        greet(lat, (partner,))
 
         def partial(e, target, zz):
             slot = e % 2
@@ -1024,7 +1017,6 @@
         lax.fori_loop(0, 4 * per + 1, slab_step, 0)
         for e in (4 * per - 2, 4 * per - 1):
             keep(e, 1).wait()
-        carry.wait()
 
         def settle(zz, carry):
             cross(zz).wait_send()
@@ -1043,15 +1035,14 @@
 
     vmem = pl.BlockSpec(memory_space=pltpu.VMEM)
     hbm = pl.BlockSpec(memory_space=pl.ANY)
-    total, gate_half, up_half, swapped = pl.pallas_call(
+    total, gate_half, up_half = pl.pallas_call(
         kernel,
-        in_specs=[hbm, hbm, hbm, hbm, hbm, vmem, vmem, vmem],
-        out_specs=[vmem, hbm, hbm, hbm],
+        in_specs=[hbm, hbm, hbm, hbm, vmem, vmem, vmem],
+        out_specs=[vmem] + [hbm] * 2,
         out_shape=[
             jax.ShapeDtypeStruct((rows, model), jnp.float32),
             jax.ShapeDtypeStruct((per, slab, hidden), low),
             jax.ShapeDtypeStruct((per, slab, hidden), low),
-            jax.ShapeDtypeStruct(carried.shape, low),
         ],
         scratch_shapes=[
             pltpu.VMEM((2, rows, model), low),
@@ -1074,7 +1065,6 @@
             pltpu.SemaphoreType.DMA((2,)),
             pltpu.SemaphoreType.DMA((2, per)),
             pltpu.SemaphoreType.DMA((2,)),
-            pltpu.SemaphoreType.DMA((2,)),
         ],
         compiler_params=pltpu.CompilerParams(
             collective_id=collective_id, has_side_effects=True, vmem_limit_bytes=67043328
@@ -1085,10 +1075,9 @@
         gates.reshape(wide_count, rows, hidden),
         ups.reshape(wide_count, rows, hidden),
         hidden_rows.reshape(wide_count, rows, model),
-        carried,
         gate_weight, up_weight, down_weight,
     )
-    return total, gate_half.reshape(half, hidden), up_half.reshape(half, hidden), swapped
+    return total, gate_half.reshape(half, hidden), up_half.reshape(half, hidden)
 
 
 AXES = ("narrow", "wide")
@@ -1184,6 +1173,349 @@
         compiler_params=pltpu.CompilerParams(collective_id=collective_id, has_side_effects=True),
         name="sum_everywhere",
     )(values)
+
+
+def greet_wide(counts, partners=()):
+    barrier = pltpu.get_barrier_semaphore()
+    peers(1, counts, lambda who: pl.semaphore_signal(
+        barrier, inc=1, device_id={"wide": who}, device_id_type=MESH))
+    for partner in partners:
+        pl.semaphore_signal(
+            barrier, inc=1, device_id={"narrow": partner}, device_id_type=MESH
+        )
+    pl.semaphore_wait(barrier, counts[1] - 1 + len(partners))
+
+
+class Blocks:
+    def __init__(self, counts, blocks, held, sends, recvs):
+        self.counts, self.blocks, self.held = counts, blocks, held
+        self.sends, self.recvs = sends, recvs
+        self.me = lax.axis_index("wide")
+
+    def copy(self, who, slot):
+        return pltpu.make_async_remote_copy(
+            src_ref=self.blocks.at[who], dst_ref=self.held.at[slot],
+            send_sem=self.sends.at[who], recv_sem=self.recvs.at[slot],
+            device_id={"wide": who}, device_id_type=MESH,
+        )
+
+    def start(self, who):
+        self.copy(who, self.me).start()
+
+    def each(self, act):
+        peers(1, self.counts, act)
+
+    def arrived(self, who):
+        self.copy(who, who).wait_recv()
+
+    def settle(self):
+        self.each(lambda who: self.copy(who, self.me).wait_send())
+
+
+def carry_over(source, target, sems):
+    across = (lax.axis_index("narrow") + 2) % 4
+    return pltpu.make_async_remote_copy(
+        src_ref=source, dst_ref=target, send_sem=sems.at[0], recv_sem=sems.at[1],
+        device_id={"narrow": across}, device_id_type=MESH,
+    )
+
+
+VMEM_SPEC = pl.BlockSpec(memory_space=pltpu.VMEM)
+HBM_SPEC = pl.BlockSpec(memory_space=pl.ANY)
+
+
+def mix_and_project(mixed, output_full, counts, collective_id):
+    wide_count = counts[1]
+    rows, width = mixed.shape[0] // wide_count, mixed.shape[1]
+    model = output_full.shape[1]
+    tile = min(512, model)
+
+    def kernel(mixed_ref, weight_ref, out_ref, held_ref, sends, recvs):
+        blocks = Blocks(counts, mixed_ref, held_ref, sends, recvs)
+        greet_wide(counts)
+        blocks.each(blocks.start)
+        held_ref[blocks.me] = mixed_ref[blocks.me]
+
+        def add(who, first):
+            rows_in = held_ref[who]
+
+            def one(t, carry):
+                at = pl.ds(pl.multiple_of(t * tile, tile), tile)
+                part = jnp.dot(
+                    rows_in, weight_ref[pl.ds(pl.multiple_of(who * width, width), width), at],
+                    preferred_element_type=jnp.float32,
+                )
+                out_ref[:, at] = part if first else out_ref[:, at] + part
+                return carry
+
+            lax.fori_loop(0, model // tile, one, 0)
+
+        add(blocks.me, True)
+
+        def later(who):
+            blocks.arrived(who)
+            add(who, False)
+
+        blocks.each(later)
+        blocks.settle()
+
+    return pl.pallas_call(
+        kernel,
+        in_specs=[VMEM_SPEC, VMEM_SPEC],
+        out_specs=[VMEM_SPEC, VMEM_SPEC],
+        out_shape=[
+            jax.ShapeDtypeStruct((rows, model), jnp.float32),
+            jax.ShapeDtypeStruct((wide_count, rows, width), mixed.dtype),
+        ],
+        scratch_shapes=[pltpu.SemaphoreType.DMA((wide_count,))] * 2,
+        compiler_params=pltpu.CompilerParams(
+            collective_id=collective_id, has_side_effects=True, vmem_limit_bytes=32 << 20
+        ),
+        name="mix_and_project",
+    )(mixed.reshape(wide_count, rows, width), output_full)
+
+
+def unmix(middle_low, output_full, mixed_blocks, carried, counts, collective_id):
+    wide_count = counts[1]
+    rows, model = middle_low.shape
+    width = mixed_blocks.shape[2]
+    strip = width // 4
+    low = jnp.bfloat16
+
+    def kernel(
+        middle_ref, weight_ref, mixed_ref, carried_ref, held_ref, half_ref, swapped_ref,
+        made, product, own, given, taken, sends, recvs, give_send, give_recv, carry_sems,
+    ):
+        blocks = Blocks(counts, made, held_ref, sends, recvs)
+        narrow = lax.axis_index("narrow")
+        core = narrow % 2
+        partner = narrow + 1 - 2 * core
+        greet_wide(counts, (partner, (narrow + 2) % 4))
+        carry = carry_over(carried_ref, swapped_ref, carry_sems)
+        carry.start()
+
+        def make(who):
+            made[who] = nt(
+                middle_ref[...], weight_ref[pl.ds(pl.multiple_of(who * width, width), width), :]
+            ).astype(low)
+
+        def make_and_start(who):
+            make(who)
+            blocks.start(who)
+
+        blocks.each(make_and_start)
+        make(blocks.me)
+        held_ref[blocks.me] = made[blocks.me]
+
+        def give(w):
+            return pltpu.make_async_remote_copy(
+                src_ref=given.at[w], dst_ref=taken.at[w],
+                send_sem=give_send.at[w], recv_sem=give_recv.at[w],
+                device_id={"narrow": partner}, device_id_type=MESH,
+            )
+
+        def multiply(w, state):
+            product[...] = tn(mixed_ref[w], middle_ref[...])
+            for y in range(2):
+                at = pl.multiple_of((2 * y + 1 - core) * strip, strip)
+                given[w, y] = product[pl.ds(at, strip), :].astype(low)
+                at = pl.multiple_of((2 * y + core) * strip, strip)
+                own[w, y] = product[pl.ds(at, strip), :]
+            give(w).start()
+            return state
+
+        def collect(w, state):
+            give(w).wait_recv()
+            for y in range(2):
+                half_ref[y, w] = (own[w, y] + taken[w, y].astype(jnp.float32)).astype(low)
+            return state
+
+        lax.fori_loop(0, wide_count, multiply, 0)
+        lax.fori_loop(0, wide_count, collect, 0)
+        blocks.each(blocks.arrived)
+        blocks.settle()
+        lax.fori_loop(0, wide_count, lambda w, state: (give(w).wait_send(), state)[1], 0)
+        carry.wait()
+
+    held, half, swapped = pl.pallas_call(
+        kernel,
+        in_specs=[VMEM_SPEC] * 3 + [HBM_SPEC],
+        out_specs=[VMEM_SPEC] * 2 + [HBM_SPEC],
+        out_shape=[
+            jax.ShapeDtypeStruct((wide_count, rows, width), low),
+            jax.ShapeDtypeStruct((2, wide_count, strip, model), low),
+            jax.ShapeDtypeStruct(carried.shape, low),
+        ],
+        scratch_shapes=[
+            pltpu.VMEM((wide_count, rows, width), low),
+            pltpu.VMEM((width, model), jnp.float32),
+            pltpu.VMEM((wide_count, 2, strip, model), jnp.float32),
+            pltpu.VMEM((wide_count, 2, strip, model), low),
+            pltpu.VMEM((wide_count, 2, strip, model), low),
+        ]
+        + [pltpu.SemaphoreType.DMA((wide_count,))] * 4
+        + [pltpu.SemaphoreType.DMA((2,))],
+        compiler_params=pltpu.CompilerParams(
+            collective_id=collective_id, has_side_effects=True, vmem_limit_bytes=48 << 20
+        ),
+        name="unmix",
+    )(middle_low, output_full, mixed_blocks, carried)
+    return (
+        held.reshape(wide_count * rows, width),
+        half.reshape(2, wide_count * strip, model),
+        swapped,
+    )
+
+
+def return_and_project(
+    grads, hidden_rows, query_turned, key_weight, value_weight, carried, counts, collective_id
+):
+    wide_count = counts[1]
+    rows, columns = grads.shape[0] // wide_count, grads.shape[1]
+    model = query_turned.shape[1]
+    width = query_turned.shape[0] // wide_count
+    head = (columns - width) // 2
+    tile = min(512, model)
+    slab = min(256, model // 2)
+    per = model // 2 // slab
+    low = jnp.bfloat16
+
+    def kernel(
+        grads_ref, hidden_ref, query_ref, key_ref, value_ref, carried_ref,
+        out_ref, weight_ref, swapped_ref,
+        held, slabs, query_all, key_all, value_all, given, taken, halves, whole,
+        sends, recvs, slab_sems, give_send, give_recv, half_sems, carry_sems,
+    ):
+        blocks = Blocks(counts, grads_ref, held, sends, recvs)
+        narrow = lax.axis_index("narrow")
+        core = narrow % 2
+        partner, across = narrow + 1 - 2 * core, (narrow + 2) % 4
+
+        def row_of(t):
+            return pl.multiple_of((jnp.where(t < per, 1 - core, core) * per + t % per) * slab, slab)
+
+        def load(t):
+            at = pl.ds(row_of(t), slab)
+            return pltpu.make_async_copy(hidden_ref.at[:, :, at], slabs.at[t % 2], slab_sems.at[t % 2])
+
+        load(0).start()
+        greet_wide(counts, (partner, across))
+        blocks.each(blocks.start)
+        carry = carry_over(carried_ref, swapped_ref, carry_sems)
+        held[blocks.me] = grads_ref[blocks.me]
+
+        def give(n):
+            return pltpu.make_async_remote_copy(
+                src_ref=given.at[n], dst_ref=taken.at[n],
+                send_sem=give_send.at[n], recv_sem=give_recv.at[n],
+                device_id={"narrow": partner}, device_id_type=MESH,
+            )
+
+        exchange = pltpu.make_async_remote_copy(
+            src_ref=halves.at[0], dst_ref=halves.at[1],
+            send_sem=half_sems.at[0], recv_sem=half_sems.at[1],
+            device_id={"narrow": across}, device_id_type=MESH,
+        )
+        hand_over = pltpu.make_async_remote_copy(
+            src_ref=whole.at[core], dst_ref=whole.at[core],
+            send_sem=half_sems.at[2], recv_sem=half_sems.at[3],
+            device_id={"narrow": partner}, device_id_type=MESH,
+        )
+
+        def weigh(t, state):
+            load(t).wait()
+
+            @pl.when(t + 1 < 2 * per)
+            def _():
+                load(t + 1).start()
+
+            value = tn(
+                slabs[t % 2].reshape(wide_count * rows, slab),
+                grads_ref[...].reshape(wide_count * rows, columns),
+            )
+            n = t % per
+
+            @pl.when(t < per)
+            def _():
+                given[n] = value.astype(low)
+                give(n).start()
+
+            @pl.when(t >= per)
+            def _():
+                give(n).wait_recv()
+                halves[0, n] = (value + taken[n].astype(jnp.float32)).astype(low)
+
+            return state
+
+        lax.fori_loop(0, 2 * per, weigh, 0)
+        exchange.start()
+        carry.start()
+        blocks.each(blocks.arrived)
+        exchange.wait()
+        whole[core] = (halves[0].astype(jnp.float32) + halves[1].astype(jnp.float32)).astype(low)
+        hand_over.start()
+        for w in range(wide_count):
+            query_all[:, w * width : (w + 1) * width] = held[w, :, :width]
+        key_all[...] = jnp.concatenate(
+            [held[w, :, width : width + head] for w in range(wide_count)], axis=1
+        )
+        value_all[...] = jnp.concatenate(
+            [held[w, :, width + head :] for w in range(wide_count)], axis=1
+        )
+
+        def one(t, state):
+            at = pl.ds(pl.multiple_of(t * tile, tile), tile)
+            out_ref[:, at] = (
+                jnp.dot(query_all[...], query_ref[:, at], preferred_element_type=jnp.float32)
+                + nt(key_all[...], key_ref[at, :])
+                + nt(value_all[...], value_ref[at, :])
+            )
+            return state
+
+        lax.fori_loop(0, model // tile, one, 0)
+        hand_over.wait()
+        weight_ref[...] = whole[...].reshape(model, columns).astype(jnp.float32)
+        blocks.settle()
+        lax.fori_loop(0, per, lambda n, state: (give(n).wait_send(), state)[1], 0)
+        carry.wait()
+
+    return pl.pallas_call(
+        kernel,
+        in_specs=[VMEM_SPEC, HBM_SPEC] + [VMEM_SPEC] * 3 + [HBM_SPEC],
+        out_specs=[VMEM_SPEC] * 2 + [HBM_SPEC],
+        out_shape=[
+            jax.ShapeDtypeStruct((rows, model), jnp.float32),
+            jax.ShapeDtypeStruct((model, columns), jnp.float32),
+            jax.ShapeDtypeStruct(carried.shape, low),
+        ],
+        scratch_shapes=[
+            pltpu.VMEM((wide_count, rows, columns), low),
+            pltpu.VMEM((2, wide_count, rows, slab), low),
+            pltpu.VMEM((rows, wide_count * width), low),
+            pltpu.VMEM((rows, wide_count * head), low),
+            pltpu.VMEM((rows, wide_count * head), low),
+            pltpu.VMEM((per, slab, columns), low),
+            pltpu.VMEM((per, slab, columns), low),
+            pltpu.VMEM((2, per, slab, columns), low),
+            pltpu.VMEM((2, per, slab, columns), low),
+            pltpu.SemaphoreType.DMA((wide_count,)),
+            pltpu.SemaphoreType.DMA((wide_count,)),
+            pltpu.SemaphoreType.DMA((2,)),
+            pltpu.SemaphoreType.DMA((per,)),
+            pltpu.SemaphoreType.DMA((per,)),
+            pltpu.SemaphoreType.DMA((4,)),
+            pltpu.SemaphoreType.DMA((2,)),
+        ],
+        compiler_params=pltpu.CompilerParams(
+            collective_id=collective_id, has_side_effects=True, vmem_limit_bytes=48 << 20
+        ),
+        name="return_and_project",
+    )(
+        grads.reshape(wide_count, rows, columns),
+        hidden_rows.reshape(wide_count, rows, model),
+        query_turned, key_weight, value_weight,
+        carried,
+    )
 
 CORPORA = 8
 GATHER_BYTES = 8 << 20
@@ -1278,12 +1610,13 @@
     head_size = query_gain.shape[0]
     own_rows, model_width = tokens.shape
     wide_count, narrow_count = lax.axis_size("wide"), lax.axis_size("narrow")
+    counts = (narrow_count, wide_count)
     wide_index, narrow_index = lax.axis_index("wide"), lax.axis_index("narrow")
     key_total = key_weight.shape[1] // head_size
     width = query_weight.shape[1]
     key_head = wide_index * key_total // wide_count
     all_rows = own_rows * wide_count
-    chained = wide_count % 2 == 0 and all_rows * model_width * 2 <= GATHER_BYTES
+    chained = wide_count == key_total and narrow_count == 4 and all_rows * model_width * 2 <= GATHER_BYTES
 
     tag_hits = corpus_tags[:, None] == jnp.arange(CORPORA, dtype=jnp.int32)[None, :]
     local_counts = jnp.sum(tag_hits.astype(wide_type), axis=0)
@@ -1296,18 +1629,6 @@
     value_columns = lax.dynamic_slice_in_dim(value_weight, key_head * head_size, head_size, 1)
     own_weights = jnp.concatenate([query_weight, key_columns, value_columns], axis=1)
     strip = width // narrow_count
-
-    def gather_strips(part):
-        return lax.all_gather(gather_wide(part), "narrow", axis=0, tiled=True)
-
-    def narrow_first(values):
-        values = values.reshape(-1, wide_count, narrow_count, strip)
-        return values.transpose(0, 2, 1, 3).reshape(-1, wide_count * width)
-
-    def wide_first(values):
-        values = values.reshape(-1, narrow_count, wide_count, strip)
-        return values.transpose(0, 2, 1, 3).reshape(-1, wide_count * width)
-
     strips = [
         own_part(output_weight, 0, narrow_index, narrow_count),
         jnp.transpose(own_part(query_weight, 1, narrow_index, narrow_count)),
@@ -1315,13 +1636,13 @@
     hidden_local = norm_scale(token_values, first_gain).astype(low)
     if chained:
         hidden_one, raw, corpus_counts, gathered = project_gathered(
-            hidden_local, own_weights, local_counts, strips, (narrow_count, wide_count), 2
+            hidden_local, own_weights, local_counts, strips, counts, 2
         )
     else:
         hidden_one = gather_wide(hidden_local)
         raw = dot_nn(hidden_one, own_weights)
-        corpus_counts = sum_everywhere(local_counts, (narrow_count, wide_count), 1)
-        gathered = [gather_strips(part) for part in strips]
+        corpus_counts = sum_everywhere(local_counts, counts, 1)
+        gathered = [lax.all_gather(part, ("wide", "narrow"), axis=0, tiled=True) for part in strips]
     output_full, query_turned = gathered
     corpus_counts = corpus_counts[0, :CORPORA]
     corpus_scale = jnp.sqrt(jnp.sum(corpus_counts) / (CORPORA * corpus_counts))
@@ -1332,8 +1653,12 @@
 
     first_block = first_blocks(segments)
     saved = attention_forward(raw, query_gain, key_gain, segments, first_block)
-    mixed = narrow_first(lax.all_to_all(saved[0], "wide", split_axis=0, concat_axis=1, tiled=True))
-    middle = token_values + dot_nn(mixed, output_full)
+    if chained:
+        branch, mixed = mix_and_project(saved[0], output_full, counts, 6)
+        middle = token_values + branch
+    else:
+        mixed = lax.all_to_all(saved[0], "wide", split_axis=0, concat_axis=1, tiled=True)
+        middle = token_values + dot_nn(mixed, output_full)
 
     together = lax.optimization_barrier
     hidden_two_local = norm_scale(middle, second_gain).astype(low)
@@ -1341,9 +1666,8 @@
         hidden_two, gate_values, up_values, activated, down_part = forward_gathered(
             hidden_two_local, gate_weight, up_weight, down_weight, wide_count, 3
         )
-        down_half = core_half(contract_first(activated, cot_low))
-        hidden_two_grad, gate_half, up_half, down_other = backward_scattered(
-            cot_low, gate_values, up_values, hidden_two, down_half, gate_weight, up_weight, down_weight,
+        hidden_two_grad, gate_half, up_half = backward_scattered(
+            cot_low, gate_values, up_values, hidden_two, gate_weight, up_weight, down_weight,
             wide_count, 4,
         )
         down_part, hidden_two_grad = together((down_part, hidden_two_grad))
@@ -1353,67 +1677,82 @@
         up_values = dot_nn(hidden_two, up_weight)
         activated = (gate_values * lax.logistic(gate_values) * up_values).astype(low)
         down_part = dot_nn(activated, down_weight)
-        down_half = core_half(contract_first(activated, cot_low))
         gate_low, up_low = swiglu_back(dot_nt(cot_low, down_weight), gate_values, up_values)
         hidden_two_grad = scatter_wide(dot_nt(gate_low, gate_weight) + dot_nt(up_low, up_weight))
         gate_half = core_half(contract_first(hidden_two, gate_low))
         up_half = core_half(contract_first(hidden_two, up_low))
-        down_other = swap_narrow(down_half, 2)
-    down_half = add_low(down_half, down_other)
-    hidden_two_grad, down_half = together((hidden_two_grad, down_half))
+        gate_other = swap_narrow(gate_half, 2)
     down_sum = scatter_wide(down_part)
 
     _, second_pull = jax.vjp(norm_scale, middle, second_gain)
     middle_part, second_gain_grad = second_pull(hidden_two_grad)
     middle_grad = out_cot + middle_part
     middle_low = middle_grad.astype(low)
-    mixed_grad = wide_first(dot_nt(middle_low, output_full).astype(low))
-    mixed_grad, mixed, middle_low = together((mixed_grad, mixed, middle_low))
-    mixed_grad = lax.all_to_all(mixed_grad, "wide", split_axis=1, concat_axis=0, tiled=True)
-    output_part = contract_first(mixed, middle_low).astype(low)
-    output_part = output_part.reshape(2, 2, wide_count * strip, model_width)
-    output_part = keep_half(output_part, 1, 1)
-    mixed_grad, output_part = together((mixed_grad, output_part))
+    if chained:
+        mixed_grad, output_part, gate_other = unmix(
+            middle_low, output_full, mixed, gate_half, counts, 7
+        )
+    else:
+        mixed_grad = lax.all_to_all(
+            dot_nt(middle_low, output_full).astype(low), "wide", split_axis=1, concat_axis=0, tiled=True
+        )
+        mixed = mixed.reshape(own_rows, wide_count, narrow_count, strip).transpose(0, 2, 1, 3)
+        output_part = contract_first(mixed.reshape(own_rows, wide_count * width), middle_low)
+        output_part = output_part.astype(low).reshape(2, 2, wide_count * strip, model_width)
+        output_part = keep_half(output_part, 1, 1)
+    mixed_grad, output_part, activated, up_half = together(
+        (mixed_grad, output_part, activated, up_half)
+    )
     output_part = keep_half(output_part, 0, 2)
-    gate_half = add_low(gate_half, swap_narrow(gate_half, 2))
+    down_half = core_half(contract_first(activated, cot_low))
+    mixed_grad, down_half = together((mixed_grad, down_half))
+    up_half = add_low(up_half, swap_narrow(up_half, 2))
+    gate_grad = hand_back(add_low(gate_half, gate_other))
     grads, query_gain_grad, key_gain_grad = attention_backward(
         raw, query_gain, key_gain, segments, first_block, saved, mixed_grad
     )
-    grads, output_part, gate_half, up_half = together((grads, output_part, gate_half, up_half))
-    up_half = add_low(up_half, swap_narrow(up_half, 2))
-    sent = lax.all_to_all(grads, "wide", split_axis=0, concat_axis=1, tiled=True).reshape(
-        own_rows, wide_count, width + 2 * head_size
-    )
-    sent, down_sum, output_part = together((sent, down_sum, output_part))
-    output_part = output_part.reshape(wide_count, strip, model_width)
-    output_part = lax.all_to_all(output_part, "wide", split_axis=0, concat_axis=0, tiled=True)
-    output_part = jnp.sum(output_part.astype(wide_type), axis=0).astype(low)
+    grads, output_part, up_half, gate_grad, down_sum = together(
+        (grads, output_part, up_half, gate_grad, down_sum)
+    )
+    output_part = lax.psum_scatter(output_part, "wide", scatter_dimension=0, tiled=True)
+    shared = wide_count // key_total
+    if chained:
+        hidden_one_grad, weight_sums, down_other = return_and_project(
+            grads, hidden_one, query_turned, key_weight, value_weight, down_half, counts, 8
+        )
+    else:
+        down_other = swap_narrow(down_half, 2)
+        weight_grads = contract_first(hidden_one, grads)
+        sent = lax.all_to_all(grads, "wide", split_axis=0, concat_axis=1, tiled=True).reshape(
+            own_rows, wide_count, width + 2 * head_size
+        )
+
+        def key_side(start):
+            part = sent[:, :, start : start + head_size]
+            if shared > 1:
+                part = jnp.sum(
+                    part.astype(wide_type).reshape(own_rows, key_total, shared, head_size), axis=2
+                ).astype(low)
+            return part.reshape(own_rows, key_total * head_size)
+
+        hidden_one_grad = (
+            dot_nn(sent[:, :, :width].reshape(own_rows, wide_count * width), query_turned)
+            + dot_nt(key_side(width), key_weight)
+            + dot_nt(key_side(width + head_size), value_weight)
+        )
+    hidden_one_grad, output_part = together((hidden_one_grad, output_part))
     output_grad = lax.all_gather(output_part, "narrow", axis=0, tiled=True).astype(wide_type)
-    down_grad, gate_grad, up_grad = (hand_back(h) for h in (down_half, gate_half, up_half))
-    shared = wide_count // key_total
-
-    def key_side(start):
-        part = sent[:, :, start : start + head_size]
-        if shared > 1:
-            part = jnp.sum(
-                part.astype(wide_type).reshape(own_rows, key_total, shared, head_size), axis=2
-            ).astype(low)
-        return part.reshape(own_rows, key_total * head_size)
-
-    hidden_one_grad = (
-        dot_nn(narrow_first(sent[:, :, :width]), query_turned)
-        + dot_nt(key_side(width), key_weight)
-        + dot_nt(key_side(width + head_size), value_weight)
-    )
+    down_grad = hand_back(add_low(down_half, down_other))
+    up_grad = hand_back(up_half)
     _, first_pull = jax.vjp(norm_scale, token_values, first_gain)
     token_part, first_gain_grad = first_pull(hidden_one_grad)
     tokens_gradient = (middle_grad + token_part).astype(low)
     tokens_gradient, down_sum = lax.optimization_barrier((tokens_gradient, down_sum))
     result = (middle + down_sum).astype(low)
 
-    weight_grads = contract_first(hidden_one, grads)
     if shared == 1:
-        weight_sums = sum_narrow(weight_grads)
+        if not chained:
+            weight_sums = sum_narrow(weight_grads)
         key_weight_grad = weight_sums[:, width : width + head_size]
         value_weight_grad = weight_sums[:, width + head_size :]
     else:
@@ -1431,7 +1770,7 @@
     gain_parts = jnp.concatenate([first_gain_grad, second_gain_grad, query_gain_grad, key_gain_grad])
     lines = -(-gain_parts.shape[0] // 1024) * 8
     gain_parts = jnp.pad(gain_parts, (0, lines * 128 - gain_parts.shape[0])).reshape(lines, 128)
-    gains = sum_everywhere(gain_parts, (narrow_count, wide_count), 5).reshape(-1)
+    gains = sum_everywhere(gain_parts, counts, 5).reshape(-1)
     starts = (0, model_width, 2 * model_width, 2 * model_width + head_size)
     sizes = (model_width, model_width, head_size, head_size)
     first_out, second_out, query_gain_out, key_gain_out = (

time: 880 us -> 859 us (0.976)
  Pallas kernels: 498 us -> 684 us
  waiting for transfers between devices: 151 us -> 36.7 us
  other arithmetic: 85.3 us -> 58 us
  matrix products: 38.3 us -> 11.3 us
  starting transfers between devices: 24.1 us -> 2.88 us
  local copies, waits for them, and re-layouts: 60.6 us -> 41.1 us
    pallas_call x1 -> x4, Pallas kernels: 119 us -> 278 us  [the longest x1 112 us: backward_scattered(): pl.pallas_call(kernel, in_specs=[hbm, hbm, hbm, hbm, vmem, vmem, vmem], o...]
    all_to_all x4 -> x0, waiting for transfers between devices: 125 us -> none  [the longest x1 52.4 us: shards(): lax.all_to_all(mixed_grad, 'wide', split_axis=1, concat_axis=0, tiled=True)]
    pallas_call x1, Pallas kernels: 138 us -> 167 us  [forward_gathered(): pl.pallas_call(kernel, in_specs=[hbm, vmem, vmem, vmem], out_specs=[hbm]...]
    all_to_all x4 -> x0, starting transfers between devices: 17.9 us -> none  [the longest x1 4.75 us: shards(): lax.all_to_all(saved[0], 'wide', split_axis=0, concat_axis=1, tiled=True)]
    dot_general x5 -> x0, matrix products: 15.3 us -> none  [the longest x2 8.64 us: dot_nn(): return jnp.dot(left, right, preferred_element_type=jnp.float32)]
    convert_element_type x8 -> x5, other arithmetic: 30 us -> 16.4 us  [add_low(): (left.astype(jnp.float32) + right.astype(jnp.float32)).astype(jnp.bfloat16)]
    dot_general x3 -> x1, matrix products: 23.1 us -> 11.3 us  [contract_first(): lax.dot_general(left, right, (((0,), (0,)), ((), ())), preferred_element_...]
    all_gather x1, waiting for transfers between devices: 0.01 us -> 10.3 us  [shards(): lax.all_gather(output_part, 'narrow', axis=0, tiled=True).astype(wide_type)]
  transfers between devices with their start and end apart: 18 -> 10, of which waited for: 6 -> 2; matrix products, arithmetic and copies ran while one was open for 15% -> 9% of each run, Pallas kernels for 26% -> 48%
where the time goes in v3:
time: 859 us; the launch traced here: 849 us
  Pallas kernels  684 us (80%)
  other arithmetic  58 us (7%)
  local copies, waits for them, and re-layouts  41.1 us (5%)
  waiting for transfers between devices  36.7 us (4%)
  between operations  15.1 us (2%)
  matrix products  11.3 us (1%)
    pallas_call x1, Pallas kernels, forward_gathered(): pl.pallas_call(kernel, in_specs=[hbm, vmem, vmem, vmem], out_specs=[hbm]...  167 us
    pallas_call x1, Pallas kernels, project_gathered(): pl.pallas_call(kernel, in_specs=[hbm, vmem, hbm] + [hbm] * len(strips), o...  154 us
    pallas_call x1, Pallas kernels, backward_scattered(): pl.pallas_call(kernel, in_specs=[hbm, hbm, hbm, hbm, vmem, vmem, vmem], o...  112 us
    pallas_call x1, Pallas kernels, return_and_project(): pl.pallas_call(kernel, in_specs=[VMEM_SPEC, HBM_SPEC] + [VMEM_SPEC] * 3 +...  86.9 us
    pallas_call x1, Pallas kernels, unmix(): pl.pallas_call(kernel, in_specs=[VMEM_SPEC] * 3 + [HBM_SPEC], out_specs=[...  55.8 us
    pallas_call x1, Pallas kernels, attention_backward(): pl.pallas_call(kernel, grid_spec=pltpu.PrefetchScalarGridSpec(num_scalar_...  44.6 us
    pallas_call x1, Pallas kernels, attention_forward(): pl.pallas_call(kernel, grid_spec=pltpu.PrefetchScalarGridSpec(num_scalar_...  30.2 us
    ppermute x6, waiting for transfers between devices, swap_narrow(): return lax.ppermute(values, 'narrow', [(i, i ^ bit) for i in range(count)])  26.3 us
  transfers between devices with their start and end apart: 10, of which 2 were waited for; matrix products, arithmetic and copies ran while one was open for 9% of the time, Pallas kernels for 48%

profile of v3, /device:TPU:0, one launch (start us, length us, event | category | flops | bytes accessed | tf_op | source)
XLA Modules:
  0.0 848.9 jit_solution(12263118790121426881)
XLA Ops:
  7.3 1.3 constant_dynamic-slice_fusion
  10.9 1.6 constant_dynamic-slice_fusion.2
  13.2 154.0 %project_gathered.1 = (bf16[8,256,2048]{2,1,0:T(8,128)(2,1)}, f32[2048,384]{1,0:T(8,128)}, f32[8,128]{1,0:T(8,128)S(1)}, bf16[8,4,64,2048]{3,2,1,0:T(8,128)(2,1)}, bf16[8,4,64,2048]{3,2,1,0:T(8,128)(2,1)}) custom-call(bf16[256,2048]{1,0:T(8,128)(2,1)S(1)} %fusion.4.local_ref, bf16[2048,384]{1,0:T(8,128)(2,1)S(1)} %pad_maximum_fusion.weights_ref, ...), custom_call_target="tpu_custom_call" | custom-call | tf_op jit(solution)/shard_map/project_gathered/pallas_call | solution.py:648
  169.1 1.2 fusion.11
  170.5 1.3 copy.41.segk_ref
  172.2 1.2 copy-done.2
  173.4 1.2 copy-done.6
  174.6 1.2 copy-done.8
  175.9 30.2 %attention_forward.1 = (bf16[2048,256]{1,0:T(8,128)(2,1)S(1)}, f32[8,2048]{1,0:T(8,128)S(1)}, bf16[2048,256]{1,0:T(8,128)(2,1)S(1)}, bf16[2048,256]{1,0:T(8,128)...) custom-call(s32[1,8]{1,0:T(1,128)S(1)} %and_select_fusion.first_ref, ...), custom_call_target="tpu_custom_call" | custom-call | tf_op jit(solution)/shard_map/attention_forward/pallas_call | solution.py:155
  208.0 4.2 copy-done
  212.3 23.5 %mix_and_project.1 = (f32[256,2048]{1,0:T(8,128)S(1)}, bf16[8,256,256]{2,1,0:T(8,128)(2,1)S(1)}) custom-call(bf16[8,256,256]{2,1,0:T(8,128)(2,1)S(1)} %bitcast.54, bf16[2048,2048]{1,0:T(8,128)(2,1)S(1)} %bitcast.53), custom_call_target="tpu_custom_call" | custom-call | tf_op jit(solution)/shard_map/mix_and_project/pallas_call | solution.py:1262
  238.1 1.2 multiply_convert_fusion.local_ref
  239.4 167.3 %forward_gathered.1 = (bf16[8,256,2048]{2,1,0:T(8,128)(2,1)}, f32[8,256,1024]{2,1,0:T(8,128)}, f32[8,256,1024]{2,1,0:T(8,128)}, bf16[8,256,1024]{2,1,0:T(8,128)(2,1)}, bf16[8,256,2048]{2,1,0:T(8,128)(2,1)}) custom-call(bf16[256,2048]{1,0:T(8,128)(2,1)} %multiply_convert_fusion.local_ref, bf16[2048,1024]{1,0:T(8,128)(2,1)} %gate_ref.3, ...), custom_call_target="tpu_custom_call" | custom-call | tf_op jit(solution)/shard_map/forward_gathered/pallas_call | solution.py:751
  406.7 111.8 %backward_scattered.1 = (f32[256,2048]{1,0:T(8,128)}, bf16[4,256,1024]{2,1,0:T(8,128)(2,1)}, bf16[4,256,1024]{2,1,0:T(8,128)(2,1)}) custom-call(bf16[8,256,2048]{2,1,0:T(8,128)(2,1)} %bitcast.65, f32[8,256,1024]{2,1,0:T(8,128)} %get-tuple-element.70.gates_ref, f32[8,256,1024]{2,1,0:T(8,128)} %get-tuple-element.71.ups_ref, ...), custom_call_target="tpu_custom_call" | custom-call | tf_op jit(solution)/shard_map/backward_scattered/pallas_call | solution.py:1038
  518.8 1.3 copy-done.31
  520.1 2.3 multiply_reduce_fusion
  522.5 2.0 fusion.14
  524.6 55.8 %unmix.1 = (bf16[8,256,256]{2,1,0:T(8,128)(2,1)S(1)}, bf16[2,8,64,2048]{3,2,1,0:T(8,128)(2,1)}, bf16[1024,1024]{1,0:T(8,128)(2,1)S(1)}) custom-call(bf16[256,2048]{1,0:T(8,128)(2,1)S(1)} %get-tuple-element.154.middle_ref, bf16[2048,2048]{1,0:T(8,128)(2,1)} %bitcast.52, bf16[8,256,256]{2,1,0:T(8,128)(2,1)S(1)} %copy-done.17, bf16[1024,1024]{1,0:T(8,128)(2,1)} %bitcast.64), custom_call_target="tpu_custom_call" | custom-call | tf_op jit(solution)/shard_map/unmix/pallas_call | solution.py:1340
  580.4 11.3 %convolution_convert_fusion = bf16[1024,2048]{1,0:T(8,128)(2,1)S(1)} fusion(bf16[2048,1024]{1,0:T(8,128)(2,1)} %bitcast.77, bf16[2048,2048]{1,0:T(8,128)(2,1)S(1)} %bitcast.67), kind=kOutput, calls=%fused_computation.15 | convolution fusion | flops 8592031744 | bytes 16777216 | tf_op jit(solution)/shard_map/dot_general | solution.py:1531
  591.7 1.5 dynamic-slice_bitcast_fusion.1
  593.2 1.3 copy-done.42
  594.8 1.1 add_convert_fusion.1
  596.2 3.2 dynamic-slice_bitcast_fusion
  599.3 1.7 collective-permute-start.1
  601.2 4.6 fusion.1.carried_ref
  605.9 44.6 %attention_backward.1 = (bf16[2048,384]{1,0:T(8,128)(2,1)}, f32[1,256]{1,0:T(1,128)S(1)}, f32[1,256]{1,0:T(1,128)S(1)}) custom-call(s32[1,8]{1,0:T(1,128)S(1)} %copy-done.29, f32[2048,384]{1,0:T(8,128)} %get-tuple-element.64.raw_ref, f32[1,256]{1,0:T(1,128)S(1)} %copy-done.25, f32[1,256]{1,0:T(1,128)S(1)} %copy-done.27, f32[2048,64]{1,0:T(8,128)S(1)} %copy-done.7, ...), custom_call_target="tpu_custom_call" | custom-call | tf_op jit(solution)/shard_map/attention_backward/pallas_call | solution.py:312
  650.5 4.5 add_convert_fusion.2
  655.1 1.9 broadcast_select_fusion.5
  656.9 4.5 maximum_convert_fusion
  661.5 26.3 %collective-permute-done.1 = bf16[512,2048]{1,0:T(8,128)(2,1)} collective-permute-done((bf16[512,2048]{1,0:T(8,128)(2,1)}, bf16[512,2048]{1,0:T(8,128)(2,1)}, u32[]{:S(2)}, u32[]{:S(2)}) %collective-permute-start.1) | collective-permute-done | bytes 2097184 | tf_op jit(solution)/shard_map/ppermute | solution.py:1553
  687.8 3.9 fusion
  691.7 2.8 convert_element_type.147
  694.6 1.4 copy-done.10
  696.0 86.9 %return_and_project.1 = (f32[256,2048]{1,0:T(8,128)S(1)}, f32[2048,384]{1,0:T(8,128)}, bf16[512,2048]{1,0:T(8,128)(2,1)S(1)}) custom-call(bf16[8,256,384]{2,1,0:T(8,128)(2,1)S(1)} %bitcast.55, bf16[8,256,2048]{2,1,0:T(8,128)(2,1)} %get-tuple-element.95.hidden_ref, bf16[2048,2048]{1,0:T(8,128)(2,1)} %bitcast.62, bf16[2048,512]{1,0:T(8,128)(2,1)} %key_ref.1, ...), custom_call_target="tpu_custom_call" | custom-call | tf_op jit(solution)/shard_map/return_and_project/pallas_call | solution.py:1482
  782.9 2.2 add_convert_fusion
  787.0 3.2 slice.44
  790.2 1.3 fusion.16
  791.5 2.4 copy.43
  793.8 1.1 copy.44
  794.9 2.5 broadcast_select_fusion.1
  797.5 4.3 maximum_convert_fusion.2
  801.7 2.5 broadcast_select_fusion.3
  804.3 4.5 maximum_convert_fusion.1
  810.3 9.9 %sum_everywhere.1 = f32[40,128]{1,0:T(8,128)} custom-call(f32[40,128]{1,0:T(8,128)} %pad_bitcast_fusion.in_ref), custom_call_target="tpu_custom_call" | custom-call | tf_op jit(solution)/shard_map/sum_everywhere/pallas_call | solution.py:1167
  824.2 3.3 fusion.8
  827.6 1.2 add_convert_fusion.3
  828.8 10.3 %all-gather.5.cloned.1.call-done = bf16[256,2048]{1,0:T(8,128)(2,1)} async-done(((bf16[64,2048]{1,0:T(8,128)(2,1)}), bf16[256,2048]{1,0:T(8,128)(2,1)}) %all-gather.5.cloned.1.call-update) | async-done | bytes 1048592 | tf_op jit(solution)/shard_map/all_gather | solution.py:1744
  839.1 2.8 convert_element_type.150
  (184 shorter events, 18.1 us)
Async XLA Ops:
  7.2 3.6 copy-start.60
  7.2 3.6 copy-start.62
  7.2 399.5 %all-gather.3.cloned.1.call-start = ((), (), s32[]{:S(2)}) async-start(), calls=%async_computation.2 | async-start | bytes 9437184 | tf_op jit(solution)/shard_map/all_gather | solution.py:1537
  8.6 3.9 copy-start.45
  13.2 155.9 %copy-start.43 = (bf16[256,2048]{1,0:T(8,128)(2,1)S(1)}, bf16[256,2048]{1,0:T(8,128)(2,1)}, u32[]{:S(2)}) copy-start(bf16[256,2048]{1,0:T(8,128)(2,1)} %param.31) | copy-start | bytes 3145732
  167.2 3.2 copy-start.20
  170.3 521.4 %reduce-scatter.3.cloned.1.call-start = ((), (), s32[]{:S(2)}) async-start(), calls=%async_computation.3 | async-start | bytes 9437184 | tf_op jit(solution)/shard_map/reduce_scatter | solution.py:1541
  171.9 65.5 %copy-start.48 = (f32[2048]{0:T(1024)}, f32[2048]{0:T(1024)S(1)}, u32[]{:S(2)}) copy-start(f32[2048]{0:T(1024)S(1)} %convert_element_type.128) | copy-start | bytes 24580
  172.0 34.1 %copy-start.24 = (f32[1,256]{1,0:T(1,128)}, f32[1,256]{1,0:T(1,128)S(1)}, u32[]{:S(2)}) copy-start(f32[1,256]{1,0:T(1,128)S(1)} %get-tuple-element.172.qg_ref) | copy-start | bytes 3076
  172.0 34.1 %copy-start.26 = (f32[1,256]{1,0:T(1,128)}, f32[1,256]{1,0:T(1,128)S(1)}, u32[]{:S(2)}) copy-start(f32[1,256]{1,0:T(1,128)S(1)} %get-tuple-element.173.kg_ref) | copy-start | bytes 3076
  172.2 33.9 %copy-start.28 = (s32[1,8]{1,0:T(1,128)}, s32[1,8]{1,0:T(1,128)S(1)}, u32[]{:S(2)}) copy-start(s32[1,8]{1,0:T(1,128)S(1)} %and_select_fusion.first_ref) | copy-start | bytes 100
  208.0 27.8 %copy-start.4 = (bf16[2048,256]{1,0:T(8,128)(2,1)}, bf16[2048,256]{1,0:T(8,128)(2,1)S(1)}, u32[]{:S(2)}) copy-start(bf16[2048,256]{1,0:T(8,128)(2,1)S(1)} %get-tuple-element.65.mixed_ref) | copy-start | bytes 3145732
  208.0 27.8 %copy-start.11 = (bf16[2048,256]{1,0:T(8,128)(2,1)}, bf16[2048,256]{1,0:T(8,128)(2,1)S(1)}, u32[]{:S(2)}) copy-start(bf16[2048,256]{1,0:T(8,128)(2,1)S(1)} %get-tuple-element.76.query_ref) | copy-start | bytes 3145732
  208.0 27.8 %copy-start.18 = (bf16[8,64,256]{2,1,0:T(8,128)(2,1)}, bf16[8,64,256]{2,1,0:T(8,128)(2,1)S(1)}, u32[]{:S(2)}) copy-start(bf16[8,64,256]{2,1,0:T(8,128)(2,1)S(1)} %get-tuple-element.88.keyt_ref) | copy-start | bytes 786436
  208.0 27.8 %copy-start.22 = (f32[8,2048]{1,0:T(8,128)}, f32[8,2048]{1,0:T(8,128)S(1)}, u32[]{:S(2)}) copy-start(f32[8,2048]{1,0:T(8,128)S(1)} %get-tuple-element.75.lse_ref) | copy-start | bytes 196612
  208.0 4.3 copy-start
  212.3 23.6 %copy-start.34 = (bf16[256,2048]{1,0:T(8,128)(2,1)S(1)}, bf16[256,2048]{1,0:T(8,128)(2,1)}, u32[]{:S(2)}) copy-start(bf16[256,2048]{1,0:T(8,128)(2,1)} %param.19) | copy-start | bytes 3145732
  518.5 290.3 %reduce-scatter.5.cloned.1.call-start = ((), (), s32[]{:S(2)}) async-start(), calls=%async_computation.4 | async-start | bytes 2359296 | tf_op jit(solution)/shard_map/reduce_scatter | solution.py:1717
  522.5 57.8 %slice-start = ((s8[8388608]{0:T(1024)(128)(4,1)}), s8[4194304]{0:T(1024)(128)(4,1)S(1)}, s32[]{:S(2)}) async-start(s8[8388608]{0:T(1024)(128)(4,1)} %bitcast.66), calls=%async_computation.6 | async-start | bytes 8388608
  524.6 55.8 %slice-start.1 = ((s8[8388608]{0:T(1024)(128)(4,1)}), s8[4194304]{0:T(1024)(128)(4,1)S(1)}, s32[]{:S(2)}) async-start(s8[8388608]{0:T(1024)(128)(4,1)} %bitcast.66), calls=%async_computation.7 | async-start | bytes 8388608
  580.3 11.3 %copy-start.15 = (bf16[8,256,256]{2,1,0:T(8,128)(2,1)}, bf16[8,256,256]{2,1,0:T(8,128)(2,1)S(1)}, u32[]{:S(2)}) copy-start(bf16[8,256,256]{2,1,0:T(8,128)(2,1)S(1)} %get-tuple-element.79) | copy-start | bytes 3145732
  594.5 6.7 collective-permute-start
  594.5 56.1 %collective-permute-start.2 = (bf16[1024,1024]{1,0:T(8,128)(2,1)}, bf16[1024,1024]{1,0:T(8,128)(2,1)}, u32[]{:S(2)}, u32[]{:S(2)}) collective-permute-start(bf16[1024,1024]{1,0:T(8,128)(2,1)} %bitcast.18), channel_id=1, source_target_pairs={{0,16},{8,24},{16,0},{24,8},{1,17},{9,25},{17,1},{25,9},{2,18},{10... | collective-permute-start | bytes 6291464 | tf_op jit(solution)/shard_map/ppermute | solution.py:1553
  595.9 59.2 %collective-permute-start.3 = (bf16[1024,1024]{1,0:T(8,128)(2,1)S(1)}, bf16[1024,1024]{1,0:T(8,128)(2,1)}, u32[]{:S(2)}, u32[]{:S(2)}) collective-permute-start(bf16[1024,1024]{1,0:T(8,128)(2,1)S(1)} %add_convert_fusion.1), channel_id=1, source_target_pairs={{0,8},{8,0},{16,24},{24,16},{1,9},{9,1},{17,25},{25,17},{2,10},{10... | collective-permute-start | bytes 6291464 | tf_op jit(solution)/shard_map/ppermute | solution.py:1553
  599.3 88.4 %collective-permute-start.1 = (bf16[512,2048]{1,0:T(8,128)(2,1)}, bf16[512,2048]{1,0:T(8,128)(2,1)}, u32[]{:S(2)}, u32[]{:S(2)}) collective-permute-start(bf16[512,2048]{1,0:T(8,128)(2,1)} %dynamic-slice_bitcast_fusion), channel_id=1, source_target_pairs={{0,16},{8,24},{16,0},{24,8},{1,17},{9,25},{17,1},{25,9},{2,18},{10... | collective-permute-start | bytes 6291464 | tf_op jit(solution)/shard_map/ppermute | solution.py:1553
  601.1 4.7 copy-start.3
  601.1 4.7 copy-start.5
  601.1 4.7 copy-start.7
  601.1 4.7 copy-start.9
  601.1 4.7 copy-start.12
  601.1 4.7 copy-start.19
  601.1 4.7 copy-start.21
  601.1 4.7 copy-start.23
  601.1 4.7 copy-start.25
  601.1 4.7 copy-start.27
  601.1 4.7 copy-start.29
  656.9 30.8 %copy-start.41 = (bf16[2,8,64,2048]{3,2,1,0:T(8,128)(2,1)S(1)}, bf16[2,8,64,2048]{3,2,1,0:T(8,128)(2,1)}, u32[]{:S(2)}) copy-start(bf16[2,8,64,2048]{3,2,1,0:T(8,128)(2,1)} %get-tuple-element.80) | copy-start | bytes 12582916
  694.5 144.6 %all-gather.5.cloned.1.call-start = ((), (), s32[]{:S(2)}) async-start(), calls=%async_computation.5 | async-start | bytes 1310720 | tf_op jit(solution)/shard_map/all_gather | solution.py:1744
  696.0 86.9 %copy-start.36 = (bf16[512,2048]{1,0:T(8,128)(2,1)S(1)}, bf16[512,2048]{1,0:T(8,128)(2,1)}, u32[]{:S(2)}) copy-start(bf16[512,2048]{1,0:T(8,128)(2,1)} %fusion.1.carried_ref) | copy-start | bytes 6291460
  785.1 9.8 %collective-permute-start.5 = (bf16[512,2048]{1,0:T(8,128)(2,1)}, bf16[512,2048]{1,0:T(8,128)(2,1)}, u32[]{:S(2)}, u32[]{:S(2)}) collective-permute-start(bf16[512,2048]{1,0:T(8,128)(2,1)} %add_convert_fusion), channel_id=1, source_target_pairs={{0,8},{8,0},{16,24},{24,16},{1,9},{9,1},{17,25},{25,17},{2,10},{10... | collective-permute-start | bytes 6291464 | tf_op jit(solution)/shard_map/ppermute | solution.py:1553
  785.2 16.6 %collective-permute-start.4 = (bf16[1024,1024]{1,0:T(8,128)(2,1)}, bf16[1024,1024]{1,0:T(8,128)(2,1)}, u32[]{:S(2)}, u32[]{:S(2)}) collective-permute-start(bf16[1024,1024]{1,0:T(8,128)(2,1)} %add_convert_fusion.2), channel_id=1, source_target_pairs={{0,8},{8,0},{16,24},{24,16},{1,9},{9,1},{17,25},{25,17},{2,10},{10... | collective-permute-start | bytes 6291464 | tf_op jit(solution)/shard_map/ppermute | solution.py:1553
  786.9 3.2 copy-start.40
  804.2 4.6 copy-start.35
  804.3 4.6 copy-start.47
  804.3 4.6 copy-start.51
  808.8 15.4 %copy-start.57 = (f32[256]{0:T(256)S(1)}, f32[256]{0:T(256)}, u32[]{:S(2)}) copy-start(f32[256]{0:T(256)} %copy-done.56) | copy-start | bytes 3076
  824.2 3.3 copy-start.32
  824.2 3.3 copy-start.37
  (29 other events, 52.3 us)
Sparse Core Ops, SparseCore 0:
  170.5 160.3 all-gather.2
  518.6 172.6 reduce-scatter.2
  695.3 100.7 reduce-scatter.4
  822.3 16.7 all-gather.4

commit v4 on v3

--- a/solution.py
+++ b/solution.py
@@ -1149,30 +1149,73 @@
     )
 
 
-def sum_everywhere(values, counts, collective_id):
-    def kernel(in_ref, out_ref, mine, held, total, load_sem, *sems):
+def sum_everywhere(values, counts, collective_id, strip=None):
+    extra = [] if strip is None else [strip]
+
+    def kernel(in_ref, *refs):
+        strip_refs, refs = refs[: len(extra)], refs[len(extra) :]
+        out_ref, refs = refs[0], refs[1:]
+        gathered_refs, refs = refs[: len(extra)], refs[len(extra) :]
+        mine, held, total, load_sem, narrow_send, narrow_recv, wide_send, wide_recv, *rest = refs
         load = pltpu.make_async_copy(in_ref, mine, load_sem)
         load.start()
         arrive = greet_all(counts)
+        me = lax.axis_index("narrow")
+        if extra:
+            strips, strip_sem, strip_send, strip_recv = rest
+            own = pltpu.make_async_copy(strip_refs[0], strips.at[me], strip_sem)
+            own.start()
+            own.wait()
+
+        def strip_copy(who, slot):
+            return pltpu.make_async_remote_copy(
+                src_ref=strips.at[me], dst_ref=strips.at[slot],
+                send_sem=strip_send.at[who], recv_sem=strip_recv.at[slot],
+                device_id={"narrow": who}, device_id_type=MESH,
+            )
+
         load.wait()
         arrive()
-        narrow, wide = exchange_pair(counts, mine, held, total, *sems)
+        narrow, wide = exchange_pair(
+            counts, mine, held, total, narrow_send, narrow_recv, wide_send, wide_recv
+        )
         narrow.start()
+        if extra:
+            peers(0, counts, lambda who: strip_copy(who, me).start())
         total[...] = narrow.total()
         wide.start()
         out_ref[...] = wide.total()
         narrow.settle()
         wide.settle()
-
-    return pl.pallas_call(
+        if extra:
+            peers(0, counts, lambda who: strip_copy(who, who).wait_recv())
+            gathered_refs[0][...] = strips[...]
+            peers(0, counts, lambda who: strip_copy(who, me).wait_send())
+
+    vmem, hbm = pl.BlockSpec(memory_space=pltpu.VMEM), pl.BlockSpec(memory_space=pl.ANY)
+    out_shape = [jax.ShapeDtypeStruct(values.shape, jnp.float32)]
+    scratch = exchange_scratch(values.shape, counts)
+    if extra:
+        whole = (counts[0],) + strip.shape
+        out_shape += [jax.ShapeDtypeStruct(whole, strip.dtype)]
+        scratch += [
+            pltpu.VMEM(whole, strip.dtype),
+            pltpu.SemaphoreType.DMA,
+            pltpu.SemaphoreType.DMA((counts[0],)),
+            pltpu.SemaphoreType.DMA((counts[0],)),
+        ]
+    results = pl.pallas_call(
         kernel,
-        in_specs=[pl.BlockSpec(memory_space=pl.ANY)],
-        out_specs=pl.BlockSpec(memory_space=pltpu.VMEM),
-        out_shape=jax.ShapeDtypeStruct(values.shape, jnp.float32),
-        scratch_shapes=exchange_scratch(values.shape, counts),
+        in_specs=[hbm] * (1 + len(extra)),
+        out_specs=[vmem] * (1 + len(extra)),
+        out_shape=out_shape,
+        scratch_shapes=scratch,
         compiler_params=pltpu.CompilerParams(collective_id=collective_id, has_side_effects=True),
         name="sum_everywhere",
-    )(values)
+    )(values, *extra)
+    if not extra:
+        return results[0]
+    return results[0], results[1].reshape(-1, strip.shape[1])
 
 
 def greet_wide(counts, partners=()):
@@ -1741,7 +1784,6 @@
             + dot_nt(key_side(width + head_size), value_weight)
         )
     hidden_one_grad, output_part = together((hidden_one_grad, output_part))
-    output_grad = lax.all_gather(output_part, "narrow", axis=0, tiled=True).astype(wide_type)
     down_grad = hand_back(add_low(down_half, down_other))
     up_grad = hand_back(up_half)
     _, first_pull = jax.vjp(norm_scale, token_values, first_gain)
@@ -1770,7 +1812,8 @@
     gain_parts = jnp.concatenate([first_gain_grad, second_gain_grad, query_gain_grad, key_gain_grad])
     lines = -(-gain_parts.shape[0] // 1024) * 8
     gain_parts = jnp.pad(gain_parts, (0, lines * 128 - gain_parts.shape[0])).reshape(lines, 128)
-    gains = sum_everywhere(gain_parts, counts, 5).reshape(-1)
+    gains, output_grad = sum_everywhere(gain_parts, counts, 5, output_part)
+    gains, output_grad = gains.reshape(-1), output_grad.astype(wide_type)
     starts = (0, model_width, 2 * model_width, 2 * model_width + head_size)
     sizes = (model_width, model_width, head_size, head_size)
     first_out, second_out, query_gain_out, key_gain_out = (

time: 859 us -> 849 us (0.988)
  waiting for transfers between devices: 36.7 us -> 25 us
    all_gather x1 -> x0, waiting for transfers between devices: 10.3 us -> none  [shards(): lax.all_gather(output_part, 'narrow', axis=0, tiled=True).astype(wide_type)]
    pallas_call x1, Pallas kernels: 23.5 us -> 32.9 us  [mix_and_project(): pl.pallas_call(kernel, in_specs=[VMEM_SPEC, VMEM_SPEC], out_specs=[VMEM_S...]
    pallas_call x1, Pallas kernels: 167 us -> 158 us  [forward_gathered(): pl.pallas_call(kernel, in_specs=[hbm, vmem, vmem, vmem], out_specs=[hbm]...]
    unnamed x137 -> x141, local copies, waits for them, and re-layouts: 21.2 us -> 22.1 us
  transfers between devices with their start and end apart: 10 -> 9, of which waited for: 2 -> 2; matrix products, arithmetic and copies ran while one was open for 9% -> 8% of each run, Pallas kernels for 48% -> 49%
where the time goes in v4:
time: 849 us; the launch traced here: 841 us
  Pallas kernels  690 us (81%)
  other arithmetic  56.6 us (7%)
  local copies, waits for them, and re-layouts  40.4 us (5%)
  waiting for transfers between devices  25 us (3%)
  between operations  15.1 us (2%)
  matrix products  11.1 us (1%)
    pallas_call x1, Pallas kernels, forward_gathered(): pl.pallas_call(kernel, in_specs=[hbm, vmem, vmem, vmem], out_specs=[hbm]...  158 us
    pallas_call x1, Pallas kernels, project_gathered(): pl.pallas_call(kernel, in_specs=[hbm, vmem, hbm] + [hbm] * len(strips), o...  154 us
    pallas_call x1, Pallas kernels, backward_scattered(): pl.pallas_call(kernel, in_specs=[hbm, hbm, hbm, hbm, vmem, vmem, vmem], o...  110 us
    pallas_call x1, Pallas kernels, return_and_project(): pl.pallas_call(kernel, in_specs=[VMEM_SPEC, HBM_SPEC] + [VMEM_SPEC] * 3 +...  87.9 us
    pallas_call x1, Pallas kernels, unmix(): pl.pallas_call(kernel, in_specs=[VMEM_SPEC] * 3 + [HBM_SPEC], out_specs=[...  53 us
    pallas_call x1, Pallas kernels, attention_backward(): pl.pallas_call(kernel, grid_spec=pltpu.PrefetchScalarGridSpec(num_scalar_...  46.1 us
    pallas_call x1, Pallas kernels, mix_and_project(): pl.pallas_call(kernel, in_specs=[VMEM_SPEC, VMEM_SPEC], out_specs=[VMEM_S...  32.9 us
    pallas_call x1, Pallas kernels, attention_forward(): pl.pallas_call(kernel, grid_spec=pltpu.PrefetchScalarGridSpec(num_scalar_...  31.3 us
  transfers between devices with their start and end apart: 9, of which 2 were waited for; matrix products, arithmetic and copies ran while one was open for 8% of the time, Pallas kernels for 49%

profile of v4, /device:TPU:0, one launch (start us, length us, event | category | flops | bytes accessed | tf_op | source)
XLA Modules:
  0.0 841.5 jit_solution(17548417919563502376)
XLA Ops:
  7.3 1.3 constant_dynamic-slice_fusion
  8.8 1.1 constant_dynamic-slice_fusion.1.refs_0_
  10.9 1.6 constant_dynamic-slice_fusion.2
  13.2 154.0 %project_gathered.1 = (bf16[8,256,2048]{2,1,0:T(8,128)(2,1)}, f32[2048,384]{1,0:T(8,128)}, f32[8,128]{1,0:T(8,128)S(1)}, bf16[8,4,64,2048]{3,2,1,0:T(8,128)(2,1)}, bf16[8,4,64,2048]{3,2,1,0:T(8,128)(2,1)}) custom-call(bf16[256,2048]{1,0:T(8,128)(2,1)S(1)} %fusion.4.local_ref, bf16[2048,384]{1,0:T(8,128)(2,1)S(1)} %pad_maximum_fusion.weights_ref, ...), custom_call_target="tpu_custom_call" | custom-call | tf_op jit(solution)/shard_map/project_gathered/pallas_call | solution.py:648
  169.2 1.2 fusion.11
  170.6 1.3 copy.41.segk_ref
  172.3 1.2 copy-done.2
  173.5 1.2 copy-done.6
  174.7 1.2 copy-done.8
  176.0 31.3 %attention_forward.1 = (bf16[2048,256]{1,0:T(8,128)(2,1)S(1)}, f32[8,2048]{1,0:T(8,128)S(1)}, bf16[2048,256]{1,0:T(8,128)(2,1)S(1)}, bf16[2048,256]{1,0:T(8,128)...) custom-call(s32[1,8]{1,0:T(1,128)S(1)} %and_select_fusion.first_ref, ...), custom_call_target="tpu_custom_call" | custom-call | tf_op jit(solution)/shard_map/attention_forward/pallas_call | solution.py:155
  209.2 4.2 copy-done
  213.5 32.9 %mix_and_project.1 = (f32[256,2048]{1,0:T(8,128)S(1)}, bf16[8,256,256]{2,1,0:T(8,128)(2,1)S(1)}) custom-call(bf16[8,256,256]{2,1,0:T(8,128)(2,1)S(1)} %bitcast.57, bf16[2048,2048]{1,0:T(8,128)(2,1)S(1)} %bitcast.56), custom_call_target="tpu_custom_call" | custom-call | tf_op jit(solution)/shard_map/mix_and_project/pallas_call | solution.py:1305
  248.8 1.2 multiply_convert_fusion.local_ref
  250.0 158.2 %forward_gathered.1 = (bf16[8,256,2048]{2,1,0:T(8,128)(2,1)}, f32[8,256,1024]{2,1,0:T(8,128)}, f32[8,256,1024]{2,1,0:T(8,128)}, bf16[8,256,1024]{2,1,0:T(8,128)(2,1)}, bf16[8,256,2048]{2,1,0:T(8,128)(2,1)}) custom-call(bf16[256,2048]{1,0:T(8,128)(2,1)} %multiply_convert_fusion.local_ref, bf16[2048,1024]{1,0:T(8,128)(2,1)} %gate_ref.3, ...), custom_call_target="tpu_custom_call" | custom-call | tf_op jit(solution)/shard_map/forward_gathered/pallas_call | solution.py:751
  408.2 110.5 %backward_scattered.1 = (f32[256,2048]{1,0:T(8,128)}, bf16[4,256,1024]{2,1,0:T(8,128)(2,1)}, bf16[4,256,1024]{2,1,0:T(8,128)(2,1)}) custom-call(bf16[8,256,2048]{2,1,0:T(8,128)(2,1)} %bitcast.68, f32[8,256,1024]{2,1,0:T(8,128)} %get-tuple-element.72.gates_ref, f32[8,256,1024]{2,1,0:T(8,128)} %get-tuple-element.73.ups_ref, ...), custom_call_target="tpu_custom_call" | custom-call | tf_op jit(solution)/shard_map/backward_scattered/pallas_call | solution.py:1038
  519.0 1.3 copy-done.31
  520.3 2.3 multiply_reduce_fusion
  522.8 2.0 fusion.14
  524.8 53.0 %unmix.1 = (bf16[8,256,256]{2,1,0:T(8,128)(2,1)S(1)}, bf16[2,8,64,2048]{3,2,1,0:T(8,128)(2,1)}, bf16[1024,1024]{1,0:T(8,128)(2,1)S(1)}) custom-call(bf16[256,2048]{1,0:T(8,128)(2,1)S(1)} %get-tuple-element.158.middle_ref, bf16[2048,2048]{1,0:T(8,128)(2,1)} %bitcast.55, bf16[8,256,256]{2,1,0:T(8,128)(2,1)S(1)} %copy-done.17, bf16[1024,1024]{1,0:T(8,128)(2,1)} %bitcast.67), custom_call_target="tpu_custom_call" | custom-call | tf_op jit(solution)/shard_map/unmix/pallas_call | solution.py:1383
  577.9 11.1 %convolution_convert_fusion = bf16[1024,2048]{1,0:T(8,128)(2,1)S(1)} fusion(bf16[2048,1024]{1,0:T(8,128)(2,1)} %bitcast.80, bf16[2048,2048]{1,0:T(8,128)(2,1)S(1)} %bitcast.70), kind=kOutput, calls=%fused_computation.15 | convolution fusion | flops 8592031744 | bytes 16777216 | tf_op jit(solution)/shard_map/dot_general | solution.py:1574
  589.1 1.5 dynamic-slice_bitcast_fusion.1
  590.5 1.4 copy-done.43
  591.9 2.2 collective-permute-start.2
  594.1 1.1 add_convert_fusion.1
  595.5 3.2 dynamic-slice_bitcast_fusion
  599.1 4.6 fusion.1.carried_ref
  603.8 46.1 %attention_backward.1 = (bf16[2048,384]{1,0:T(8,128)(2,1)}, f32[1,256]{1,0:T(1,128)S(1)}, f32[1,256]{1,0:T(1,128)S(1)}) custom-call(s32[1,8]{1,0:T(1,128)S(1)} %copy-done.29, f32[2048,384]{1,0:T(8,128)} %get-tuple-element.66.raw_ref, f32[1,256]{1,0:T(1,128)S(1)} %copy-done.25, f32[1,256]{1,0:T(1,128)S(1)} %copy-done.27, f32[2048,64]{1,0:T(8,128)S(1)} %copy-done.7, ...), custom_call_target="tpu_custom_call" | custom-call | tf_op jit(solution)/shard_map/attention_backward/pallas_call | solution.py:312
  650.0 4.9 add_convert_fusion.2
  654.9 1.9 broadcast_select_fusion.5
  656.7 4.5 maximum_convert_fusion
  661.3 24.4 %collective-permute-done.1 = bf16[512,2048]{1,0:T(8,128)(2,1)} collective-permute-done((bf16[512,2048]{1,0:T(8,128)(2,1)}, bf16[512,2048]{1,0:T(8,128)(2,1)}, u32[]{:S(2)}, u32[]{:S(2)}) %collective-permute-start.1) | collective-permute-done | bytes 2097184 | tf_op jit(solution)/shard_map/ppermute | solution.py:1596
  685.7 3.8 fusion
  690.0 2.8 convert_element_type.150
  692.8 1.4 copy-done.10
  694.2 87.9 %return_and_project.1 = (f32[256,2048]{1,0:T(8,128)S(1)}, f32[2048,384]{1,0:T(8,128)}, bf16[512,2048]{1,0:T(8,128)(2,1)S(1)}) custom-call(bf16[8,256,384]{2,1,0:T(8,128)(2,1)S(1)} %bitcast.58, bf16[8,256,2048]{2,1,0:T(8,128)(2,1)} %get-tuple-element.97.hidden_ref, bf16[2048,2048]{1,0:T(8,128)(2,1)} %bitcast.65, bf16[2048,512]{1,0:T(8,128)(2,1)} %key_ref.1, ...), custom_call_target="tpu_custom_call" | custom-call | tf_op jit(solution)/shard_map/return_and_project/pallas_call | solution.py:1525
  782.1 2.2 add_convert_fusion
  786.1 3.2 slice.44
  789.4 1.3 fusion.16
  790.7 2.3 copy.43
  793.0 1.1 copy.44
  794.1 2.5 broadcast_select_fusion.1
  796.6 4.3 maximum_convert_fusion.2
  800.9 2.5 broadcast_select_fusion.3
  803.4 4.5 maximum_convert_fusion.1
  809.4 15.8 %sum_everywhere.1 = (f32[40,128]{1,0:T(8,128)}, bf16[4,64,2048]{2,1,0:T(8,128)(2,1)}) custom-call(f32[40,128]{1,0:T(8,128)} %pad_bitcast_fusion.in_ref, bf16[64,2048]{1,0:T(8,128)(2,1)} %reduce-scatter.5.cloned.1.call-done.refs_0_), custom_call_target="tpu_custom_call" | custom-call | tf_op jit(solution)/shard_map/sum_everywhere/pallas_call | solution.py:1207
  825.2 2.9 bitcast_convert_fusion
  830.7 1.6 fusion.8
  833.3 1.2 add_convert_fusion.3
  (185 shorter events, 17.0 us)
Async XLA Ops:
  7.2 3.6 copy-start.62
  7.2 3.6 copy-start.64
  7.2 401.0 %all-gather.2.cloned.1.call-start = ((), (), s32[]{:S(2)}) async-start(), calls=%async_computation.2 | async-start | bytes 9437184 | tf_op jit(solution)/shard_map/all_gather | solution.py:1580
  8.6 3.9 copy-start.46
  13.2 156.0 %copy-start.44 = (bf16[256,2048]{1,0:T(8,128)(2,1)S(1)}, bf16[256,2048]{1,0:T(8,128)(2,1)}, u32[]{:S(2)}) copy-start(bf16[256,2048]{1,0:T(8,128)(2,1)} %param.31) | copy-start | bytes 3145732
  167.2 3.3 copy-start.20
  169.2 3.1 copy-start.1
  170.4 519.5 %reduce-scatter.3.cloned.1.call-start = ((), (), s32[]{:S(2)}) async-start(), calls=%async_computation.3 | async-start | bytes 9437184 | tf_op jit(solution)/shard_map/reduce_scatter | solution.py:1584
  171.9 76.1 %copy-start.49 = (f32[2048]{0:T(1024)}, f32[2048]{0:T(1024)S(1)}, u32[]{:S(2)}) copy-start(f32[2048]{0:T(1024)S(1)} %convert_element_type.131) | copy-start | bytes 24580
  172.0 35.2 %copy-start.24 = (f32[1,256]{1,0:T(1,128)}, f32[1,256]{1,0:T(1,128)S(1)}, u32[]{:S(2)}) copy-start(f32[1,256]{1,0:T(1,128)S(1)} %get-tuple-element.176.qg_ref) | copy-start | bytes 3076
  172.0 35.2 %copy-start.26 = (f32[1,256]{1,0:T(1,128)}, f32[1,256]{1,0:T(1,128)S(1)}, u32[]{:S(2)}) copy-start(f32[1,256]{1,0:T(1,128)S(1)} %get-tuple-element.177.kg_ref) | copy-start | bytes 3076
  172.3 35.0 %copy-start.28 = (s32[1,8]{1,0:T(1,128)}, s32[1,8]{1,0:T(1,128)S(1)}, u32[]{:S(2)}) copy-start(s32[1,8]{1,0:T(1,128)S(1)} %and_select_fusion.first_ref) | copy-start | bytes 100
  209.2 37.2 %copy-start.4 = (bf16[2048,256]{1,0:T(8,128)(2,1)}, bf16[2048,256]{1,0:T(8,128)(2,1)S(1)}, u32[]{:S(2)}) copy-start(bf16[2048,256]{1,0:T(8,128)(2,1)S(1)} %get-tuple-element.67.mixed_ref) | copy-start | bytes 3145732
  209.2 37.2 %copy-start.11 = (bf16[2048,256]{1,0:T(8,128)(2,1)}, bf16[2048,256]{1,0:T(8,128)(2,1)S(1)}, u32[]{:S(2)}) copy-start(bf16[2048,256]{1,0:T(8,128)(2,1)S(1)} %get-tuple-element.78.query_ref) | copy-start | bytes 3145732
  209.2 37.2 %copy-start.18 = (bf16[8,64,256]{2,1,0:T(8,128)(2,1)}, bf16[8,64,256]{2,1,0:T(8,128)(2,1)S(1)}, u32[]{:S(2)}) copy-start(bf16[8,64,256]{2,1,0:T(8,128)(2,1)S(1)} %get-tuple-element.90.keyt_ref) | copy-start | bytes 786436
  209.2 37.2 %copy-start.22 = (f32[8,2048]{1,0:T(8,128)}, f32[8,2048]{1,0:T(8,128)S(1)}, u32[]{:S(2)}) copy-start(f32[8,2048]{1,0:T(8,128)S(1)} %get-tuple-element.77.lse_ref) | copy-start | bytes 196612
  209.2 4.3 copy-start
  213.5 33.0 %copy-start.34 = (bf16[256,2048]{1,0:T(8,128)(2,1)S(1)}, bf16[256,2048]{1,0:T(8,128)(2,1)}, u32[]{:S(2)}) copy-start(bf16[256,2048]{1,0:T(8,128)(2,1)} %param.19) | copy-start | bytes 3145732
  518.7 289.2 %reduce-scatter.5.cloned.1.call-start = ((), (), s32[]{:S(2)}) async-start(), calls=%async_computation.4 | async-start | bytes 2359296 | tf_op jit(solution)/shard_map/reduce_scatter | solution.py:1760
  522.8 55.1 %slice-start = ((s8[8388608]{0:T(1024)(128)(4,1)}), s8[4194304]{0:T(1024)(128)(4,1)S(1)}, s32[]{:S(2)}) async-start(s8[8388608]{0:T(1024)(128)(4,1)} %bitcast.69), calls=%async_computation.5 | async-start | bytes 8388608
  524.8 53.1 %slice-start.1 = ((s8[8388608]{0:T(1024)(128)(4,1)}), s8[4194304]{0:T(1024)(128)(4,1)S(1)}, s32[]{:S(2)}) async-start(s8[8388608]{0:T(1024)(128)(4,1)} %bitcast.69), calls=%async_computation.6 | async-start | bytes 8388608
  577.9 11.2 %copy-start.15 = (bf16[8,256,256]{2,1,0:T(8,128)(2,1)}, bf16[8,256,256]{2,1,0:T(8,128)(2,1)S(1)}, u32[]{:S(2)}) copy-start(bf16[8,256,256]{2,1,0:T(8,128)(2,1)S(1)} %get-tuple-element.81) | copy-start | bytes 3145732
  589.1 5.1 copy-start.39
  591.9 7.2 collective-permute-start
  591.9 58.0 %collective-permute-start.2 = (bf16[1024,1024]{1,0:T(8,128)(2,1)}, bf16[1024,1024]{1,0:T(8,128)(2,1)}, u32[]{:S(2)}, u32[]{:S(2)}) collective-permute-start(bf16[1024,1024]{1,0:T(8,128)(2,1)} %bitcast.18), channel_id=1, source_target_pairs={{0,16},{8,24},{16,0},{24,8},{1,17},{9,25},{17,1},{25,9},{2,18},{10... | collective-permute-start | bytes 6291464 | tf_op jit(solution)/shard_map/ppermute | solution.py:1596
  595.2 59.6 %collective-permute-start.3 = (bf16[1024,1024]{1,0:T(8,128)(2,1)S(1)}, bf16[1024,1024]{1,0:T(8,128)(2,1)}, u32[]{:S(2)}, u32[]{:S(2)}) collective-permute-start(bf16[1024,1024]{1,0:T(8,128)(2,1)S(1)} %add_convert_fusion.1), channel_id=1, source_target_pairs={{0,8},{8,0},{16,24},{24,16},{1,9},{9,1},{17,25},{25,17},{2,10},{10... | collective-permute-start | bytes 6291464 | tf_op jit(solution)/shard_map/ppermute | solution.py:1596
  598.7 87.0 %collective-permute-start.1 = (bf16[512,2048]{1,0:T(8,128)(2,1)}, bf16[512,2048]{1,0:T(8,128)(2,1)}, u32[]{:S(2)}, u32[]{:S(2)}) collective-permute-start(bf16[512,2048]{1,0:T(8,128)(2,1)} %dynamic-slice_bitcast_fusion), channel_id=1, source_target_pairs={{0,16},{8,24},{16,0},{24,8},{1,17},{9,25},{17,1},{25,9},{2,18},{10... | collective-permute-start | bytes 6291464 | tf_op jit(solution)/shard_map/ppermute | solution.py:1596
  599.0 4.7 copy-start.3
  599.0 4.7 copy-start.5
  599.0 4.7 copy-start.7
  599.0 4.7 copy-start.9
  599.0 4.8 copy-start.12
  599.0 4.8 copy-start.19
  599.0 4.7 copy-start.21
  599.0 4.7 copy-start.23
  599.0 4.7 copy-start.25
  599.0 4.7 copy-start.27
  599.1 4.7 copy-start.29
  656.7 29.0 %copy-start.42 = (bf16[2,8,64,2048]{3,2,1,0:T(8,128)(2,1)S(1)}, bf16[2,8,64,2048]{3,2,1,0:T(8,128)(2,1)}, u32[]{:S(2)}) copy-start(bf16[2,8,64,2048]{3,2,1,0:T(8,128)(2,1)} %get-tuple-element.82) | copy-start | bytes 12582916
  694.2 87.9 %copy-start.36 = (bf16[512,2048]{1,0:T(8,128)(2,1)S(1)}, bf16[512,2048]{1,0:T(8,128)(2,1)}, u32[]{:S(2)}) copy-start(bf16[512,2048]{1,0:T(8,128)(2,1)} %fusion.1.carried_ref) | copy-start | bytes 6291460
  784.3 9.8 %collective-permute-start.5 = (bf16[512,2048]{1,0:T(8,128)(2,1)}, bf16[512,2048]{1,0:T(8,128)(2,1)}, u32[]{:S(2)}, u32[]{:S(2)}) collective-permute-start(bf16[512,2048]{1,0:T(8,128)(2,1)} %add_convert_fusion), channel_id=1, source_target_pairs={{0,8},{8,0},{16,24},{24,16},{1,9},{9,1},{17,25},{25,17},{2,10},{10... | collective-permute-start | bytes 6291464 | tf_op jit(solution)/shard_map/ppermute | solution.py:1596
  784.3 16.6 %collective-permute-start.4 = (bf16[1024,1024]{1,0:T(8,128)(2,1)}, bf16[1024,1024]{1,0:T(8,128)(2,1)}, u32[]{:S(2)}, u32[]{:S(2)}) collective-permute-start(bf16[1024,1024]{1,0:T(8,128)(2,1)} %add_convert_fusion.2), channel_id=1, source_target_pairs={{0,8},{8,0},{16,24},{24,16},{1,9},{9,1},{17,25},{25,17},{2,10},{10... | collective-permute-start | bytes 6291464 | tf_op jit(solution)/shard_map/ppermute | solution.py:1596
  786.1 3.2 copy-start.41
  803.4 4.6 copy-start.35
  803.4 4.6 copy-start.48
  803.4 4.5 copy-start.52
  808.7 21.9 %copy-start.59 = (f32[256]{0:T(256)S(1)}, f32[256]{0:T(256)}, u32[]{:S(2)}) copy-start(f32[256]{0:T(256)} %copy-done.58) | copy-start | bytes 3076
  825.2 5.5 copy-start.37
  (30 other events, 53.5 us)
Sparse Core Ops, SparseCore 0:
  170.6 156.1 all-gather.1
  518.9 171.0 reduce-scatter.2
  693.9 100.6 reduce-scatter.4

commit v5 on v4

--- a/solution.py
+++ b/solution.py
@@ -1754,8 +1754,9 @@
     grads, query_gain_grad, key_gain_grad = attention_backward(
         raw, query_gain, key_gain, segments, first_block, saved, mixed_grad
     )
-    grads, output_part, up_half, gate_grad, down_sum = together(
-        (grads, output_part, up_half, gate_grad, down_sum)
+    grads, up_half, gate_grad = together((grads, up_half, gate_grad))
+    grads, output_part, up_grad, down_sum = together(
+        (grads, output_part, hand_back(up_half), down_sum)
     )
     output_part = lax.psum_scatter(output_part, "wide", scatter_dimension=0, tiled=True)
     shared = wide_count // key_total
@@ -1785,7 +1786,6 @@
         )
     hidden_one_grad, output_part = together((hidden_one_grad, output_part))
     down_grad = hand_back(add_low(down_half, down_other))
-    up_grad = hand_back(up_half)
     _, first_pull = jax.vjp(norm_scale, token_values, first_gain)
     token_part, first_gain_grad = first_pull(hidden_one_grad)
     tokens_gradient = (middle_grad + token_part).astype(low)

time: 849 us -> 863 us (1.016)
  waiting for transfers between devices: 25 us -> 37.8 us
    ppermute x6, waiting for transfers between devices: 24.4 us -> 37.7 us  [swap_narrow(): return lax.ppermute(values, 'narrow', [(i, i ^ bit) for i in range(count)])]
    pallas_call x1, Pallas kernels: 32.9 us -> 23.5 us  [mix_and_project(): pl.pallas_call(kernel, in_specs=[VMEM_SPEC, VMEM_SPEC], out_specs=[VMEM_S...]
    pallas_call x1, Pallas kernels: 158 us -> 167 us  [forward_gathered(): pl.pallas_call(kernel, in_specs=[hbm, vmem, vmem, vmem], out_specs=[hbm]...]
    unnamed x141 -> x139, local copies, waits for them, and re-layouts: 22.1 us -> 23.4 us
  transfers between devices with their start and end apart: 9 -> 9, of which waited for: 2 -> 1; matrix products, arithmetic and copies ran while one was open for 8% -> 8% of each run, Pallas kernels for 49% -> 48%
where the time goes in v5:
time: 863 us; the launch traced here: 855 us
  Pallas kernels  693 us (80%)
  other arithmetic  54.2 us (6%)
  local copies, waits for them, and re-layouts  41.8 us (5%)
  waiting for transfers between devices  37.8 us (4%)
  between operations  15.1 us (2%)
  matrix products  11.4 us (1%)
    pallas_call x1, Pallas kernels, forward_gathered(): pl.pallas_call(kernel, in_specs=[hbm, vmem, vmem, vmem], out_specs=[hbm]...  167 us
    pallas_call x1, Pallas kernels, project_gathered(): pl.pallas_call(kernel, in_specs=[hbm, vmem, hbm] + [hbm] * len(strips), o...  154 us
    pallas_call x1, Pallas kernels, backward_scattered(): pl.pallas_call(kernel, in_specs=[hbm, hbm, hbm, hbm, vmem, vmem, vmem], o...  113 us
    pallas_call x1, Pallas kernels, return_and_project(): pl.pallas_call(kernel, in_specs=[VMEM_SPEC, HBM_SPEC] + [VMEM_SPEC] * 3 +...  86.9 us
    pallas_call x1, Pallas kernels, unmix(): pl.pallas_call(kernel, in_specs=[VMEM_SPEC] * 3 + [HBM_SPEC], out_specs=[...  57.8 us
    pallas_call x1, Pallas kernels, attention_backward(): pl.pallas_call(kernel, grid_spec=pltpu.PrefetchScalarGridSpec(num_scalar_...  44.6 us
    ppermute x6, waiting for transfers between devices, swap_narrow(): return lax.ppermute(values, 'narrow', [(i, i ^ bit) for i in range(count)])  37.7 us
    pallas_call x1, Pallas kernels, attention_forward(): pl.pallas_call(kernel, grid_spec=pltpu.PrefetchScalarGridSpec(num_scalar_...  30.2 us
  transfers between devices with their start and end apart: 9, of which 1 were waited for; matrix products, arithmetic and copies ran while one was open for 8% of the time, Pallas kernels for 48%

profile of v5, /device:TPU:0, one launch (start us, length us, event | category | flops | bytes accessed | tf_op | source)
XLA Modules:
  0.0 855.5 jit_solution(14741184104187978076)
XLA Ops:
  7.3 1.3 constant_dynamic-slice_fusion
  8.8 1.1 constant_dynamic-slice_fusion.1.refs_0_
  10.9 1.6 constant_dynamic-slice_fusion.2
  13.2 154.0 %project_gathered.1 = (bf16[8,256,2048]{2,1,0:T(8,128)(2,1)}, f32[2048,384]{1,0:T(8,128)}, f32[8,128]{1,0:T(8,128)S(1)}, bf16[8,4,64,2048]{3,2,1,0:T(8,128)(2,1)}, bf16[8,4,64,2048]{3,2,1,0:T(8,128)(2,1)}) custom-call(bf16[256,2048]{1,0:T(8,128)(2,1)S(1)} %fusion.4.local_ref, bf16[2048,384]{1,0:T(8,128)(2,1)S(1)} %pad_maximum_fusion.weights_ref, ...), custom_call_target="tpu_custom_call" | custom-call | tf_op jit(solution)/shard_map/project_gathered/pallas_call | solution.py:648
  169.2 1.2 fusion.11
  170.6 1.3 copy.41.segk_ref
  172.3 1.2 copy-done.2
  173.5 1.2 copy-done.6
  174.7 1.2 copy-done.8
  175.9 30.2 %attention_forward.1 = (bf16[2048,256]{1,0:T(8,128)(2,1)S(1)}, f32[8,2048]{1,0:T(8,128)S(1)}, bf16[2048,256]{1,0:T(8,128)(2,1)S(1)}, bf16[2048,256]{1,0:T(8,128)...) custom-call(s32[1,8]{1,0:T(1,128)S(1)} %and_select_fusion.first_ref, ...), custom_call_target="tpu_custom_call" | custom-call | tf_op jit(solution)/shard_map/attention_forward/pallas_call | solution.py:155
  208.1 4.2 copy-done
  212.4 23.5 %mix_and_project.1 = (f32[256,2048]{1,0:T(8,128)S(1)}, bf16[8,256,256]{2,1,0:T(8,128)(2,1)S(1)}) custom-call(bf16[8,256,256]{2,1,0:T(8,128)(2,1)S(1)} %bitcast.57, bf16[2048,2048]{1,0:T(8,128)(2,1)S(1)} %bitcast.56), custom_call_target="tpu_custom_call" | custom-call | tf_op jit(solution)/shard_map/mix_and_project/pallas_call | solution.py:1305
  238.3 1.2 multiply_convert_fusion.local_ref
  239.5 167.2 %forward_gathered.1 = (bf16[8,256,2048]{2,1,0:T(8,128)(2,1)}, f32[8,256,1024]{2,1,0:T(8,128)}, f32[8,256,1024]{2,1,0:T(8,128)}, bf16[8,256,1024]{2,1,0:T(8,128)(2,1)}, bf16[8,256,2048]{2,1,0:T(8,128)(2,1)}) custom-call(bf16[256,2048]{1,0:T(8,128)(2,1)} %multiply_convert_fusion.local_ref, bf16[2048,1024]{1,0:T(8,128)(2,1)} %gate_ref.3, ...), custom_call_target="tpu_custom_call" | custom-call | tf_op jit(solution)/shard_map/forward_gathered/pallas_call | solution.py:751
  406.8 113.0 %backward_scattered.1 = (f32[256,2048]{1,0:T(8,128)}, bf16[4,256,1024]{2,1,0:T(8,128)(2,1)}, bf16[4,256,1024]{2,1,0:T(8,128)(2,1)}) custom-call(bf16[8,256,2048]{2,1,0:T(8,128)(2,1)} %bitcast.68, f32[8,256,1024]{2,1,0:T(8,128)} %get-tuple-element.74.gates_ref, f32[8,256,1024]{2,1,0:T(8,128)} %get-tuple-element.75.ups_ref, ...), custom_call_target="tpu_custom_call" | custom-call | tf_op jit(solution)/shard_map/backward_scattered/pallas_call | solution.py:1038
  520.2 1.3 copy-done.31
  521.5 2.3 multiply_reduce_fusion
  523.9 2.0 fusion.14
  526.0 57.8 %unmix.1 = (bf16[8,256,256]{2,1,0:T(8,128)(2,1)S(1)}, bf16[2,8,64,2048]{3,2,1,0:T(8,128)(2,1)}, bf16[1024,1024]{1,0:T(8,128)(2,1)S(1)}) custom-call(bf16[256,2048]{1,0:T(8,128)(2,1)S(1)} %get-tuple-element.162.middle_ref, bf16[2048,2048]{1,0:T(8,128)(2,1)} %bitcast.55, bf16[8,256,256]{2,1,0:T(8,128)(2,1)S(1)} %copy-done.17, bf16[1024,1024]{1,0:T(8,128)(2,1)} %bitcast.67), custom_call_target="tpu_custom_call" | custom-call | tf_op jit(solution)/shard_map/unmix/pallas_call | solution.py:1383
  583.8 1.1 add_convert_fusion.1
  585.0 1.6 copy-done.67
  586.6 11.4 %convolution_convert_fusion = bf16[1024,2048]{1,0:T(8,128)(2,1)S(1)} fusion(bf16[2048,1024]{1,0:T(8,128)(2,1)S(1)} %bitcast.78, bf16[2048,2048]{1,0:T(8,128)(2,1)} %all-gather.2.cloned.1.call-done), kind=kOutput, calls=%fused_computation.15 | convolution fusion | flops 8592031744 | bytes 16777216 | tf_op jit(solution)/shard_map/dot_general | solution.py:1574
  598.0 1.6 dynamic-slice_bitcast_fusion.1
  600.6 3.2 dynamic-slice_bitcast_fusion
  603.8 2.0 collective-permute-start.3
  605.8 1.9 broadcast_select_fusion.5
  607.7 3.9 fusion.1.carried_ref
  611.7 37.7 %collective-permute-done.1 = bf16[1024,1024]{1,0:T(8,128)(2,1)} collective-permute-done((bf16[1024,1024]{1,0:T(8,128)(2,1)}, bf16[1024,1024]{1,0:T(8,128)(2,1)}, u32[]{:S(2)}, u32[]{:S(2)}) %collective-permute-start.1) | collective-permute-done | bytes 2097184 | tf_op jit(solution)/shard_map/ppermute | solution.py:1596
  649.4 3.2 add_convert_fusion.2
  652.7 44.6 %attention_backward.1 = (bf16[2048,384]{1,0:T(8,128)(2,1)}, f32[1,256]{1,0:T(1,128)S(1)}, f32[1,256]{1,0:T(1,128)S(1)}) custom-call(s32[1,8]{1,0:T(1,128)S(1)} %copy-done.29, f32[2048,384]{1,0:T(8,128)} %get-tuple-element.68.raw_ref, f32[1,256]{1,0:T(1,128)S(1)} %copy-done.25, f32[1,256]{1,0:T(1,128)S(1)} %copy-done.27, f32[2048,64]{1,0:T(8,128)S(1)} %copy-done.7, ...), custom_call_target="tpu_custom_call" | custom-call | tf_op jit(solution)/shard_map/attention_backward/pallas_call | solution.py:312
  697.3 4.5 maximum_convert_fusion
  701.8 4.4 fusion
  706.2 1.9 broadcast_select_fusion.3
  708.1 4.5 maximum_convert_fusion.1
  712.6 2.8 convert_element_type.151
  715.5 1.4 copy-done.10
  716.9 86.9 %return_and_project.1 = (f32[256,2048]{1,0:T(8,128)S(1)}, f32[2048,384]{1,0:T(8,128)}, bf16[512,2048]{1,0:T(8,128)(2,1)S(1)}) custom-call(bf16[8,256,384]{2,1,0:T(8,128)(2,1)S(1)} %bitcast.58, bf16[8,256,2048]{2,1,0:T(8,128)(2,1)} %get-tuple-element.101.hidden_ref, bf16[2048,2048]{1,0:T(8,128)(2,1)} %bitcast.65, bf16[2048,512]{1,0:T(8,128)(2,1)} %key_ref.1, ...), custom_call_target="tpu_custom_call" | custom-call | tf_op jit(solution)/shard_map/return_and_project/pallas_call | solution.py:1525
  803.8 2.2 add_convert_fusion
  807.3 3.2 slice.44
  810.6 1.3 fusion.16
  811.9 2.3 copy.43
  814.2 1.1 copy.44
  815.3 2.5 broadcast_select_fusion.1
  817.9 4.3 maximum_convert_fusion.2
  823.6 15.5 %sum_everywhere.1 = (f32[40,128]{1,0:T(8,128)}, bf16[4,64,2048]{2,1,0:T(8,128)(2,1)}) custom-call(f32[40,128]{1,0:T(8,128)} %pad_bitcast_fusion.in_ref, bf16[64,2048]{1,0:T(8,128)(2,1)} %reduce-scatter.5.cloned.1.call-done.refs_0_), custom_call_target="tpu_custom_call" | custom-call | tf_op jit(solution)/shard_map/sum_everywhere/pallas_call | solution.py:1207
  839.2 2.9 bitcast_convert_fusion
  844.7 1.6 fusion.8
  847.3 1.2 add_convert_fusion.3
  (182 shorter events, 16.6 us)
Async XLA Ops:
  7.2 3.6 copy-start.62
  7.2 3.6 copy-start.64
  7.2 399.6 %all-gather.2.cloned.1.call-start = ((), (), s32[]{:S(2)}) async-start(), calls=%async_computation.2 | async-start | bytes 9437184 | tf_op jit(solution)/shard_map/all_gather | solution.py:1580
  8.6 3.9 copy-start.46
  13.2 156.0 %copy-start.44 = (bf16[256,2048]{1,0:T(8,128)(2,1)S(1)}, bf16[256,2048]{1,0:T(8,128)(2,1)}, u32[]{:S(2)}) copy-start(bf16[256,2048]{1,0:T(8,128)(2,1)} %param.31) | copy-start | bytes 3145732
  167.2 3.2 copy-start.20
  169.2 2.8 copy-start.66
  169.2 3.1 copy-start.1
  170.4 542.2 %reduce-scatter.3.cloned.1.call-start = ((), (), s32[]{:S(2)}) async-start(), calls=%async_computation.3 | async-start | bytes 9437184 | tf_op jit(solution)/shard_map/reduce_scatter | solution.py:1584
  171.9 65.6 %copy-start.49 = (f32[2048]{0:T(1024)}, f32[2048]{0:T(1024)S(1)}, u32[]{:S(2)}) copy-start(f32[2048]{0:T(1024)S(1)} %convert_element_type.131) | copy-start | bytes 24580
  172.0 34.1 %copy-start.24 = (f32[1,256]{1,0:T(1,128)}, f32[1,256]{1,0:T(1,128)S(1)}, u32[]{:S(2)}) copy-start(f32[1,256]{1,0:T(1,128)S(1)} %get-tuple-element.180.qg_ref) | copy-start | bytes 3076
  172.0 34.1 %copy-start.26 = (f32[1,256]{1,0:T(1,128)}, f32[1,256]{1,0:T(1,128)S(1)}, u32[]{:S(2)}) copy-start(f32[1,256]{1,0:T(1,128)S(1)} %get-tuple-element.181.kg_ref) | copy-start | bytes 3076
  172.2 33.9 %copy-start.28 = (s32[1,8]{1,0:T(1,128)}, s32[1,8]{1,0:T(1,128)S(1)}, u32[]{:S(2)}) copy-start(s32[1,8]{1,0:T(1,128)S(1)} %and_select_fusion.first_ref) | copy-start | bytes 100
  208.1 27.8 %copy-start.4 = (bf16[2048,256]{1,0:T(8,128)(2,1)}, bf16[2048,256]{1,0:T(8,128)(2,1)S(1)}, u32[]{:S(2)}) copy-start(bf16[2048,256]{1,0:T(8,128)(2,1)S(1)} %get-tuple-element.69.mixed_ref) | copy-start | bytes 3145732
  208.1 27.8 %copy-start.11 = (bf16[2048,256]{1,0:T(8,128)(2,1)}, bf16[2048,256]{1,0:T(8,128)(2,1)S(1)}, u32[]{:S(2)}) copy-start(bf16[2048,256]{1,0:T(8,128)(2,1)S(1)} %get-tuple-element.80.query_ref) | copy-start | bytes 3145732
  208.1 27.8 %copy-start.18 = (bf16[8,64,256]{2,1,0:T(8,128)(2,1)}, bf16[8,64,256]{2,1,0:T(8,128)(2,1)S(1)}, u32[]{:S(2)}) copy-start(bf16[8,64,256]{2,1,0:T(8,128)(2,1)S(1)} %get-tuple-element.92.keyt_ref) | copy-start | bytes 786436
  208.1 27.8 %copy-start.22 = (f32[8,2048]{1,0:T(8,128)}, f32[8,2048]{1,0:T(8,128)S(1)}, u32[]{:S(2)}) copy-start(f32[8,2048]{1,0:T(8,128)S(1)} %get-tuple-element.79.lse_ref) | copy-start | bytes 196612
  208.1 4.3 copy-start
  212.4 23.6 %copy-start.34 = (bf16[256,2048]{1,0:T(8,128)(2,1)S(1)}, bf16[256,2048]{1,0:T(8,128)(2,1)}, u32[]{:S(2)}) copy-start(bf16[256,2048]{1,0:T(8,128)(2,1)} %param.19) | copy-start | bytes 3145732
  519.9 302.3 %reduce-scatter.5.cloned.1.call-start = ((), (), s32[]{:S(2)}) async-start(), calls=%async_computation.4 | async-start | bytes 2359296 | tf_op jit(solution)/shard_map/reduce_scatter | solution.py:1761
  526.0 57.8 %copy-start.39 = (bf16[4,256,1024]{2,1,0:T(8,128)(2,1)S(1)}, bf16[4,256,1024]{2,1,0:T(8,128)(2,1)}, u32[]{:S(2)}) copy-start(bf16[4,256,1024]{2,1,0:T(8,128)(2,1)} %get-tuple-element.82) | copy-start | bytes 6291460
  583.8 2.8 copy-start.67
  585.0 20.9 %collective-permute-start.2 = (bf16[1024,1024]{1,0:T(8,128)(2,1)S(1)}, bf16[1024,1024]{1,0:T(8,128)(2,1)}, u32[]{:S(2)}, u32[]{:S(2)}) collective-permute-start(bf16[1024,1024]{1,0:T(8,128)(2,1)S(1)} %add_convert_fusion.1), channel_id=1, source_target_pairs={{0,8},{8,0},{16,24},{24,16},{1,9},{9,1},{17,25},{25,17},{2,10},{10... | collective-permute-start | bytes 6291464 | tf_op jit(solution)/shard_map/ppermute | solution.py:1596
  600.6 7.1 collective-permute-start
  600.6 48.7 %collective-permute-start.1 = (bf16[1024,1024]{1,0:T(8,128)(2,1)}, bf16[1024,1024]{1,0:T(8,128)(2,1)}, u32[]{:S(2)}, u32[]{:S(2)}) collective-permute-start(bf16[1024,1024]{1,0:T(8,128)(2,1)} %bitcast.18), channel_id=1, source_target_pairs={{0,16},{8,24},{16,0},{24,8},{1,17},{9,25},{17,1},{25,9},{2,18},{10... | collective-permute-start | bytes 6291464 | tf_op jit(solution)/shard_map/ppermute | solution.py:1596
  603.8 3.9 copy-start.43
  603.8 98.0 %collective-permute-start.3 = (bf16[512,2048]{1,0:T(8,128)(2,1)}, bf16[512,2048]{1,0:T(8,128)(2,1)}, u32[]{:S(2)}, u32[]{:S(2)}) collective-permute-start(bf16[512,2048]{1,0:T(8,128)(2,1)} %dynamic-slice_bitcast_fusion), channel_id=1, source_target_pairs={{0,16},{8,24},{16,0},{24,8},{1,17},{9,25},{17,1},{25,9},{2,18},{10... | collective-permute-start | bytes 6291464 | tf_op jit(solution)/shard_map/ppermute | solution.py:1596
  611.6 41.0 %copy-start.3 = (s32[2048,1]{1,0:T(8,128)S(1)}, s32[2048,1]{1,0:T(8,128)}, u32[]{:S(2)}) copy-start(s32[2048,1]{1,0:T(8,128)} %copy.41.segk_ref) | copy-start | bytes 24580
  611.6 41.0 %copy-start.5 = (bf16[2048,256]{1,0:T(8,128)(2,1)S(1)}, bf16[2048,256]{1,0:T(8,128)(2,1)}, u32[]{:S(2)}) copy-start(bf16[2048,256]{1,0:T(8,128)(2,1)} %copy-done.4) | copy-start | bytes 3145732
  611.6 41.0 %copy-start.7 = (f32[2048,64]{1,0:T(8,128)S(1)}, f32[2048,64]{1,0:T(8,128)}, u32[]{:S(2)}) copy-start(f32[2048,64]{1,0:T(8,128)} %constant.116.clone.cos_ref) | copy-start | bytes 1572868
  611.6 41.0 %copy-start.9 = (f32[2048,64]{1,0:T(8,128)S(1)}, f32[2048,64]{1,0:T(8,128)}, u32[]{:S(2)}) copy-start(f32[2048,64]{1,0:T(8,128)} %constant.117.clone.sin_ref) | copy-start | bytes 1572868
  611.6 41.0 %copy-start.12 = (bf16[2048,256]{1,0:T(8,128)(2,1)S(1)}, bf16[2048,256]{1,0:T(8,128)(2,1)}, u32[]{:S(2)}) copy-start(bf16[2048,256]{1,0:T(8,128)(2,1)} %copy-done.11) | copy-start | bytes 3145732
  611.6 41.0 %copy-start.19 = (bf16[8,64,256]{2,1,0:T(8,128)(2,1)S(1)}, bf16[8,64,256]{2,1,0:T(8,128)(2,1)}, u32[]{:S(2)}) copy-start(bf16[8,64,256]{2,1,0:T(8,128)(2,1)} %copy-done.18) | copy-start | bytes 786436
  611.6 41.0 %copy-start.21 = (s32[1,2048]{1,0:T(1,128)S(1)}, s32[1,2048]{1,0:T(1,128)}, u32[]{:S(2)}) copy-start(s32[1,2048]{1,0:T(1,128)} %param.33) | copy-start | bytes 24580
  611.6 41.0 %copy-start.23 = (f32[8,2048]{1,0:T(8,128)S(1)}, f32[8,2048]{1,0:T(8,128)}, u32[]{:S(2)}) copy-start(f32[8,2048]{1,0:T(8,128)} %copy-done.22) | copy-start | bytes 196612
  611.7 41.0 %copy-start.25 = (f32[1,256]{1,0:T(1,128)S(1)}, f32[1,256]{1,0:T(1,128)}, u32[]{:S(2)}) copy-start(f32[1,256]{1,0:T(1,128)} %copy-done.24) | copy-start | bytes 3076
  611.7 41.0 %copy-start.27 = (f32[1,256]{1,0:T(1,128)S(1)}, f32[1,256]{1,0:T(1,128)}, u32[]{:S(2)}) copy-start(f32[1,256]{1,0:T(1,128)} %copy-done.26) | copy-start | bytes 3076
  611.7 41.0 %copy-start.29 = (s32[1,8]{1,0:T(1,128)S(1)}, s32[1,8]{1,0:T(1,128)}, u32[]{:S(2)}) copy-start(s32[1,8]{1,0:T(1,128)} %copy-done.28) | copy-start | bytes 100
  701.8 4.5 collective-permute-start.4
  716.9 86.9 %copy-start.36 = (bf16[512,2048]{1,0:T(8,128)(2,1)S(1)}, bf16[512,2048]{1,0:T(8,128)(2,1)}, u32[]{:S(2)}) copy-start(bf16[512,2048]{1,0:T(8,128)(2,1)} %fusion.1.carried_ref) | copy-start | bytes 6291460
  806.0 9.3 %collective-permute-start.5 = (bf16[512,2048]{1,0:T(8,128)(2,1)}, bf16[512,2048]{1,0:T(8,128)(2,1)}, u32[]{:S(2)}, u32[]{:S(2)}) collective-permute-start(bf16[512,2048]{1,0:T(8,128)(2,1)} %add_convert_fusion), channel_id=1, source_target_pairs={{0,8},{8,0},{16,24},{24,16},{1,9},{9,1},{17,25},{25,17},{2,10},{10... | collective-permute-start | bytes 6291464 | tf_op jit(solution)/shard_map/ppermute | solution.py:1596
  807.3 3.2 copy-start.41
  817.9 4.3 copy-start.35
  817.9 4.3 copy-start.48
  817.9 4.3 copy-start.52
  822.9 21.7 %copy-start.59 = (f32[256]{0:T(256)S(1)}, f32[256]{0:T(256)}, u32[]{:S(2)}) copy-start(f32[256]{0:T(256)} %copy-done.58) | copy-start | bytes 3076
  839.2 3.0 copy-start.55
  839.2 5.5 copy-start.37
  (29 other events, 48.8 us)
Sparse Core Ops, SparseCore 0:
  170.5 161.9 all-gather.1
  520.0 174.3 reduce-scatter.2
  715.6 100.8 reduce-scatter.4
